TPU v7x, 32 devices: a whole 2x2x4 slice. The times are simulated.
32 devices in a mesh: dp: 8 (over y, x, core), tensor: 4 (over z).
Axes of the slice: x: 2, y: 2, z: 4, core: 2. Of those that a mesh axis runs over, the one named last changes fastest.
Arguments:
- tokens: bfloat16 [16384, 1536], P(('dp', 'tensor')), may hold values from -6 to 6
- lengths: int32 [8], P('dp'), may hold values from 1024 to 2048, as said below
- cotangent: bfloat16 [16384, 1536], P(('dp', 'tensor')), may hold values from -6 to 6
- attn_gain: bfloat16 [1536], P('dp'), may hold values from 0.099609375 to 1.8984375
- query_weight: bfloat16 [1536, 1536], P('dp', 'tensor'), may hold values from -0.15625 to 0.15625
- key_matrix: bfloat16 [1536, 768], P('dp', 'tensor'), may hold values from -0.15625 to 0.15625
- value_matrix: bfloat16 [1536, 768], P('dp', 'tensor'), may hold values from -0.15625 to 0.15625
- out_weight: bfloat16 [1536, 1536], P('tensor', 'dp'), may hold values from -2.5 to 2.5
- mlp_gain: bfloat16 [1536], P('dp'), may hold values from 0.099609375 to 1.8984375
- gate_weight: bfloat16 [1536, 4096], P('dp', 'tensor'), may hold values from -0.15625 to 0.15625
- up_weight: bfloat16 [1536, 4096], P('dp', 'tensor'), may hold values from -0.15625 to 0.15625
- down_weight: bfloat16 [4096, 1536], P('tensor', 'dp'), may hold values from -0.09375 to 0.09375
Outputs:
- block_out: bfloat16 [16384, 1536], P(('dp', 'tensor'))
- tokens_grad: bfloat16 [16384, 1536], P(('dp', 'tensor'))
- attn_gain_grad: float32 [1536], P('dp')
- query_grad: float32 [1536, 1536], P('dp', 'tensor')
- key_grad: float32 [1536, 768], P('dp', 'tensor')
- value_grad: float32 [1536, 768], P('dp', 'tensor')
- out_grad: float32 [1536, 1536], P('tensor', 'dp')
- mlp_gain_grad: float32 [1536], P('dp')
- gate_grad: float32 [1536, 4096], P('dp', 'tensor')
- up_grad: float32 [1536, 4096], P('dp', 'tensor')
- down_grad: float32 [4096, 1536], P('tensor', 'dp')
Inputs may be any that keep to these rules, and one draw needn't show every extreme that they name: `lengths`: in every draw one slot is full and one holds exactly half of 2048.
All inputs are finite; a program needn't handle non-finite values.
Results may differ from a plain program's by a relative error of at most 0.014.
Values may be sent and summed in bfloat16 or wider, within the bound.
A program may use at most 192 MiB of HBM per device.

v0:
```python
import math

import jax
import jax.numpy as jnp
from jax import lax
from jax.sharding import PartitionSpec as P

HEAD_SIZE = 96


eps_norm = 1e-05
rope_base = 100000.0


def tables(count, head_dim):
    half = head_dim // 2
    freqs = rope_base ** (-(jnp.arange(half, dtype=jnp.float32) * 2.0) / head_dim)
    angles = jnp.arange(count, dtype=jnp.float32)[:, None] * freqs[None, :]
    cosine_table = jnp.cos(angles)
    sine_table = jnp.sin(angles)
    return (
        jnp.concatenate([cosine_table, cosine_table], axis=1),
        jnp.concatenate([sine_table, sine_table], axis=1),
    )


def rotate_pairs(values, cosine_table, sine_table):
    half = values.shape[-1] // 2
    swapped = jnp.concatenate([-values[..., half:], values[..., :half]], axis=-1)
    return values * cosine_table[:, None, :] + swapped * sine_table[:, None, :]


def norm_rows(rows, gain):
    inverse = lax.rsqrt(jnp.mean(rows * rows, axis=1, keepdims=True) + eps_norm)
    return (rows * inverse * gain, inverse)


def norm_back(rows, inverse, gain, grad):
    scaled = grad * gain
    inner = jnp.mean(scaled * rows, axis=1, keepdims=True)
    d_rows = inverse * scaled - rows * inverse * inverse * inverse * inner
    d_gain = jnp.sum(grad * rows * inverse, axis=0)
    return (d_rows, d_gain)


def local(
    tokens,
    lengths,
    cotangent,
    attn_gain,
    query_weight,
    key_matrix,
    value_matrix,
    out_weight,
    mlp_gain,
    gate_weight,
    up_weight,
    down_weight,
):
    f32 = jnp.float32
    bf16 = jnp.bfloat16
    rows = tokens.shape[0]
    sequence_length = rows * lax.axis_size("tensor")
    head_dim = HEAD_SIZE
    first = lax.axis_index("tensor") * rows
    local_pos = first + jnp.arange(rows, dtype=jnp.int32)
    seq_length = lengths[0]
    live = (local_pos < seq_length).astype(f32)[:, None]
    x_rows = tokens.astype(f32)
    gain_one, wq_all, wk_all, wv_all, wo_all = (
        lax.all_gather(attn_gain, "dp", axis=0, tiled=True),
        lax.all_gather(query_weight, "dp", axis=0, tiled=True),
        lax.all_gather(key_matrix, "dp", axis=0, tiled=True),
        lax.all_gather(value_matrix, "dp", axis=0, tiled=True),
        lax.all_gather(out_weight, "dp", axis=1, tiled=True),
    )
    gain_one = gain_one.astype(f32)
    normed_one, inv_one = norm_rows(x_rows, gain_one)
    n1_full = lax.all_gather(normed_one.astype(bf16), "tensor", axis=0, tiled=True)
    q_pre = jnp.dot(n1_full, wq_all, preferred_element_type=f32)
    k_pre = jnp.dot(n1_full, wk_all, preferred_element_type=f32)
    v_pre = jnp.dot(n1_full, wv_all, preferred_element_type=f32)
    heads_q = q_pre.shape[1] // head_dim
    heads_kv = k_pre.shape[1] // head_dim
    repeat = heads_q // heads_kv
    cosine_table, sine_table = tables(sequence_length, head_dim)
    rotated_query = rotate_pairs(
        q_pre.reshape(sequence_length, heads_q, head_dim), cosine_table, sine_table
    ).astype(bf16)
    rotated_key = rotate_pairs(
        k_pre.reshape(sequence_length, heads_kv, head_dim), cosine_table, sine_table
    ).astype(bf16)
    value_reduced = v_pre.astype(bf16).reshape(sequence_length, heads_kv, head_dim)
    query_block = min(512, sequence_length)
    block_count = sequence_length // query_block
    query_block_list = rotated_query.reshape(block_count, query_block, heads_kv, repeat, head_dim)
    starts = jnp.arange(block_count, dtype=jnp.int32) * query_block
    key_pos = jnp.arange(sequence_length, dtype=jnp.int32)
    scale = 1.0 / math.sqrt(head_dim)

    def scores_of(q_part, start):
        raw = jnp.einsum("qgre,kge->grqk", q_part, rotated_key, preferred_element_type=f32)
        row_pos = start + jnp.arange(query_block, dtype=jnp.int32)
        allowed = (key_pos[None, :] <= row_pos[:, None]) & (key_pos[None, :] < seq_length)
        return jnp.where(allowed, raw * scale, -1e30)

    def forward_block(item):
        q_part, start = item
        scores = scores_of(q_part, start)
        top = jnp.max(scores, axis=-1, keepdims=True)
        total = jnp.sum(jnp.exp(scores - top), axis=-1, keepdims=True)
        log_total = top + jnp.log(total)
        probs_low = jnp.exp(scores - log_total).astype(bf16)
        out = jnp.einsum("grqk,kge->qgre", probs_low, value_reduced, preferred_element_type=f32)
        return (out, log_total)

    att_blocks, log_totals = lax.map(forward_block, (query_block_list, starts))
    attended = att_blocks.reshape(sequence_length, heads_q * head_dim).astype(bf16)
    part = attended
    h_one = x_rows + lax.psum_scatter(
        jnp.dot(part, wo_all, preferred_element_type=f32), "tensor", scatter_dimension=0, tiled=True
    )
    gain_two, wg_all, wu_all, wd_all = (
        lax.all_gather(mlp_gain, "dp", axis=0, tiled=True),
        lax.all_gather(gate_weight, "dp", axis=0, tiled=True),
        lax.all_gather(up_weight, "dp", axis=0, tiled=True),
        lax.all_gather(down_weight, "dp", axis=1, tiled=True),
    )
    gain_two = gain_two.astype(f32)
    normed_two, inv_two = norm_rows(h_one, gain_two)
    n2_full = lax.all_gather(normed_two.astype(bf16), "tensor", axis=0, tiled=True)
    gate = jnp.dot(n2_full, wg_all, preferred_element_type=f32)
    upper = jnp.dot(n2_full, wu_all, preferred_element_type=f32)
    sigma = jax.nn.sigmoid(gate)
    active = gate * sigma
    hidden = (active * upper).astype(bf16)
    part = hidden
    mlp_mine = lax.psum_scatter(
        jnp.dot(part, wd_all, preferred_element_type=f32).astype(jnp.bfloat16),
        "tensor",
        scatter_dimension=0,
        tiled=True,
    ).astype(jnp.float32)
    block_out = (live * (h_one + mlp_mine)).astype(bf16)
    grad_rows = cotangent.astype(f32) * live
    grad_full = lax.all_gather(grad_rows.astype(bf16), "tensor", axis=0, tiled=True)
    down_grad = jnp.einsum("sf,sd->fd", hidden, grad_full, preferred_element_type=f32)
    d_hidden = jnp.einsum("sd,fd->sf", grad_full, wd_all, preferred_element_type=f32)
    d_gate = (d_hidden * upper * sigma * (1.0 + gate * (1.0 - sigma))).astype(bf16)
    d_upper = (d_hidden * active).astype(bf16)
    gate_grad = jnp.einsum("sd,sf->df", n2_full, d_gate, preferred_element_type=f32)
    up_grad = jnp.einsum("sd,sf->df", n2_full, d_upper, preferred_element_type=f32)
    d_normed_two = lax.psum_scatter(
        jnp.einsum("sf,df->sd", d_gate, wg_all, preferred_element_type=f32)
        + jnp.einsum("sf,df->sd", d_upper, wu_all, preferred_element_type=f32),
        "tensor",
        scatter_dimension=0,
        tiled=True,
    )
    d_h_norm, gain_two_grad = norm_back(h_one, inv_two, gain_two, d_normed_two)
    d_h_one = grad_rows + d_h_norm
    d_att_full = lax.all_gather(d_h_one.astype(bf16), "tensor", axis=0, tiled=True)
    out_grad = jnp.einsum("sh,sd->hd", attended, d_att_full, preferred_element_type=f32)
    d_att = jnp.einsum("sd,hd->sh", d_att_full, wo_all, preferred_element_type=f32).astype(bf16)
    d_blocks = d_att.reshape(block_count, query_block, heads_kv, repeat, head_dim)

    def backward_block(carry, item):
        dk_sum, dv_sum = carry
        q_part, d_part, log_total, start = item
        scores = scores_of(q_part, start)
        probs = jnp.exp(scores - log_total)
        d_probs = jnp.einsum("qgre,kge->grqk", d_part, value_reduced, preferred_element_type=f32)
        delta = jnp.sum(probs * d_probs, axis=-1, keepdims=True)
        d_scores = (probs * (d_probs - delta)).astype(bf16)
        dv_sum = dv_sum + jnp.einsum(
            "grqk,qgre->kge", probs.astype(bf16), d_part, preferred_element_type=f32
        )
        dk_sum = (
            dk_sum
            + jnp.einsum("grqk,qgre->kge", d_scores, q_part, preferred_element_type=f32) * scale
        )
        d_q_part = (
            jnp.einsum("grqk,kge->qgre", d_scores, rotated_key, preferred_element_type=f32) * scale
        )
        return ((dk_sum, dv_sum), d_q_part)

    zero_keys = jnp.zeros((sequence_length, heads_kv, head_dim), f32)
    (dk_rot, dv_total), dq_blocks = lax.scan(
        backward_block, (zero_keys, zero_keys), (query_block_list, d_blocks, log_totals, starts)
    )
    d_query = (
        rotate_pairs(
            dq_blocks.reshape(sequence_length, heads_q, head_dim), cosine_table, -sine_table
        )
        .reshape(sequence_length, heads_q * head_dim)
        .astype(bf16)
    )
    d_key = (
        rotate_pairs(dk_rot, cosine_table, -sine_table)
        .reshape(sequence_length, heads_kv * head_dim)
        .astype(bf16)
    )
    d_value = dv_total.reshape(sequence_length, heads_kv * head_dim).astype(bf16)
    query_grad = jnp.einsum("sd,sh->dh", n1_full, d_query, preferred_element_type=f32)
    key_grad = jnp.einsum("sd,sh->dh", n1_full, d_key, preferred_element_type=f32)
    value_grad = jnp.einsum("sd,sh->dh", n1_full, d_value, preferred_element_type=f32)
    total = jnp.einsum("sh,dh->sd", d_query, wq_all, preferred_element_type=f32)
    total = total + jnp.einsum("sh,dh->sd", d_key, wk_all, preferred_element_type=f32)
    d_normed_one = lax.psum_scatter(
        total + jnp.einsum("sh,dh->sd", d_value, wv_all, preferred_element_type=f32),
        "tensor",
        scatter_dimension=0,
        tiled=True,
    )
    d_x_norm, gain_one_grad = norm_back(x_rows, inv_one, gain_one, d_normed_one)
    tokens_grad = (d_h_one + d_x_norm).astype(bf16)
    every = (
        lax.psum_scatter(gain_one_grad, "dp", scatter_dimension=0, tiled=True),
        lax.psum_scatter(query_grad, "dp", scatter_dimension=0, tiled=True),
        lax.psum_scatter(key_grad, "dp", scatter_dimension=0, tiled=True),
        lax.psum_scatter(value_grad, "dp", scatter_dimension=0, tiled=True),
        lax.psum_scatter(out_grad, "dp", scatter_dimension=1, tiled=True),
        lax.psum_scatter(gain_two_grad, "dp", scatter_dimension=0, tiled=True),
        lax.psum_scatter(gate_grad, "dp", scatter_dimension=0, tiled=True),
        lax.psum_scatter(up_grad, "dp", scatter_dimension=0, tiled=True),
        lax.psum_scatter(down_grad, "dp", scatter_dimension=1, tiled=True),
    )
    (
        gain_one_share,
        query_share,
        key_share,
        value_share,
        out_share,
        gain_two_share,
        gate_share,
        up_share,
        down_share,
    ) = every
    gain_one_total, gain_two_total = lax.psum((gain_one_share, gain_two_share), "tensor")
    return (
        block_out,
        tokens_grad,
        gain_one_total,
        query_share,
        key_share,
        value_share,
        out_share,
        gain_two_total,
        gate_share,
        up_share,
        down_share,
    )


def solution(mesh):
    in_specs = (
        P(("dp", "tensor"), None),
        P("dp"),
        P(("dp", "tensor"), None),
        P("dp"),
        P("dp", "tensor"),
        P("dp", "tensor"),
        P("dp", "tensor"),
        P("tensor", "dp"),
        P("dp"),
        P("dp", "tensor"),
        P("dp", "tensor"),
        P("tensor", "dp"),
    )
    out_specs = (
        P(("dp", "tensor"), None),
        P(("dp", "tensor"), None),
        P("dp"),
        P("dp", "tensor"),
        P("dp", "tensor"),
        P("dp", "tensor"),
        P("tensor", "dp"),
        P("dp"),
        P("dp", "tensor"),
        P("dp", "tensor"),
        P("tensor", "dp"),
    )
    return jax.shard_map(local, mesh=mesh, in_specs=in_specs, out_specs=out_specs, check_vma=False)
```

profile of v0, /device:TPU:0, one launch (start us, length us, event | category | flops | bytes accessed | tf_op | source)
XLA Modules:
  0.0 2226.6 jit_solution(12457156320131539805)
XLA Ops:
  62.5 84.2 %all-gather.10.cloned.1.call-done = bf16[2048,1536]{1,0:T(8,128)(2,1)} async-done(((bf16[512,1536]{1,0:T(8,128)(2,1)}), bf16[2048,1536]{1,0:T(8,128)(2,1)}) %all-gather.10.cloned.1.call-update) | async-done | bytes 6291472 | tf_op jit(solution)/shard_map/all_gather | solution.py:79
  153.0 18.0 all-gather.12.cloned.1.call-done
  202.4 71.5 %while.30 = (s32[]{:T(128)}, bf16[4,512,2,2,96]{1,4,3,2,0:T(8,128)(2,1)}, f32[4,2,2,512,1]{3,2,1,4,0:T(2,128)}, s32[4]{0:T(128)S(1)}, s32[]{:T(128)}, /*index=5*...) while((s32[]{:T(128)}, ...), condition=%wide.region_4.5_spmd.clone.clone, body=%wide.region_1.4_spmd.clone.clone.sunk | while | flops 1658847744 | bytes 69935288 | solution.py:117
  289.5 211.3 %reduce-scatter.12.cloned.1.call-done = f32[512,1536]{1,0:T(8,128)} async-done(((f32[2048,1536]{1,0:T(8,128)}), f32[512,1536]{1,0:T(8,128)}) %reduce-scatter.12.cloned.1.call-update) | async-done | bytes 3145744 | tf_op jit(solution)/shard_map/reduce_scatter | solution.py:120
  510.4 25.6 %all-gather.20.cloned.1.call-done = bf16[1536,1024]{1,0:T(8,128)(2,1)} async-done(((bf16[192,1024]{1,0:T(8,128)(2,1)}), bf16[1536,1024]{1,0:T(8,128)(2,1)}) %all-gather.20.cloned.1.call-update) | async-done | bytes 3145744 | tf_op jit(solution)/shard_map/all_gather | solution.py:126
  536.0 117.4 %all-gather.16.cloned.1.call-done = bf16[2048,1536]{1,0:T(8,128)(2,1)} async-done(((bf16[512,1536]{1,0:T(8,128)(2,1)}), bf16[2048,1536]{1,0:T(8,128)(2,1)}) %all-gather.16.cloned.1.call-update) | async-done | bytes 6291472 | tf_op jit(solution)/shard_map/all_gather | solution.py:131
  665.2 20.7 all-gather.18.cloned.1.call-done
  697.6 22.5 %all-gather.22.cloned.1.call-done = bf16[1024,1536]{0,1:T(8,128)(2,1)} async-done(((bf16[1024,192]{0,1:T(8,128)(2,1)}), bf16[1024,1536]{0,1:T(8,128)(2,1)}) %all-gather.22.cloned.1.call-update) | async-done | bytes 3145744 | tf_op jit(solution)/shard_map/all_gather | solution.py:127
  720.1 117.0 %all-gather.24.cloned.1.call-done = bf16[2048,1536]{1,0:T(8,128)(2,1)} async-done(((bf16[512,1536]{1,0:T(8,128)(2,1)}), bf16[2048,1536]{1,0:T(8,128)(2,1)}) %all-gather.24.cloned.1.call-update) | async-done | bytes 6291472 | tf_op jit(solution)/shard_map/all_gather | solution.py:146
  837.1 18.4 multiply_convert_fusion
  893.3 198.6 %reduce-scatter.16.cloned.1.call-done = f32[512,1536]{1,0:T(8,128)} async-done(((f32[2048,1536]{1,0:T(8,128)}), f32[512,1536]{1,0:T(8,128)}) %reduce-scatter.16.cloned.1.call-update) | async-done | bytes 3145744 | tf_op jit(solution)/shard_map/reduce_scatter | solution.py:153
  1095.2 110.9 %reduce-scatter.14.cloned.1.call-done = bf16[512,1536]{1,0:T(8,128)(2,1)} async-done(((bf16[2048,1536]{1,0:T(8,128)(2,1)}), bf16[512,1536]{1,0:T(8,128)(2,1)}) %reduce-scatter.14.cloned.1.call-update) | async-done | bytes 1572880 | tf_op jit(solution)/shard_map/reduce_scatter | solution.py:138
  1211.6 116.0 %all-gather.26.cloned.1.call-done = bf16[2048,1536]{1,0:T(8,128)(2,1)} async-done(((bf16[512,1536]{1,0:T(8,128)(2,1)}), bf16[2048,1536]{1,0:T(8,128)(2,1)}) %all-gather.26.cloned.1.call-update) | async-done | bytes 6291472 | tf_op jit(solution)/shard_map/all_gather | solution.py:162
  1345.9 252.1 %while.31 = (s32[]{:T(128)}, f32[2048,2,96]{0,2,1:T(8,128)}, f32[2048,2,96]{0,2,1:T(8,128)}, f32[4,512,2,2,96]{1,0,4,3,2:T(4,128)}, bf16[4,512,2,2,96]{1,4,3,2,0...) while((s32[]{:T(128)}, f32[2048,2,96]{0,2,1:T(8,128)}, ...), condition=%wide.region_12.13_spmd.clone.clone, body=%wide.region_10.12_spmd.clone.clone.sunk | while | flops 4093706752 | bytes 190382320 | solution.py:188
  1392.5 16.0 dynamic_update_slice.24
  1697.4 145.6 %reduce-scatter.18.cloned.1.call-done = f32[512,1536]{1,0:T(8,128)} async-done(((f32[2048,1536]{1,0:T(8,128)}), f32[512,1536]{1,0:T(8,128)}) %reduce-scatter.18.cloned.1.call-update) | async-done | bytes 3145744 | tf_op jit(solution)/shard_map/reduce_scatter | solution.py:209
  1846.0 24.0 %all-reduce.4 = (f32[1536]{0:T(1024)S(1)}, f32[1536]{0:T(1024)S(1)}) all-reduce(f32[1536]{0:T(1024)S(1)} %get-tuple-element.291, f32[1536]{0:T(1024)S(1)} %copy-done.28), channel_id=6, replica_groups=mesh['dp'=8,'tensor'=4] {'dp'}, use_global_device_ids=true, to_apply=%region_16.17.clone | all-reduce | flops 3072 | bytes 24576
  1887.6 22.2 reduce-scatter.32.cloned.1.call-done
  1909.8 65.9 %reduce-scatter.28.cloned.1.call-done = f32[192,1024]{1,0:T(8,128)} async-done(((f32[1536,1024]{1,0:T(8,128)}), f32[192,1024]{1,0:T(8,128)}) %reduce-scatter.28.cloned.1.call-update) | async-done | bytes 786448 | tf_op jit(solution)/shard_map/reduce_scatter | solution.py:224
  1975.7 65.6 %reduce-scatter.30.cloned.1.call-done = f32[192,1024]{1,0:T(8,128)} async-done(((f32[1536,1024]{1,0:T(8,128)}), f32[192,1024]{1,0:T(8,128)}) %reduce-scatter.30.cloned.1.call-update) | async-done | bytes 786448 | tf_op jit(solution)/shard_map/reduce_scatter | solution.py:225
  2041.3 42.5 %reduce-scatter.24.cloned.1.call-done = f32[192,192]{1,0:T(8,128)} async-done(((f32[1536,192]{1,0:T(8,128)}), f32[192,192]{1,0:T(8,128)}) %reduce-scatter.24.cloned.1.call-update) | async-done | bytes 147472 | tf_op jit(solution)/shard_map/reduce_scatter | solution.py:221
  2083.8 42.6 %reduce-scatter.22.cloned.1.call-done = f32[192,192]{1,0:T(8,128)} async-done(((f32[1536,192]{1,0:T(8,128)}), f32[192,192]{1,0:T(8,128)}) %reduce-scatter.22.cloned.1.call-update) | async-done | bytes 147472 | tf_op jit(solution)/shard_map/reduce_scatter | solution.py:220
  2126.4 46.8 %reduce-scatter.26.cloned.1.call-done = f32[384,192]{0,1:T(8,128)} async-done(((f32[384,1536]{0,1:T(8,128)}), f32[384,192]{0,1:T(8,128)}) %reduce-scatter.26.cloned.1.call-update) | async-done | bytes 294928 | tf_op jit(solution)/shard_map/reduce_scatter | solution.py:222
  2173.2 46.3 %reduce-scatter.20.cloned.1.call-done = f32[192,384]{1,0:T(8,128)} async-done(((f32[1536,384]{1,0:T(8,128)}), f32[192,384]{1,0:T(8,128)}) %reduce-scatter.20.cloned.1.call-update) | async-done | bytes 294928 | tf_op jit(solution)/shard_map/reduce_scatter | solution.py:219
  (307 shorter events, 629.8 us)
Async XLA Ops:
  7.2 139.6 %all-gather.10.cloned.1.call-start = ((), (), s32[]{:S(2)}) async-start(), calls=%async_computation.11 | async-start | bytes 7864320 | tf_op jit(solution)/shard_map/all_gather | solution.py:79
  31.9 139.1 %all-gather.12.cloned.1.call-start = ((), (), s32[]{:S(2)}) async-start(), calls=%async_computation.12 | async-start | bytes 1327104 | tf_op jit(solution)/shard_map/all_gather | solution.py:72
  32.6 246.5 %all-gather.14.cloned.1.call-start = ((), (), s32[]{:S(2)}) async-start(), calls=%async_computation.13 | async-start | bytes 1327104 | tf_op jit(solution)/shard_map/all_gather | solution.py:75
  33.3 467.6 %reduce-scatter.12.cloned.1.call-start = ((), (), s32[]{:S(2)}) async-start(), calls=%async_computation.14 | async-start | bytes 15728640 | tf_op jit(solution)/shard_map/reduce_scatter | solution.py:120
  288.9 247.1 %all-gather.20.cloned.1.call-start = ((), (), s32[]{:S(2)}) async-start(), calls=%async_computation.17 | async-start | bytes 3538944 | tf_op jit(solution)/shard_map/all_gather | solution.py:126
  289.5 363.9 %all-gather.16.cloned.1.call-start = ((), (), s32[]{:S(2)}) async-start(), calls=%async_computation.15 | async-start | bytes 7864320 | tf_op jit(solution)/shard_map/all_gather | solution.py:131
  505.2 180.6 %all-gather.18.cloned.1.call-start = ((), (), s32[]{:S(2)}) async-start(), calls=%async_computation.16 | async-start | bytes 3538944 | tf_op jit(solution)/shard_map/all_gather | solution.py:125
  506.0 214.1 %all-gather.22.cloned.1.call-start = ((), (), s32[]{:S(2)}) async-start(), calls=%async_computation.18 | async-start | bytes 3538944 | tf_op jit(solution)/shard_map/all_gather | solution.py:127
  506.7 330.3 %all-gather.24.cloned.1.call-start = ((), (), s32[]{:S(2)}) async-start(), calls=%async_computation.20 | async-start | bytes 7864320 | tf_op jit(solution)/shard_map/all_gather | solution.py:146
  510.4 581.6 %reduce-scatter.16.cloned.1.call-start = ((), (), s32[]{:S(2)}) async-start(), calls=%async_computation.21 | async-start | bytes 15728640 | tf_op jit(solution)/shard_map/reduce_scatter | solution.py:153
  881.7 324.4 %reduce-scatter.14.cloned.1.call-start = ((), (), s32[]{:S(2)}) async-start(), calls=%async_computation.19 | async-start | bytes 7864320 | tf_op jit(solution)/shard_map/reduce_scatter | solution.py:138
  893.3 434.3 %all-gather.26.cloned.1.call-start = ((), (), s32[]{:S(2)}) async-start(), calls=%async_computation.22 | async-start | bytes 7864320 | tf_op jit(solution)/shard_map/all_gather | solution.py:162
  1211.5 631.6 %reduce-scatter.18.cloned.1.call-start = ((), (), s32[]{:S(2)}) async-start(), calls=%async_computation.23 | async-start | bytes 15728640 | tf_op jit(solution)/shard_map/reduce_scatter | solution.py:209
  1632.8 276.9 %reduce-scatter.32.cloned.1.call-start = ((), (), s32[]{:S(2)}) async-start(), calls=%async_computation.30 | async-start | bytes 7077888 | tf_op jit(solution)/shard_map/reduce_scatter | solution.py:226
  1644.9 330.8 %reduce-scatter.28.cloned.1.call-start = ((), (), s32[]{:S(2)}) async-start(), calls=%async_computation.28 | async-start | bytes 7077888 | tf_op jit(solution)/shard_map/reduce_scatter | solution.py:224
  1657.0 384.3 %reduce-scatter.30.cloned.1.call-start = ((), (), s32[]{:S(2)}) async-start(), calls=%async_computation.29 | async-start | bytes 7077888 | tf_op jit(solution)/shard_map/reduce_scatter | solution.py:225
  1668.9 414.9 %reduce-scatter.24.cloned.1.call-start = ((), (), s32[]{:S(2)}) async-start(), calls=%async_computation.26 | async-start | bytes 1769472 | tf_op jit(solution)/shard_map/reduce_scatter | solution.py:221
  1674.8 451.6 %reduce-scatter.22.cloned.1.call-start = ((), (), s32[]{:S(2)}) async-start(), calls=%async_computation.25 | async-start | bytes 1769472 | tf_op jit(solution)/shard_map/reduce_scatter | solution.py:220
  1681.2 492.0 %reduce-scatter.26.cloned.1.call-start = ((), (), s32[]{:S(2)}) async-start(), calls=%async_computation.27 | async-start | bytes 2654208 | tf_op jit(solution)/shard_map/reduce_scatter | solution.py:222
  1688.9 154.1 %copy-start.25 = (f32[1536]{0:T(1024)S(1)}, f32[1536]{0:T(1024)}, u32[]{:S(2)}) copy-start(f32[1536]{0:T(1024)} %copy-done.24) | copy-start | bytes 18436
  1688.9 154.1 %copy-start.30 = (f32[512]{0:T(512)S(1)}, f32[512]{0:T(512)}, u32[]{:S(2)}) copy-start(f32[512]{0:T(512)} %copy-done.29) | copy-start | bytes 6148
  1689.0 530.5 %reduce-scatter.20.cloned.1.call-start = ((), (), s32[]{:S(2)}) async-start(), calls=%async_computation.24 | async-start | bytes 2654208 | tf_op jit(solution)/shard_map/reduce_scatter | solution.py:219
  1696.7 146.4 %copy-start.4 = (bf16[512,1536]{1,0:T(8,128)(2,1)S(1)}, bf16[512,1536]{1,0:T(8,128)(2,1)}, u32[]{:S(2)}) copy-start(bf16[512,1536]{1,0:T(8,128)(2,1)} %param.16) | copy-start | bytes 4718596
  1696.7 149.3 %copy-start.28 = (f32[1536]{0:T(1024)S(1)}, f32[1536]{0:T(1024)}, u32[]{:S(2)}) copy-start(f32[1536]{0:T(1024)} %get-tuple-element.289) | copy-start | bytes 18436
  (47 other events, 404.4 us)
Sparse Core Ops, SparseCore 0:
  32.0 114.7 all-gather.9
  148.6 22.2 all-gather.11
  172.8 24.0 all-gather.13
  289.0 211.8 reduce-scatter.11
  502.6 33.3 all-gather.19
  538.0 115.3 all-gather.15
  655.3 30.5 all-gather.17
  687.8 32.3 all-gather.21
  721.7 115.3 all-gather.23
  881.8 210.0 reduce-scatter.15
  1094.3 111.7 reduce-scatter.13
  1211.6 115.8 all-gather.25
  1633.0 210.0 reduce-scatter.17
  1846.9 62.8 reduce-scatter.31
  1913.9 61.7 reduce-scatter.27
  1979.5 61.7 reduce-scatter.29
  2045.3 38.4 reduce-scatter.23
  2087.9 38.4 reduce-scatter.21
  2130.7 42.4 reduce-scatter.25
  2177.0 42.4 reduce-scatter.19
where the time goes:
time: 2240 us; the launch traced here: 2230 us
  waiting for transfers between devices  1520 us (68%)
  matrix products  357 us (16%)
  other arithmetic  132 us (6%)
  local copies, waits for them, and re-layouts  122 us (5%)
  blocking collectives  72.5 us (3%)
    reduce_scatter x1, waiting for transfers between devices, local(): lax.psum_scatter(jnp.dot(part, wo_all, preferred_element_type=f32), 'tens...  211 us
    reduce_scatter x1, waiting for transfers between devices, local(): lax.psum_scatter(jnp.einsum('sf,df->sd', d_gate, wg_all, preferred_elemen...  199 us
    reduce_scatter x1, waiting for transfers between devices, local(): lax.psum_scatter(total + jnp.einsum('sh,dh->sd', d_value, wv_all, preferr...  146 us
    all_gather x1, waiting for transfers between devices, local(): lax.all_gather(normed_two.astype(bf16), 'tensor', axis=0, tiled=True)  117 us
    all_gather x1, waiting for transfers between devices, local(): lax.all_gather(grad_rows.astype(bf16), 'tensor', axis=0, tiled=True)  117 us
    all_gather x1, waiting for transfers between devices, local(): lax.all_gather(d_h_one.astype(bf16), 'tensor', axis=0, tiled=True)  116 us
    reduce_scatter x1, waiting for transfers between devices, local(): lax.psum_scatter(jnp.dot(part, wd_all, preferred_element_type=f32).astype...  111 us
    all_gather x1, waiting for transfers between devices, local(): lax.all_gather(normed_one.astype(bf16), 'tensor', axis=0, tiled=True)  84.2 us
  transfers between devices with their start and end apart: 20, of which 19 were waited for; matrix products, arithmetic and copies ran while one was open for 10% of the time, Pallas kernels for 0%

commit v1 on v0

v1 whole, which is shorter than its diff:
```python
import functools
import math

import jax
import jax.numpy as jnp
from jax import lax
from jax.experimental import pallas as pl
from jax.experimental.pallas import tpu as pltpu
from jax.sharding import PartitionSpec as P

HEAD_SIZE = 96
HALF = HEAD_SIZE // 2
GAIN_LANES = 128
CHUNKS = 4
KEY_TILE = 256
NEG = -1e30

eps_norm = 1e-05
rope_base = 100000.0
SCALE = 1.0 / math.sqrt(HEAD_SIZE)
SCALE2 = SCALE * math.log2(math.e)

f32 = jnp.float32
bf16 = jnp.bfloat16
VMEM_LIMIT = 56 * 1024 * 1024


def dot(a, b, dims=((1,), (0,))):
    return lax.dot_general(a, b, (dims, ((), ())), preferred_element_type=f32)


def params(*semantics):
    return pltpu.CompilerParams(dimension_semantics=semantics, vmem_limit_bytes=VMEM_LIMIT)


def cost(flops, nbytes, trans=0):
    return pl.CostEstimate(flops=int(flops), bytes_accessed=int(nbytes), transcendentals=int(trans))


def turn(y, cosine, sine, sign):
    parts = []
    for h in range(y.shape[0] // HEAD_SIZE):
        a = y[h * HEAD_SIZE : h * HEAD_SIZE + HALF]
        b = y[h * HEAD_SIZE + HALF : (h + 1) * HEAD_SIZE]
        parts.append(a * cosine - sign * (b * sine))
        parts.append(b * cosine + sign * (a * sine))
    return jnp.concatenate(parts, axis=0)


def qkv_kernel(nq, nk, n1_ref, w_ref, cos_ref, sin_ref, q_ref, kv_ref):
    w = w_ref[0, :, : nq + 2 * nk]
    y = dot(n1_ref[...], w).T
    cosine, sine = cos_ref[...], sin_ref[...]
    q_ref[0] = turn(y[:nq], cosine, sine, 1.0).astype(bf16)
    kv_ref[0] = turn(y[nq : nq + nk], cosine, sine, 1.0).astype(bf16)
    kv_ref[1] = y[nq + nk :].astype(bf16)


def qkv_project(n1, w, cosine, sine, nq, nk):
    rows, width = n1.shape
    zs, _, cols = w.shape
    return pl.pallas_call(
        functools.partial(qkv_kernel, nq, nk),
        grid=(zs,),
        in_specs=[
            pl.BlockSpec((rows, width), lambda z: (0, 0)),
            pl.BlockSpec((1, width, cols), lambda z: (z, 0, 0)),
            pl.BlockSpec((HALF, rows), lambda z: (0, 0)),
            pl.BlockSpec((HALF, rows), lambda z: (0, 0)),
        ],
        out_specs=[
            pl.BlockSpec((1, nq, rows), lambda z: (z, 0, 0)),
            pl.BlockSpec((2, nk, rows), lambda z: (0, z, 0)),
        ],
        out_shape=[
            jax.ShapeDtypeStruct((zs, nq, rows), bf16),
            jax.ShapeDtypeStruct((2, zs * nk, rows), bf16),
        ],
        compiler_params=params("arbitrary"),
        cost_estimate=cost(2 * rows * width * cols * zs, 2 * zs * width * cols + 8 * rows * width),
        name="qkv_project",
    )(n1, w, cosine, sine)


def out_kernel(att_ref, w_ref, x_ref, h_ref):
    z = pl.program_id(0)

    @pl.when(z == 0)
    def _():
        h_ref[...] = x_ref[...].astype(f32)

    h_ref[...] += dot(att_ref[0].T, w_ref[0], ((1,), (1,)))


def out_project(att, w, x, no, col):
    zs, _, rows = att.shape
    width = x.shape[1]
    return pl.pallas_call(
        out_kernel,
        grid=(zs,),
        in_specs=[
            pl.BlockSpec((1, no, rows), lambda z: (z, 0, 0)),
            pl.BlockSpec((1, width, no), lambda z: (z, 0, col)),
            pl.BlockSpec((rows, width), lambda z: (0, 0)),
        ],
        out_specs=pl.BlockSpec((rows, width), lambda z: (0, 0)),
        out_shape=jax.ShapeDtypeStruct((rows, width), f32),
        compiler_params=params("arbitrary"),
        cost_estimate=cost(2 * rows * width * no * zs, 2 * zs * width * no + 8 * rows * width),
        name="out_project",
    )(att, w, x)


def out_back_kernel(me_ref, dh_ref, dht_ref, att_ref, w_ref, da_ref, keep_ref, send_ref):
    w = w_ref[0]
    da_ref[0] = dot(dh_ref[...], w).T.astype(bf16)
    grad = dot(dht_ref[...], att_ref[0].T).astype(bf16)
    half = grad.shape[0] // 2
    keep_ref[0] = grad[:half]
    send_ref[0] = grad[half:]


def out_back(me, dh, dht, att, w, no, col):
    zs, _, rows = att.shape
    width = dh.shape[1]
    half = width // 2
    return pl.pallas_call(
        out_back_kernel,
        grid_spec=pltpu.PrefetchScalarGridSpec(
            num_scalar_prefetch=1,
            grid=(zs,),
            in_specs=[
                pl.BlockSpec((rows, width), lambda z, m: (0, 0)),
                pl.BlockSpec((width, rows), lambda z, m: (0, 0)),
                pl.BlockSpec((1, no, rows), lambda z, m: (z, 0, 0)),
                pl.BlockSpec((1, width, no), lambda z, m: (z, 0, col)),
            ],
            out_specs=[
                pl.BlockSpec((1, no, rows), lambda z, m: (z, 0, 0)),
                pl.BlockSpec((1, half, no), lambda z, m: (z ^ m[0], 0, 0)),
                pl.BlockSpec((1, half, no), lambda z, m: (z ^ m[0], 0, 0)),
            ],
        ),
        out_shape=[
            jax.ShapeDtypeStruct((zs, no, rows), bf16),
            jax.ShapeDtypeStruct((zs, half, no), bf16),
            jax.ShapeDtypeStruct((zs, half, no), bf16),
        ],
        compiler_params=params("arbitrary"),
        cost_estimate=cost(4 * rows * width * no * zs, 4 * zs * width * no + 8 * rows * width),
        name="out_back",
    )(me, dh, dht, att, w)


def qkv_back_kernel(
    nq, nk, me_ref, dq_ref, dkv_ref, cos_ref, sin_ref, n1t_ref, w_ref, dn_ref, keep_ref, send_ref
):
    z = pl.program_id(0)

    @pl.when(z == 0)
    def _():
        dn_ref[...] = jnp.zeros_like(dn_ref)

    cosine, sine = cos_ref[...], sin_ref[...]
    dq = turn(dq_ref[0], cosine, sine, -1.0).astype(bf16)
    dk = turn(dkv_ref[0].astype(f32), cosine, sine, -1.0).astype(bf16)
    d = jnp.concatenate([dq, dk, dkv_ref[1]], axis=0).T
    w = w_ref[0, :, : nq + 2 * nk]
    dn_ref[...] += dot(d, w, ((1,), (1,)))
    grad = dot(n1t_ref[...], d).astype(bf16)
    half = grad.shape[0] // 2
    keep_ref[0] = grad[:half]
    send_ref[0] = grad[half:]


def qkv_back(me, dq, dkv, cosine, sine, n1t, w, nq, nk):
    zs, _, rows = dq.shape
    width = n1t.shape[0]
    half = width // 2
    cols = w.shape[2]
    out = nq + 2 * nk
    return pl.pallas_call(
        functools.partial(qkv_back_kernel, nq, nk),
        grid_spec=pltpu.PrefetchScalarGridSpec(
            num_scalar_prefetch=1,
            grid=(zs,),
            in_specs=[
                pl.BlockSpec((1, nq, rows), lambda z, m: (z, 0, 0)),
                pl.BlockSpec((2, nk, rows), lambda z, m: (0, z, 0)),
                pl.BlockSpec((HALF, rows), lambda z, m: (0, 0)),
                pl.BlockSpec((HALF, rows), lambda z, m: (0, 0)),
                pl.BlockSpec((width, rows), lambda z, m: (0, 0)),
                pl.BlockSpec((1, width, cols), lambda z, m: (z, 0, 0)),
            ],
            out_specs=[
                pl.BlockSpec((rows, width), lambda z, m: (0, 0)),
                pl.BlockSpec((1, half, out), lambda z, m: (z ^ m[0], 0, 0)),
                pl.BlockSpec((1, half, out), lambda z, m: (z ^ m[0], 0, 0)),
            ],
        ),
        out_shape=[
            jax.ShapeDtypeStruct((rows, width), f32),
            jax.ShapeDtypeStruct((zs, half, out), bf16),
            jax.ShapeDtypeStruct((zs, half, out), bf16),
        ],
        compiler_params=params("arbitrary"),
        cost_estimate=cost(4 * rows * width * out * zs, 4 * zs * width * cols + 8 * rows * width),
        name="qkv_back",
    )(me, dq, dkv, cosine, sine, n1t, w)


def side_by_side(ref):
    group = ref.shape[0] // HEAD_SIZE
    return jnp.concatenate(
        [ref[a * HEAD_SIZE : (a + 1) * HEAD_SIZE] for a in range(group)], axis=1
    )


def key_mask(s, key_first, query_first, length, rows, diagonal):
    key = key_first + lax.broadcasted_iota(jnp.int32, (s.shape[0], 1), 0)
    ok = key < length
    if diagonal:
        lane = lax.broadcasted_iota(jnp.int32, s.shape, 1)
        query = query_first + lax.rem(lane, rows)
        ok = ok & (key <= query)
    return jnp.broadcast_to(ok, s.shape)


def attend_kernel(blocks, group, sc_ref, q_ref, *refs):
    kv_refs = refs[: 2 * blocks]
    o_ref, lse_ref, m_ref, l_ref, acc_ref = refs[2 * blocks :]
    z, length = sc_ref[0], sc_ref[1]
    rows = q_ref.shape[1]
    first = z * rows
    m_ref[...] = jnp.full_like(m_ref, NEG)
    l_ref[...] = jnp.zeros_like(l_ref)
    acc_ref[...] = jnp.zeros_like(acc_ref)

    for r in range(blocks):
        k_ref, v_ref = kv_refs[2 * r], kv_refs[2 * r + 1]

        @pl.when((z >= r) & (first - r * rows < length))
        def _():
            q = side_by_side(q_ref)
            for j in range(rows // KEY_TILE):
                part = slice(j * KEY_TILE, (j + 1) * KEY_TILE)
                k, v = k_ref[0, :, part], v_ref[0, :, part]
                s = dot(k, q, ((0,), (0,)))
                ok = key_mask(s, first - r * rows + j * KEY_TILE, first, length, rows, r == 0)
                s = jnp.where(ok, s, NEG)
                old = m_ref[...]
                new = jnp.maximum(old, jnp.max(s, axis=0, keepdims=True))
                shrink = jnp.exp2((old - new) * SCALE2)
                p = jnp.exp2(s * SCALE2 - new * SCALE2)
                l_ref[...] = l_ref[...] * shrink + jnp.sum(p, axis=0, keepdims=True)
                acc_ref[...] = acc_ref[...] * shrink + dot(v, p.astype(bf16))
                m_ref[...] = new

    total = l_ref[...]
    total = jnp.where(total > 0.0, total, 1.0)
    out = acc_ref[...] / total
    log_total = m_ref[...] * SCALE2 + jnp.log2(total)
    for a in range(group):
        lanes = slice(a * rows, (a + 1) * rows)
        o_ref[a * HEAD_SIZE : (a + 1) * HEAD_SIZE] = out[:, lanes].astype(bf16)
    lse_ref[0] = log_total


def attend(sc, q, kvs):
    heads_rows, rows = q.shape
    blocks = len(kvs)
    groups = kvs[0].shape[1] // HEAD_SIZE
    per = heads_rows // groups
    group = per // HEAD_SIZE
    kv_specs, kv_args = [], []
    for kv in kvs:
        for which in (0, 1):
            kv_specs.append(
                pl.BlockSpec((1, HEAD_SIZE, rows), lambda g, s, which=which: (which, g, 0))
            )
            kv_args.append(kv)
    work = heads_rows // HEAD_SIZE * rows * rows * blocks
    return pl.pallas_call(
        functools.partial(attend_kernel, blocks, group),
        grid_spec=pltpu.PrefetchScalarGridSpec(
            num_scalar_prefetch=1,
            grid=(groups,),
            in_specs=[pl.BlockSpec((per, rows), lambda g, s: (g, 0))] + kv_specs,
            out_specs=[
                pl.BlockSpec((per, rows), lambda g, s: (g, 0)),
                pl.BlockSpec((1, 1, group * rows), lambda g, s: (g, 0, 0)),
            ],
            scratch_shapes=[
                pltpu.VMEM((1, group * rows), f32),
                pltpu.VMEM((1, group * rows), f32),
                pltpu.VMEM((HEAD_SIZE, group * rows), f32),
            ],
        ),
        out_shape=[
            jax.ShapeDtypeStruct((heads_rows, rows), bf16),
            jax.ShapeDtypeStruct((groups, 1, group * rows), f32),
        ],
        compiler_params=params("arbitrary"),
        cost_estimate=cost(4 * work * HEAD_SIZE, 2 * (blocks + 2) * heads_rows * rows, work),
        name="attend",
    )(sc, q, *kv_args)


def mlp_kernel(
    tile, first, me_ref, n2_ref, n2t_ref, g_ref, gt_ref, w_ref, *refs
):
    if first:
        out_ref, dn_ref, keep_ref, send_ref = refs
    else:
        out_in, dn_in, out_ref, dn_ref, keep_ref, send_ref = refs
    z = pl.program_id(0)

    @pl.when(z == 0)
    def _():
        if first:
            out_ref[...] = jnp.zeros_like(out_ref)
            dn_ref[...] = jnp.zeros_like(dn_ref)
        else:
            out_ref[...] = out_in[...]
            dn_ref[...] = dn_in[...]

    wg = w_ref[0, :, :tile]
    wu = w_ref[0, :, tile : 2 * tile]
    wd = w_ref[0, :, 2 * tile : 3 * tile]
    n2, g = n2_ref[...], g_ref[...]
    gate = dot(n2, wg)
    up = dot(n2, wu)
    d_hidden = dot(g, wd)
    sigma = 1.0 / (1.0 + jnp.exp(-gate))
    active = gate * sigma
    hidden = (active * up).astype(bf16)
    d_gate = (d_hidden * up * (sigma * (1.0 + gate * (1.0 - sigma)))).astype(bf16)
    d_up = (d_hidden * active).astype(bf16)
    out_ref[...] += dot(hidden, wd, ((1,), (1,)))
    dn_ref[...] += dot(d_gate, wg, ((1,), (1,))) + dot(d_up, wu, ((1,), (1,)))
    half = n2t_ref.shape[0] // 2
    for ref, rows in ((keep_ref, slice(0, half)), (send_ref, slice(half, 2 * half))):
        n2t, gt = n2t_ref[rows], gt_ref[rows]
        ref[0, :, :tile] = dot(n2t, d_gate).astype(bf16)
        ref[0, :, tile : 2 * tile] = dot(n2t, d_up).astype(bf16)
        ref[0, :, 2 * tile :] = dot(gt, hidden).astype(bf16)


def mlp(me, n2, n2t, g, gt, w, chunk, tile, carry):
    rows, width = n2.shape
    zs = w.shape[0]
    half = width // 2
    full = pl.BlockSpec((rows, width), lambda z, m: (0, 0))
    full_t = pl.BlockSpec((width, rows), lambda z, m: (0, 0))
    grad_spec = pl.BlockSpec((1, half, 3 * tile), lambda z, m: (z ^ m[0], 0, 0))
    first = carry is None
    in_specs = [
        full,
        full_t,
        full,
        full_t,
        pl.BlockSpec((1, width, 3 * tile), lambda z, m: (z, 0, chunk)),
    ]
    args = [me, n2, n2t, g, gt, w]
    aliases = {}
    if not first:
        in_specs += [full, full]
        aliases = {6: 0, 7: 1}
        args += list(carry)
    return pl.pallas_call(
        functools.partial(mlp_kernel, tile, first),
        grid_spec=pltpu.PrefetchScalarGridSpec(
            num_scalar_prefetch=1,
            grid=(zs,),
            in_specs=in_specs,
            out_specs=[full, full, grad_spec, grad_spec],
        ),
        out_shape=[
            jax.ShapeDtypeStruct((rows, width), f32),
            jax.ShapeDtypeStruct((rows, width), f32),
            jax.ShapeDtypeStruct((zs, half, 3 * tile), bf16),
            jax.ShapeDtypeStruct((zs, half, 3 * tile), bf16),
        ],
        input_output_aliases=aliases,
        compiler_params=params("arbitrary"),
        cost_estimate=cost(
            18 * rows * width * tile * zs, 4 * zs * width * 3 * tile + 24 * rows * width
        ),
        name="mlp",
    )(*args)


def pairs(count, mask):
    return [(i, i ^ mask) for i in range(count)]


def bits_of(count):
    return [1 << b for b in range(count.bit_length() - 1)]


def relative_order(count):
    return [r for low in (0, 1) for r in range(count) if (r & 1) == low]


def to_relative(rows_first, me, count):
    block = rows_first.shape[0] // count
    parts = [
        lax.dynamic_slice_in_dim(rows_first, (me ^ r) * block, block, axis=0)
        for r in relative_order(count)
    ]
    return jnp.concatenate(parts, axis=0)


def reduce_small(values, me, n_dp, n_t):
    order = relative_order(n_dp)
    buf = values
    left = n_dp
    buf = buf[: left // 2] + lax.ppermute(buf[left // 2 :], "dp", pairs(n_dp, 1))
    left //= 2
    for bit in [b for b in bits_of(n_dp) if b > 1][::-1]:
        buf = buf[: left // 2] + lax.ppermute(buf[left // 2 :], "dp", pairs(n_dp, bit))
        left //= 2
    buf = buf[0]
    for bit in bits_of(n_t):
        buf = buf + lax.ppermute(buf, "tensor", pairs(n_t, bit))
    return buf


MESH = pl.DeviceIdType.MESH


def log2(n):
    return n.bit_length() - 1


def nearest_first(n_t):
    return [sorted(range(n_t), key=lambda p: (abs(p - z), p)) for z in range(n_t)]


def pick(values, z):
    out = jnp.int32(values[0])
    for i in range(1, len(values)):
        out = jnp.where(z == i, jnp.int32(values[i]), out)
    return out


def neighbours(n_dp, n_t, me, z):
    barrier = pltpu.get_barrier_semaphore()
    masks = [1 << b for b in range(log2(n_dp))]
    for mask in masks:
        pl.semaphore_signal(barrier, 1, device_id=(me ^ mask, z), device_id_type=MESH)

    @pl.when(z > 0)
    def _():
        pl.semaphore_signal(barrier, 1, device_id=(me, z - 1), device_id_type=MESH)

    @pl.when(z < n_t - 1)
    def _():
        pl.semaphore_signal(barrier, 1, device_id=(me, z + 1), device_id_type=MESH)

    count = len(masks) + (z > 0).astype(jnp.int32) + (z < n_t - 1).astype(jnp.int32)
    pl.semaphore_wait(barrier, count)


class Gather:
    def __init__(self, n_dp, n_t, me, z, index, shard, whole, sems):
        self.n_dp, self.n_t, self.me, self.z = n_dp, n_t, me, z
        self.index, self.shard, self.whole = index, shard, whole
        self.own, self.z_send, self.z_recv, self.x_send, self.x_recv = sems
        self.bits = log2(n_dp) - 1

    def local(self):
        return pltpu.make_async_copy(
            self.shard, self.whole.at[self.z, self.me], self.own.at[self.index]
        )

    def hop(self, piece, direction, hops):
        source = self.whole.at[piece, self.me]
        step = 1 - 2 * direction
        return pltpu.make_async_remote_copy(
            source,
            source,
            self.z_send.at[self.index, direction, hops],
            self.z_recv.at[self.index, direction, hops],
            device_id=(self.me, jnp.clip(self.z + step, 0, self.n_t - 1)),
            device_id_type=MESH,
        )

    def send_own(self):
        local = self.local()
        local.start()
        local.wait()

        @pl.when(self.z < self.n_t - 1)
        def _():
            self.hop(self.z, 0, 0).start()

        @pl.when(self.z > 0)
        def _():
            self.hop(self.z, 1, 0).start()

    def order(self, k):
        return pick([row[k] for row in nearest_first(self.n_t)], self.z)

    def arrive(self, k):
        if k == 0:
            return
        piece = self.order(k)
        direction = (piece > self.z).astype(jnp.int32)
        hops = jnp.abs(piece - self.z)
        self.hop(piece, direction, hops - 1).wait_recv()
        on = jnp.where(direction == 0, self.z < self.n_t - 1, self.z > 0)

        @pl.when(on)
        def _():
            self.hop(piece, direction, hops).start()

    def doubling(self, k, stage, i, incoming=False):
        piece = self.order(k)
        odd = (piece & 1) == 1
        bit = jnp.where(odd, 1 << (self.bits - stage), 2 << stage)
        shift = jnp.where(odd, self.bits - stage + 1, 1)
        partner = self.me ^ bit
        origin = partner if incoming else self.me
        held = self.whole.at[piece, origin ^ (i << shift)]
        at = (1 << stage) - 1 + i
        return pltpu.make_async_remote_copy(
            held,
            held,
            self.x_send.at[self.index, k, at],
            self.x_recv.at[self.index, k, at],
            device_id=(partner, self.z),
            device_id_type=MESH,
        )

    def core(self, k, i, incoming=False):
        piece = self.order(k)
        partner = self.me ^ 1
        origin = partner if incoming else self.me
        held = self.whole.at[piece, origin ^ (i << 1)]
        at = (1 << self.bits) - 1 + i
        return pltpu.make_async_remote_copy(
            held,
            held,
            self.x_send.at[self.index, k, at],
            self.x_recv.at[self.index, k, at],
            device_id=(partner, self.z),
            device_id_type=MESH,
        )

    def each(self, count, body):
        if count <= 4:
            for i in range(count):
                body(i)
        else:
            lax.fori_loop(0, count, lambda i, _: (body(i), 0)[1], 0)

    def spread(self, k, stage):
        if stage > 0:
            self.each(1 << (stage - 1), lambda i: self.doubling(k, stage - 1, i, True).wait_recv())
        if stage < self.bits:
            self.each(1 << stage, lambda i: self.doubling(k, stage, i).start())
        else:
            self.each(1 << self.bits, lambda i: self.core(k, i).start())

    def finish(self, k):
        self.each(1 << self.bits, lambda i: self.core(k, i, True).wait_recv())
        for stage in range(self.bits):
            self.each(1 << stage, lambda i: self.doubling(k, stage, i).wait_send())
        self.each(1 << self.bits, lambda i: self.core(k, i).wait_send())
        piece = self.order(k)
        hops = jnp.abs(piece - self.z)
        if k == 0:

            @pl.when(self.z < self.n_t - 1)
            def _():
                self.hop(piece, 0, 0).wait_send()

            @pl.when(self.z > 0)
            def _():
                self.hop(piece, 1, 0).wait_send()
        else:
            direction = (piece > self.z).astype(jnp.int32)
            on = jnp.where(direction == 0, self.z < self.n_t - 1, self.z > 0)

            @pl.when(on)
            def _():
                self.hop(piece, direction, hops).wait_send()


class Climb:
    def __init__(self, n_t, me, z, own, kept, sems):
        self.n_t, self.me, self.z, self.own, self.kept = n_t, me, z, own, kept
        self.send, self.recv = sems

    def hop(self, r):
        source = self.own if r == 0 else self.kept[r - 1]
        return pltpu.make_async_remote_copy(
            source,
            self.kept[r],
            self.send.at[r],
            self.recv.at[r],
            device_id=(self.me, jnp.minimum(self.z + 1, self.n_t - 1)),
            device_id_type=MESH,
        )

    def start(self, r):
        @pl.when((self.z >= r) & (self.z < self.n_t - 1))
        def _():
            self.hop(r).start()

    def arrive(self, r):
        @pl.when(self.z >= r)
        def _():
            self.hop(r - 1).wait_recv()

    def finish(self, r):
        @pl.when((self.z >= r) & (self.z < self.n_t - 1))
        def _():
            self.hop(r).wait_send()


def gather_kernel(n_dp, n_t, count, climbs, *refs):
    shards, refs = refs[:count], refs[count:]
    if climbs:
        own, refs = refs[0], refs[1:]
    wholes, refs = refs[:count], refs[count:]
    if climbs:
        kept, refs = refs[: n_t - 1], refs[n_t - 1 :]
    sems, refs = refs[:5], refs[5:]
    me, z = lax.axis_index("dp"), lax.axis_index("tensor")
    neighbours(n_dp, n_t, me, z)
    works = [
        Gather(n_dp, n_t, me, z, c, shards[c], wholes[c], sems) for c in range(count)
    ]
    climb = Climb(n_t, me, z, own, kept, refs) if climbs else None
    stages = log2(n_dp)
    works[0].send_own()
    if climbs:
        climb.start(0)
    total = count * n_t
    passed = 0
    for n in range(total + 2 * (stages - 1)):
        if n < total:
            c, k = divmod(n, n_t)
            works[c].arrive(k)
            works[c].spread(k, 0)
            if k == 0 and c + 1 < count:
                works[c + 1].send_own()
            if climbs and n in (5, 9, 13)[: n_t - 1]:
                passed += 1
                climb.arrive(passed)
                if passed < n_t - 1:
                    climb.start(passed)
        for stage in range(1, stages):
            at = n - 2 * stage
            if 0 <= at < total:
                works[at // n_t].spread(at % n_t, stage)
    for c in range(count):
        for k in range(n_t):
            works[c].finish(k)
    if climbs:
        for r in range(n_t - 1):
            climb.finish(r)


def gather(shards, n_dp, n_t, collective_id, own=None):
    count = len(shards)
    shapes = [
        jax.ShapeDtypeStruct((n_t, n_dp) + s.shape, s.dtype) for s in shards
    ]
    args = list(shards)
    scratch = [
        pltpu.SemaphoreType.DMA((count,)),
        pltpu.SemaphoreType.DMA((count, 2, n_t)),
        pltpu.SemaphoreType.DMA((count, 2, n_t)),
        pltpu.SemaphoreType.DMA((count, n_t, n_dp - 1)),
        pltpu.SemaphoreType.DMA((count, n_t, n_dp - 1)),
    ]
    if own is not None:
        args.append(own)
        shapes += [jax.ShapeDtypeStruct(own.shape, own.dtype)] * (n_t - 1)
        scratch += [pltpu.SemaphoreType.DMA((n_t,))] * 2
    anywhere = pl.BlockSpec(memory_space=pl.ANY)
    return pl.pallas_call(
        functools.partial(gather_kernel, n_dp, n_t, count, own is not None),
        in_specs=[anywhere] * len(args),
        out_specs=[anywhere] * len(shapes),
        out_shape=shapes,
        scratch_shapes=scratch,
        compiler_params=pltpu.CompilerParams(collective_id=collective_id, has_side_effects=True),
        name="gather_weights",
    )(*args)


def greet_all(n_dp, n_t, me, z):
    barrier = pltpu.get_barrier_semaphore()
    masks = [1 << b for b in range(log2(n_dp))]
    for mask in masks:
        pl.semaphore_signal(barrier, 1, device_id=(me ^ mask, z), device_id_type=MESH)
    for other in range(1, n_t):
        pl.semaphore_signal(barrier, 1, device_id=(me, z ^ other), device_id_type=MESH)
    pl.semaphore_wait(barrier, len(masks) + n_t - 1)


def count_of(shape):
    return math.prod(shape)


def add_blocks(target, source, dtype=bf16):
    lead = target.shape[:-2]

    def body(i, _):
        at = []
        for extent in lead[::-1]:
            at.append(lax.rem(i, extent))
            i = i // extent
        at = tuple(at[::-1])
        target[at] = (target[at].astype(f32) + source[at].astype(f32)).astype(dtype)
        return 0

    lax.fori_loop(0, count_of(lead), body, 0)


class Scatter:
    def __init__(self, n_dp, n_t, me, z, index, keep, send, land, out, held, tile, landings, sems):
        self.n_t, self.me, self.z, self.index = n_t, me, z, index
        self.keep, self.send, self.land, self.out, self.held = keep, send, land, out, held
        self.tile, self.landings, self.sems = tile, landings, sems
        self.bits, self.t_bits = log2(n_dp) - 1, log2(n_t)
        self.stages = 2 + self.bits + self.t_bits
        self.cols = held.shape[-1]

    def remote(self, source, target, slot, dp, z):
        send, recv = self.sems[0], self.sems[1]
        return pltpu.make_async_remote_copy(
            source,
            target,
            send.at[self.index, slot],
            recv.at[self.index, slot],
            device_id=(dp, z),
            device_id_type=MESH,
        )

    def load(self):
        return pltpu.make_async_copy(self.keep, self.held, self.sems[2].at[self.index])

    def core(self):
        return self.remote(self.send, self.land, 0, self.me ^ 1, self.z)

    def part(self, half, stage, bit):
        rest = (slice(None),) * (self.bits - 1 - stage)
        done = (0,) * stage
        if half == 0:
            return self.held.at[(slice(0, self.n_t // 2),) + rest + (bit,) + done]
        return self.held.at[(slice(self.n_t // 2, self.n_t),) + done + (bit,) + rest]

    def landing(self, which):
        ref = self.landings[which]
        at = (self.index % 2,) + (slice(None),) * (len(ref.shape) - 2) + (slice(0, self.cols),)
        return ref.at[at]

    def plane(self, half, stage):
        mask = 2 << stage if half == 0 else 1 << (self.bits - stage)
        return self.remote(
            self.part(half, stage, 1),
            self.landing(2 * stage + half),
            1 + 2 * stage + half,
            self.me ^ mask,
            self.z,
        )

    def column(self, stage, first, count):
        return self.held.at[(slice(first, first + count),) + (0,) * self.bits]

    def along(self, stage):
        count = self.n_t >> (stage + 1)
        return self.remote(
            self.column(stage, count, count),
            self.landing(2 * self.bits + stage),
            1 + 2 * self.bits + stage,
            self.me,
            self.z ^ count,
        )

    def start(self, stage):
        if stage < self.bits:
            self.plane(0, stage).start()
            self.plane(1, stage).start()
        elif stage < self.bits + self.t_bits:
            self.along(stage - self.bits).start()

    def event(self, number):
        if number == 0:
            self.core().start()
            self.load().start()
        elif number == 1:
            self.load().wait()
            self.core().wait_recv()
            self.add_land()
            self.start(0)
        elif number <= 1 + self.bits:
            stage = number - 2
            for half in (0, 1):
                self.plane(half, stage).wait_recv()
                add_blocks(self.part(half, stage, 0), self.landing(2 * stage + half))
            self.start(stage + 1)
        else:
            stage = number - 2 - self.bits
            self.along(stage).wait_recv()
            count = self.n_t >> (stage + 1)
            if stage < self.t_bits - 1:
                add_blocks(
                    self.column(stage, 0, count), self.landing(2 * self.bits + stage)
                )
                self.start(number - 1)
            else:
                mine = self.held[(0,) * (1 + self.bits)].astype(f32)
                got = self.landing(2 * self.bits + stage)[0].astype(f32)
                self.out[...] = mine + got

    def add_land(self):
        lead = self.held.shape[:-2]

        def at_of(i):
            at = []
            for extent in lead[::-1]:
                at.append(lax.rem(i, extent))
                i = i // extent
            return tuple(at[::-1])

        def fetch(i):
            return pltpu.make_async_copy(
                self.land.at[at_of(i)],
                self.tile.at[lax.rem(i, 2), :, pl.ds(0, self.cols)],
                self.sems[3].at[lax.rem(i, 2)],
            )

        total = count_of(lead)
        fetch(0).start()

        def body(i, _):
            @pl.when(i + 1 < total)
            def _():
                fetch(i + 1).start()

            fetch(i).wait()
            at = at_of(i)
            got = self.tile[lax.rem(i, 2), :, pl.ds(0, self.cols)].astype(f32)
            self.held[at] = (self.held[at].astype(f32) + got).astype(bf16)
            return 0

        lax.fori_loop(0, total, body, 0)

    def finish(self):
        self.core().wait_send()
        for stage in range(self.bits):
            for half in (0, 1):
                self.plane(half, stage).wait_send()
        for stage in range(self.t_bits):
            self.along(stage).wait_send()


class Descend:
    def __init__(self, n_t, me, z, sums, landed, sems):
        self.n_t, self.me, self.z = n_t, me, z
        self.sums, self.landed, self.send, self.recv = sums, landed, sems[0], sems[1]

    def hop(self, r):
        return pltpu.make_async_remote_copy(
            self.sums[r],
            self.landed[r - 1],
            self.send.at[r],
            self.recv.at[r],
            device_id=(self.me, jnp.maximum(self.z - 1, 0)),
            device_id_type=MESH,
        )

    def start(self, r):
        @pl.when(self.z >= r)
        def _():
            self.hop(r).start()

    def finish(self, r):
        @pl.when(self.z >= r)
        def _():
            self.hop(r).wait_send()


def attention_part(r, group, n_t, z, length, q_ref, do_ref, lse_ref, delta_ref, kv_ref, got_ref, dq_ref, sum_ref):
    rows = q_ref.shape[1]
    groups = lse_ref.shape[0]
    per = group * HEAD_SIZE
    first = z * rows
    active = z >= r
    fresh = r == n_t - 1

    def beside(ref, base):
        return jnp.concatenate(
            [ref[pl.ds(base + a * HEAD_SIZE, HEAD_SIZE), :] for a in range(group)], axis=1
        )

    @pl.when(active)
    def _():
        def body(g, _):
            base = pl.multiple_of(g * per, 32)
            at = pl.multiple_of(g * HEAD_SIZE, 32)
            q = beside(q_ref, base)
            do = beside(do_ref, base)
            delta, lse = delta_ref[g], lse_ref[g]
            dq = jnp.zeros(q.shape, f32)
            for j in range(rows // KEY_TILE):
                part = slice(j * KEY_TILE, (j + 1) * KEY_TILE)
                k, v = kv_ref[0, pl.ds(at, HEAD_SIZE), part], kv_ref[1, pl.ds(at, HEAD_SIZE), part]
                s = dot(k, q, ((0,), (0,)))
                ok = key_mask(s, first - r * rows + j * KEY_TILE, first, length, rows, r == 0)
                p = jnp.where(ok, jnp.exp2(s * SCALE2 - lse), 0.0)
                dp = dot(v, do, ((0,), (0,)))
                ds = (p * (dp - delta)).astype(bf16)
                dv = dot(do, p.astype(bf16), ((1,), (1,)))
                dk = dot(q, ds, ((1,), (1,))) * SCALE
                sum_ref[0, pl.ds(at, HEAD_SIZE), part] = dk.astype(bf16)
                sum_ref[1, pl.ds(at, HEAD_SIZE), part] = dv.astype(bf16)
                dq += dot(k, ds)
            for a in range(group):
                own = pl.ds(base + a * HEAD_SIZE, HEAD_SIZE)
                term = dq[:, a * rows : (a + 1) * rows] * SCALE
                if fresh:
                    dq_ref[own, :] = term
                else:
                    dq_ref[own, :] += term
            return 0

        lax.fori_loop(0, groups, body, 0)

    @pl.when(jnp.logical_not(active))
    def _():
        sum_ref[...] = jnp.zeros_like(sum_ref)
        if fresh:
            dq_ref[...] = jnp.zeros_like(dq_ref)


def scatter_kernel(n_dp, n_t, count, group, *refs):
    refs = list(refs)

    def take(k):
        out = refs[:k]
        del refs[:k]
        return out

    attention = group > 0
    keeps, sends = take(count), take(count)
    if attention:
        (sc_ref, q_ref, do_ref, lse_ref, delta_ref) = take(5)
        kvs = take(n_t)
    lands, outs = take(count), take(count)
    if attention:
        dq_ref, dkv_ref = take(2)
    helds = take(count)
    (tile,) = take(1)
    landings = take(2 * (log2(n_dp) - 1) + log2(n_t))
    sems = take(4)
    me, z = lax.axis_index("dp"), lax.axis_index("tensor")
    greet_all(n_dp, n_t, me, z)
    works = [
        Scatter(
            n_dp, n_t, me, z, c, keeps[c], sends[c], lands[c], outs[c], helds[c], tile, landings, sems
        )
        for c in range(count)
    ]
    stages = works[0].stages

    def tick(k):
        for number in range(stages - 1, 0, -1):
            c = k - (number - 1)
            if 0 <= c < count:
                works[c].event(number)
        if k + 2 < count:
            works[k + 2].event(0)

    works[0].event(0)
    if count > 1:
        works[1].event(0)
    ticks = list(range(count + stages - 2))
    if attention:
        sums = take(n_t - 1)
        landed = take(n_t - 1)
        chain_sems = take(2)
        length = sc_ref[1]
        descend = Descend(n_t, me, z, [dkv_ref] + sums, landed, chain_sems)
        for r in range(n_t - 1, -1, -1):
            target = dkv_ref if r == 0 else sums[r - 1]
            attention_part(
                r, group, n_t, z, length, q_ref, do_ref, lse_ref, delta_ref, kvs[r], None, dq_ref, target
            )
            if r < n_t - 1:
                @pl.when((z + 1 < n_t) & (z >= r))
                def _():
                    descend.hop(r + 1).wait_recv()
                    add_blocks(target, landed[r])

            if r > 0:
                descend.start(r)
            tick(ticks.pop(0))
    for k in ticks:
        tick(k)
    for work in works:
        work.finish()
    if attention:
        for r in range(1, n_t):
            descend.finish(r)


def scatter(keeps, sends, n_dp, n_t, collective_id, attention=None):
    count = len(keeps)
    bits = log2(n_dp) - 1
    block = keeps[0].shape[1] >> bits
    widest = max(k.shape[2] for k in keeps)
    shapes = [(n_t,) + (2,) * bits + (block, k.shape[2]) for k in keeps]
    args = [k.reshape(s) for k, s in zip(keeps, shapes)] + [
        k.reshape(s) for k, s in zip(sends, shapes)
    ]
    anywhere = pl.BlockSpec(memory_space=pl.ANY)
    vmem = pl.BlockSpec(memory_space=pltpu.VMEM)
    smem = pl.BlockSpec(memory_space=pltpu.SMEM)
    in_specs = [anywhere] * len(args)
    out_shape = [jax.ShapeDtypeStruct(s, bf16) for s in shapes] + [
        jax.ShapeDtypeStruct((block, s[-1]), f32) for s in shapes
    ]
    out_specs = [anywhere] * count + [vmem] * count
    scratch = [pltpu.VMEM(s, bf16) for s in shapes]
    scratch.append(pltpu.VMEM((2, block, widest), bf16))
    for stage in range(bits):
        for _ in (0, 1):
            scratch.append(
                pltpu.VMEM((2, n_t // 2) + (2,) * (bits - 1 - stage) + (block, widest), bf16)
            )
    for stage in range(log2(n_t)):
        scratch.append(pltpu.VMEM((2, n_t >> (stage + 1), block, widest), bf16))
    copies = 1 + 2 * bits + log2(n_t)
    scratch += [
        pltpu.SemaphoreType.DMA((count, copies)),
        pltpu.SemaphoreType.DMA((count, copies)),
        pltpu.SemaphoreType.DMA((count,)),
        pltpu.SemaphoreType.DMA((2,)),
    ]
    group = 0
    if attention is not None:
        sc, q, do, lse, delta, kvs = attention
        args += [sc, q, do, lse, delta] + list(kvs)
        in_specs += [smem] + [vmem] * (4 + n_t)
        group = q.shape[0] // kvs[0].shape[1]
        out_shape += [jax.ShapeDtypeStruct(q.shape, f32), jax.ShapeDtypeStruct(kvs[0].shape, bf16)]
        out_specs += [vmem, vmem]
        scratch += [pltpu.VMEM(kvs[0].shape, bf16)] * (2 * (n_t - 1))
        scratch += [pltpu.SemaphoreType.DMA((n_t,))] * 2
    outs = pl.pallas_call(
        functools.partial(scatter_kernel, n_dp, n_t, count, group),
        in_specs=in_specs,
        out_specs=out_specs,
        out_shape=out_shape,
        scratch_shapes=scratch,
        compiler_params=pltpu.CompilerParams(
            collective_id=collective_id, has_side_effects=True, vmem_limit_bytes=62 * 1024 * 1024
        ),
        name="scatter_grads",
    )(*args)
    return outs[count:]


def local(
    n_dp,
    n_t,
    tokens,
    lengths,
    cotangent,
    attn_gain,
    query_weight,
    key_matrix,
    value_matrix,
    out_weight,
    mlp_gain,
    gate_weight,
    up_weight,
    down_weight,
):
    rows, width = tokens.shape
    block = query_weight.shape[0]
    nq, nk = query_weight.shape[1], key_matrix.shape[1]
    no = out_weight.shape[0]
    units = gate_weight.shape[1]
    tile = units // CHUNKS
    me_dp = lax.axis_index("dp")
    me_t = lax.axis_index("tensor")
    length = lengths[0]
    me = jnp.stack([me_t, me_t]).astype(jnp.int32)
    sc = jnp.stack([me_t.astype(jnp.int32), length])

    gains = jnp.stack([attn_gain, mlp_gain], axis=1)
    gains = jnp.pad(gains, ((0, 0), (0, GAIN_LANES - 2)))
    shard_qkv = jnp.concatenate([query_weight, key_matrix, value_matrix, gains], axis=1)
    down_t = down_weight.T
    shard_mlp = []
    for c in range(CHUNKS):
        cols = slice(c * tile, (c + 1) * tile)
        shard_mlp.append(
            jnp.concatenate([gate_weight[:, cols], up_weight[:, cols], down_t[:, cols]], axis=1)
        )
    (w_qkv,) = gather([shard_qkv], n_dp, n_t, 0)
    w_qkv = w_qkv.reshape(n_t, width, shard_qkv.shape[1])
    gain_cols = w_qkv[0, :, nq + 2 * nk : nq + 2 * nk + 2].astype(f32)
    gain_one, gain_two = gain_cols[:, 0], gain_cols[:, 1]

    position = (me_t * rows + jnp.arange(rows, dtype=jnp.int32)).astype(f32)
    freqs = rope_base ** (-(jnp.arange(HALF, dtype=f32) * 2.0) / HEAD_SIZE)
    angles = freqs[:, None] * position[None, :]
    cosine, sine = jnp.cos(angles), jnp.sin(angles)
    live = (me_t * rows + jnp.arange(rows, dtype=jnp.int32) < length).astype(f32)[:, None]
    x = tokens.astype(f32)
    inv_one = lax.rsqrt(jnp.mean(x * x, axis=1, keepdims=True) + eps_norm)
    g32 = cotangent.astype(f32) * live
    g = g32.astype(bf16)
    gt = to_relative(g.T, me_dp, n_dp)
    n1 = (x * inv_one * gain_one).astype(bf16)
    q, kv = qkv_project(n1, w_qkv, cosine, sine, nq, nk)
    q = q.reshape(n_t * nq, rows)

    *w_all, = gather([out_weight.T] + shard_mlp, n_dp, n_t, 1, kv)
    kvs = [kv] + w_all[1 + CHUNKS :]
    w_all = w_all[: 1 + CHUNKS]
    w_out, *w_mlp = [w.reshape(n_t, width, w.shape[-1]) for w in w_all]
    att, lse = attend(sc, q, kvs)
    att_z = att.reshape(n_t, no, rows)
    h_one = out_project(att_z, w_out, tokens, no, 0)

    inv_two = lax.rsqrt(jnp.mean(h_one * h_one, axis=1, keepdims=True) + eps_norm)
    n2 = (h_one * inv_two * gain_two).astype(bf16)
    n2t = to_relative(n2.T, me_dp, n_dp)
    carry = None
    shares = []
    for c in range(CHUNKS):
        out_sum, dn_sum, keep, send = mlp(me, n2, n2t, g, gt, w_mlp[c], 0, tile, carry)
        carry = (out_sum, dn_sum)
        shares.append((keep, send))
    mlp_out, d_n2 = carry
    block_out = (live * (h_one + mlp_out)).astype(bf16)

    scaled = d_n2 * gain_two
    inner = jnp.mean(scaled * h_one, axis=1, keepdims=True)
    gain_two_part = jnp.sum(d_n2 * h_one * inv_two, axis=0)
    d_h = g32 + inv_two * scaled - h_one * (inv_two * inv_two * inv_two * inner)
    d_h_low = d_h.astype(bf16)
    d_h_t = to_relative(d_h_low.T, me_dp, n_dp)
    d_att, keep, send = out_back(me, d_h_low, d_h_t, att_z, w_out, no, 0)
    shares.append((keep, send))

    d_att = d_att.reshape(n_t * no, rows)
    groups, _, lanes = lse.shape
    delta = (d_att.astype(f32) * att.astype(f32)).reshape(groups, -1, HEAD_SIZE, rows).sum(axis=2)
    delta = delta.reshape(groups, 1, lanes)
    *grads, out_share, d_q, d_kv = scatter(
        [s[0] for s in shares],
        [s[1] for s in shares],
        n_dp,
        n_t,
        2,
        (sc, q, d_att, lse, delta, kvs),
    )
    n1t = to_relative(n1.T, me_dp, n_dp)
    d_n1, keep, send = qkv_back(
        me, d_q.reshape(n_t, nq, rows), d_kv, cosine, sine, n1t, w_qkv, nq, nk
    )
    middle = nq
    q_share, kv_share = scatter(
        [keep[:, :, :middle], keep[:, :, middle:]], [send[:, :, :middle], send[:, :, middle:]], n_dp, n_t, 3
    )

    scaled = d_n1 * gain_one
    inner = jnp.mean(scaled * x, axis=1, keepdims=True)
    gain_one_part = jnp.sum(d_n1 * x * inv_one, axis=0)
    d_x = inv_one * scaled - x * (inv_one * inv_one * inv_one * inner)
    tokens_grad = (d_h + d_x).astype(bf16)

    gain_parts = jnp.stack([gain_one_part.reshape(n_dp, block), gain_two_part.reshape(n_dp, block)], 1)
    gain_parts = to_relative(gain_parts, me_dp, n_dp)
    gain_share = reduce_small(gain_parts, me_dp, n_dp, n_t)

    gate_share = jnp.concatenate([s[:, :tile] for s in grads], axis=1)
    up_share = jnp.concatenate([s[:, tile : 2 * tile] for s in grads], axis=1)
    down_share = jnp.concatenate([s[:, 2 * tile :].T for s in grads], axis=0)
    return (
        block_out,
        tokens_grad,
        gain_share[0],
        q_share,
        kv_share[:, :nk],
        kv_share[:, nk:],
        out_share.T,
        gain_share[1],
        gate_share,
        up_share,
        down_share,
    )


def solution(mesh):
    in_specs = (
        P(("dp", "tensor"), None),
        P("dp"),
        P(("dp", "tensor"), None),
        P("dp"),
        P("dp", "tensor"),
        P("dp", "tensor"),
        P("dp", "tensor"),
        P("tensor", "dp"),
        P("dp"),
        P("dp", "tensor"),
        P("dp", "tensor"),
        P("tensor", "dp"),
    )
    out_specs = (
        P(("dp", "tensor"), None),
        P(("dp", "tensor"), None),
        P("dp"),
        P("dp", "tensor"),
        P("dp", "tensor"),
        P("dp", "tensor"),
        P("tensor", "dp"),
        P("dp"),
        P("dp", "tensor"),
        P("dp", "tensor"),
        P("tensor", "dp"),
    )
    fn = functools.partial(local, mesh.shape["dp"], mesh.shape["tensor"])
    return jax.shard_map(fn, mesh=mesh, in_specs=in_specs, out_specs=out_specs, check_vma=False)
```

time: 2240 us -> 1030 us (0.46)
  waiting for transfers between devices: 1520 us -> 0.57 us
  Pallas kernels: 0 us -> 878 us
  matrix products: 357 us -> 0 us
  other arithmetic: 132 us -> 32.6 us
  blocking collectives: 72.5 us -> 0 us
  local copies, waits for them, and re-layouts: 122 us -> 96.8 us
    reduce_scatter x11 -> x0, waiting for transfers between devices: 998 us -> none  [the longest x1 211 us: local(): lax.psum_scatter(jnp.dot(part, wo_all, preferred_element_type=f32), 'tens...]
    pallas_call x0 -> x13, Pallas kernels: none -> 878 us  [the longest x2 414 us: scatter(): pl.pallas_call(functools.partial(scatter_kernel, n_dp, n_t, count, group)...]
    all_gather x9 -> x0, waiting for transfers between devices: 521 us -> none  [the longest x1 117 us: local(): lax.all_gather(normed_two.astype(bf16), 'tensor', axis=0, tiled=True)]
    dot_general x49 -> x0, matrix products: 357 us -> none  [the longest x4 45.2 us: backward_block(): jnp.einsum('qgre,kge->grqk', d_part, value_reduced, preferred_element_typ...]
    dynamic_update_slice x8 -> x0, local copies, waits for them, and re-layouts: 67.4 us -> none  [local(): att_blocks, log_totals = lax.map(forward_block, (query_block_list, starts))]
    convert_element_type x17 -> x8, other arithmetic: 70.3 us -> 10.3 us  [the longest x1 2.95 us: local(): tokens_grad = (d_h + d_x).astype(bf16)]
    unnamed x2 -> x0, blocking collectives: 39.5 us -> none
    unnamed x73 -> x149, local copies, waits for them, and re-layouts: 16.9 us -> 44.4 us
  transfers between devices with their start and end apart: 20 -> 5, of which waited for: 19 -> 1; matrix products, arithmetic and copies ran while one was open for 10% -> 3% of each run, Pallas kernels for 0% -> 7%
where the time goes in v1:
time: 1030 us; the launch traced here: 1020 us
  Pallas kernels  878 us (85%)
  local copies, waits for them, and re-layouts  96.8 us (9%)
  other arithmetic  32.6 us (3%)
    pallas_call x2, Pallas kernels, scatter(): pl.pallas_call(functools.partial(scatter_kernel, n_dp, n_t, count, group)...  414 us
    pallas_call x2, Pallas kernels, gather(): pl.pallas_call(functools.partial(gather_kernel, n_dp, n_t, count, own is...  310 us
    pallas_call x4, Pallas kernels, mlp(): pl.pallas_call(functools.partial(mlp_kernel, tile, first), grid_spec=pltp...  93.1 us
    unnamed x149, local copies, waits for them, and re-layouts  44.4 us
  transfers between devices with their start and end apart: 5, of which 1 were waited for; matrix products, arithmetic and copies ran while one was open for 3% of the time, Pallas kernels for 7%

profile of v1, /device:TPU:0, one launch (start us, length us, event | category | flops | bytes accessed | tf_op | source)
XLA Modules:
  0.0 1020.2 jit_solution(9081589802878143804)
XLA Ops:
  11.9 76.9 %gather_weights.2 = bf16[4,8,192,896]{3,2,1,0:T(8,128)(2,1)} custom-call(bf16[192,896]{1,0:T(8,128)(2,1)} %fusion.12.refs_0_), custom_call_target="tpu_custom_call" | custom-call | tf_op jit(solution)/shard_map/gather_weights/pallas_call | solution.py:685
  94.5 10.1 qkv_project.1
  106.4 232.9 %gather_weights.3 = (bf16[4,8,192,384]{3,2,1,0:T(8,128)(2,1)}, bf16[4,8,192,768]{3,2,1,0:T(8,128)(2,1)}, bf16[4,8,192,768]{3,2,1,0:T(8,128)(2,1)}, bf16[4,8,192,...) custom-call(bf16[192,384]{1,0:T(8,128)(2,1)} %bitcast.140, ...), custom_call_target="tpu_custom_call" | custom-call | tf_op jit(solution)/shard_map/gather_weights/pallas_call | solution.py:685
  339.3 15.2 %attend.1 = (bf16[1536,512]{1,0:T(8,128)(2,1)}, f32[8,1,1024]{2,1,0:T(1,128)}) custom-call(s32[2]{0:T(128)} %get-tuple-element.180.sc_ref.refs_10_, bf16[1536,512]{1,0:T(8,128)(2,1)} %bitcast.136, bf16[2,768,512]{2,1,0:T(8,128)(2,1)} %get-tuple-element.55.refs_5_.refs_0_.refs_1_.refs_15_, ...), custom_call_target="tpu_custom_call" | custom-call | flops 6442450944 | bytes 9437184 | tf_op jit(solution)/shard_map/attend/pallas_call | solution.py:283
  354.5 8.3 out_project.1
  367.4 3.7 copy.83
  371.1 2.8 fusion.9
  406.7 22.2 %mlp.4 = (f32[512,1536]{1,0:T(8,128)}, f32[512,1536]{1,0:T(8,128)}, bf16[4,768,768]{2,1,0:T(8,128)(2,1)}, bf16[4,768,768]{2,1,0:T(8,128)(2,1)}) custom-call(s32[2]{0:T(128)} %get-tuple-element.181.me_ref, bf16[512,1536]{1,0:T(8,128)(2,1)} %copy.90.n2_ref, bf16[1536,512]{1,0:T(8,128)(2,1)} %bitcast_dynamic-update-slice_fusion.24.n2t_ref, ...), custom_call_target="tpu_custom_call" | custom-call | flops 14495514624 | bytes 37748736 | tf_op jit(solution)/shard_map/mlp/pallas_call | solution.py:370
  428.9 23.6 %mlp.5 = (f32[512,1536]{1,0:T(8,128)}, f32[512,1536]{1,0:T(8,128)}, bf16[4,768,768]{2,1,0:T(8,128)(2,1)}, bf16[4,768,768]{2,1,0:T(8,128)(2,1)}) custom-call(s32[2]{0:T(128)} %get-tuple-element.181.me_ref, bf16[512,1536]{1,0:T(8,128)(2,1)} %copy.90.n2_ref, ...), custom_call_target="tpu_custom_call", output_to_operand_aliasing={{0}: (6, {}), {1}: (7, {})} | custom-call | flops 14495514624 | bytes 37748736 | tf_op jit(solution)/shard_map/mlp/pallas_call | solution.py:370
  452.5 23.6 %mlp.6 = (f32[512,1536]{1,0:T(8,128)}, f32[512,1536]{1,0:T(8,128)}, bf16[4,768,768]{2,1,0:T(8,128)(2,1)}, bf16[4,768,768]{2,1,0:T(8,128)(2,1)}) custom-call(s32[2]{0:T(128)} %get-tuple-element.181.me_ref, bf16[512,1536]{1,0:T(8,128)(2,1)} %copy.90.n2_ref, ...), custom_call_target="tpu_custom_call", output_to_operand_aliasing={{0}: (6, {}), {1}: (7, {})} | custom-call | flops 14495514624 | bytes 37748736 | tf_op jit(solution)/shard_map/mlp/pallas_call | solution.py:370
  476.0 23.7 %mlp.7 = (f32[512,1536]{1,0:T(8,128)}, f32[512,1536]{1,0:T(8,128)}, bf16[4,768,768]{2,1,0:T(8,128)(2,1)}, bf16[4,768,768]{2,1,0:T(8,128)(2,1)}) custom-call(s32[2]{0:T(128)} %get-tuple-element.181.me_ref, bf16[512,1536]{1,0:T(8,128)(2,1)} %copy.90.n2_ref, ...), custom_call_target="tpu_custom_call", output_to_operand_aliasing={{0}: (6, {}), {1}: (7, {})} | custom-call | flops 14495514624 | bytes 37748736 | tf_op jit(solution)/shard_map/mlp/pallas_call | solution.py:370
  499.7 3.5 copy.94
  503.3 2.9 multiply_reduce_fusion
  521.8 11.4 %out_back.1 = (bf16[4,384,512]{2,1,0:T(8,128)(2,1)}, bf16[4,768,384]{2,1,0:T(8,128)(2,1)}, bf16[4,768,384]{2,1,0:T(8,128)(2,1)}) custom-call(s32[2]{0:T(128)} %get-tuple-element.181.me_ref, bf16[512,1536]{1,0:T(8,128)(2,1)} %copy.97.dh_ref, bf16[1536,512]{1,0:T(8,128)(2,1)} %bitcast_dynamic-update-slice_fusion.8.dht_ref, bf16[4,384,512]{2,1,0:T(8,128)(2,1)} %bitcast.122, ...), custom_call_target="tpu_custom_call" | custom-call | flops 4831838208 | bytes 15728640 | tf_op jit(solution)/shard_map/out_back/pallas_call | solution.py:127
  536.2 337.7 %scatter_grads.2 = (bf16[4,2,2,192,768]{4,3,2,1,0:T(8,128)(2,1)}, bf16[4,2,2,192,768]{4,3,2,1,0:T(8,128)(2,1)}, bf16[4,2,2,192,768]{4,3,2,1,0:T(8,128)(2,1)}, bf...) custom-call(bf16[4,2,2,192,768]{4,3,2,1,0:T(8,128)(2,1)} %bitcast.12, ...), custom_call_target="tpu_custom_call" | custom-call | tf_op jit(solution)/shard_map/scatter_grads/pallas_call | solution.py:1057
  873.9 15.7 %qkv_back.1 = (f32[512,1536]{1,0:T(8,128)}, bf16[4,768,768]{2,1,0:T(8,128)(2,1)}, bf16[4,768,768]{2,1,0:T(8,128)(2,1)}) custom-call(s32[2]{0:T(128)} %get-tuple-element.181.me_ref, f32[4,384,512]{2,1,0:T(8,128)} %bitcast.147, bf16[2,768,512]{2,1,0:T(8,128)(2,1)} %get-tuple-element.86.dkv_ref, f32[48,512]{1,0:T(8,128)} %get-tuple-element.177.cos_ref, ...), custom_call_target="tpu_custom_call" | custom-call | flops 9663676416 | bytes 28311552 | tf_op jit(solution)/shard_map/qkv_back/pallas_call | solution.py:182
  889.7 3.6 copy.98
  893.3 3.0 fusion.8
  897.6 3.6 copy.93
  904.8 5.2 fusion.29
  910.0 5.4 fusion.28
  916.9 2.9 fusion.6
  920.7 76.4 %scatter_grads.3 = (bf16[4,2,2,192,384]{4,3,2,1,0:T(8,128)(2,1)}, bf16[4,2,2,192,384]{4,3,2,1,0:T(8,128)(2,1)}, f32[192,384]{1,0:T(8,128)}, f32[192,384]{1,0:T(8,128)}) custom-call(bf16[4,2,2,192,384]{4,3,2,1,0:T(8,128)(2,1)} %bitcast.118, bf16[4,2,2,192,384]{4,3,2,1,0:T(8,128)(2,1)} %bitcast.117, bf16[4,2,2,192,384]{4,3,2,1,0:T(8,128)(2,1)} %bitcast.120, ...), custom_call_target="tpu_custom_call" | custom-call | tf_op jit(solution)/shard_map/scatter_grads/pallas_call | solution.py:1057
  1010.5 3.3 collective-permute-start.4
  (216 shorter events, 100.2 us)
Async XLA Ops:
  9.6 81.0 %copy-start.4 = (bf16[512,1536]{0,1:T(8,128)(2,1)}, bf16[512,1536]{0,1:T(8,128)(2,1)S(1)}, u32[]{:S(2)}) copy-start(bf16[512,1536]{0,1:T(8,128)(2,1)S(1)} %copy.79) | copy-start | bytes 4718596
  10.0 78.8 %copy-start.48 = (f32[512]{0:T(512)}, f32[512]{0:T(512)S(1)}, u32[]{:S(2)}) copy-start(f32[512]{0:T(512)S(1)} %fusion) | copy-start | bytes 6148
  94.5 11.1 %copy-start.26 = (bf16[192,256]{1,0:T(8,128)(2,1)S(1)}, bf16[192,256]{1,0:T(8,128)(2,1)}, u32[]{:S(2)}) copy-start(bf16[192,256]{1,0:T(8,128)(2,1)} %get-tuple-element.164) | copy-start | bytes 294916
  94.5 11.1 %copy-start.27 = (bf16[192,256]{1,0:T(8,128)(2,1)S(1)}, bf16[192,256]{1,0:T(8,128)(2,1)}, u32[]{:S(2)}) copy-start(bf16[192,256]{1,0:T(8,128)(2,1)} %get-tuple-element.165) | copy-start | bytes 294916
  367.4 138.8 %copy-start = (f32[512,1536]{0,1:T(8,128)}, f32[512,1536]{0,1:T(8,128)S(1)}, u32[]{:S(2)}) copy-start(f32[512,1536]{0,1:T(8,128)S(1)} %copy.92) | copy-start | bytes 9437188
  367.4 138.8 %copy-start.46 = (f32[512]{0:T(512)}, f32[512]{0:T(512)S(1)}, u32[]{:S(2)}) copy-start(f32[512]{0:T(512)S(1)} %fusion.26) | copy-start | bytes 6148
  378.3 127.8 %copy-start.41 = (f32[512]{0:T(512)}, f32[512]{0:T(512)S(1)}, u32[]{:S(2)}) copy-start(f32[512]{0:T(512)S(1)} %add_rsqrt_fusion) | copy-start | bytes 6148
  521.8 11.4 %copy-start.15 = (bf16[1536,512]{1,0:T(8,128)(2,1)S(1)}, bf16[1536,512]{1,0:T(8,128)(2,1)}, u32[]{:S(2)}) copy-start(bf16[1536,512]{1,0:T(8,128)(2,1)} %get-tuple-element.59) | copy-start | bytes 4718596
  897.6 99.5 %collective-permute-start = (f32[4,2,192]{2,1,0:T(2,128)}, f32[4,2,192]{2,1,0:T(2,128)}, u32[]{:S(2)}, u32[]{:S(2)}) collective-permute-start(f32[4,2,192]{2,1,0:T(2,128)} %pad_maximum_fusion.7), channel_id=1, source_target_pairs={{0,4},{4,0},{8,12},{12,8},{16,20},{20,16},{24,28},{28,24},{1,5},{5... | collective-permute-start | bytes 18440 | tf_op jit(solution)/shard_map/ppermute | solution.py:418
  904.8 10.6 %copy-start.45 = (f32[512]{0:T(512)S(1)}, f32[512]{0:T(512)}, u32[]{:S(2)}) copy-start(f32[512]{0:T(512)} %add_rsqrt_fusion.1) | copy-start | bytes 6148
  904.8 10.6 %copy-start.47 = (f32[512]{0:T(512)S(1)}, f32[512]{0:T(512)}, u32[]{:S(2)}) copy-start(f32[512]{0:T(512)} %copy-done.46) | copy-start | bytes 6148
  904.8 10.6 %copy-start.51 = (f32[512]{0:T(512)S(1)}, f32[512]{0:T(512)}, u32[]{:S(2)}) copy-start(f32[512]{0:T(512)} %copy-done.50) | copy-start | bytes 6148
  920.7 76.4 %copy-start.53 = (f32[1,2,192]{2,1,0:T(2,128)S(1)}, f32[1,2,192]{2,1,0:T(2,128)}, u32[]{:S(2)}) copy-start(f32[1,2,192]{2,1,0:T(2,128)} %get-tuple-element.168) | copy-start | bytes 4612
  920.7 76.5 %copy-start.54 = (f32[1,2,192]{2,1,0:T(2,128)S(1)}, f32[1,2,192]{2,1,0:T(2,128)}, u32[]{:S(2)}) copy-start(f32[1,2,192]{2,1,0:T(2,128)} %get-tuple-element.169) | copy-start | bytes 4612
  920.7 76.5 %copy-start.55 = (f32[1,2,192]{2,1,0:T(2,128)S(1)}, f32[1,2,192]{2,1,0:T(2,128)}, u32[]{:S(2)}) copy-start(f32[1,2,192]{2,1,0:T(2,128)} %get-tuple-element.170) | copy-start | bytes 4612
  920.7 76.5 %copy-start.56 = (f32[1,2,192]{2,1,0:T(2,128)S(1)}, f32[1,2,192]{2,1,0:T(2,128)}, u32[]{:S(2)}) copy-start(f32[1,2,192]{2,1,0:T(2,128)} %get-tuple-element.171) | copy-start | bytes 4612
  997.1 11.8 %copy-start.18 = (f32[192,256]{1,0:T(8,128)S(1)}, f32[192,256]{1,0:T(8,128)}, u32[]{:S(2)}) copy-start(f32[192,256]{1,0:T(8,128)} %get-tuple-element.143) | copy-start | bytes 589828
  997.1 11.8 %copy-start.19 = (f32[192,256]{1,0:T(8,128)S(1)}, f32[192,256]{1,0:T(8,128)}, u32[]{:S(2)}) copy-start(f32[192,256]{1,0:T(8,128)} %get-tuple-element.146) | copy-start | bytes 589828
  997.1 11.8 %copy-start.20 = (f32[192,256]{1,0:T(8,128)S(1)}, f32[192,256]{1,0:T(8,128)}, u32[]{:S(2)}) copy-start(f32[192,256]{1,0:T(8,128)} %get-tuple-element.149) | copy-start | bytes 589828
  997.1 11.8 %copy-start.22 = (f32[192,256]{1,0:T(8,128)S(1)}, f32[192,256]{1,0:T(8,128)}, u32[]{:S(2)}) copy-start(f32[192,256]{1,0:T(8,128)} %get-tuple-element.152) | copy-start | bytes 589828
  998.0 4.4 collective-permute-start.1
  1002.4 3.9 collective-permute-start.2
  1006.3 4.1 collective-permute-start.3
  1010.5 7.5 collective-permute-start.4
  (39 other events, 204.3 us)

commit v2 on v1

--- a/solution.py
+++ b/solution.py
@@ -12,6 +12,8 @@
 HALF = HEAD_SIZE // 2
 GAIN_LANES = 128
 CHUNKS = 4
+CLIMB_AT = 8
+CLIMB_STEP = 5
 KEY_TILE = 256
 NEG = -1e30
 
@@ -35,6 +37,14 @@
 
 def cost(flops, nbytes, trans=0):
     return pl.CostEstimate(flops=int(flops), bytes_accessed=int(nbytes), transcendentals=int(trans))
+
+
+def place(ref, me_ref, grad, col=0):
+    count, block = ref.shape[1], ref.shape[2]
+    for d in range(count):
+        r = me_ref[1] ^ d
+        at = (r & 1) * (count // 2) + (r >> 1)
+        ref[0, at, :, col : col + grad.shape[1]] = grad[d * block : (d + 1) * block]
 
 
 def turn(y, cosine, sine, sign):
@@ -111,19 +121,16 @@
     )(att, w, x)
 
 
-def out_back_kernel(me_ref, dh_ref, dht_ref, att_ref, w_ref, da_ref, keep_ref, send_ref):
+def out_back_kernel(me_ref, dh_ref, dht_ref, att_ref, w_ref, da_ref, grad_ref):
     w = w_ref[0]
     da_ref[0] = dot(dh_ref[...], w).T.astype(bf16)
-    grad = dot(dht_ref[...], att_ref[0].T).astype(bf16)
-    half = grad.shape[0] // 2
-    keep_ref[0] = grad[:half]
-    send_ref[0] = grad[half:]
-
-
-def out_back(me, dh, dht, att, w, no, col):
+    place(grad_ref, me_ref, dot(dht_ref[...], att_ref[0].T).astype(bf16))
+
+
+def out_back(me, dh, dht, att, w, no, col, n_dp):
     zs, _, rows = att.shape
     width = dh.shape[1]
-    half = width // 2
+    block = width // n_dp
     return pl.pallas_call(
         out_back_kernel,
         grid_spec=pltpu.PrefetchScalarGridSpec(
@@ -137,14 +144,12 @@
             ],
             out_specs=[
                 pl.BlockSpec((1, no, rows), lambda z, m: (z, 0, 0)),
-                pl.BlockSpec((1, half, no), lambda z, m: (z ^ m[0], 0, 0)),
-                pl.BlockSpec((1, half, no), lambda z, m: (z ^ m[0], 0, 0)),
+                pl.BlockSpec((1, n_dp, block, no), lambda z, m: (z ^ m[0], 0, 0, 0)),
             ],
         ),
         out_shape=[
             jax.ShapeDtypeStruct((zs, no, rows), bf16),
-            jax.ShapeDtypeStruct((zs, half, no), bf16),
-            jax.ShapeDtypeStruct((zs, half, no), bf16),
+            jax.ShapeDtypeStruct((zs, n_dp, block, no), bf16),
         ],
         compiler_params=params("arbitrary"),
         cost_estimate=cost(4 * rows * width * no * zs, 4 * zs * width * no + 8 * rows * width),
@@ -153,7 +158,7 @@
 
 
 def qkv_back_kernel(
-    nq, nk, me_ref, dq_ref, dkv_ref, cos_ref, sin_ref, n1t_ref, w_ref, dn_ref, keep_ref, send_ref
+    nq, nk, me_ref, dq_ref, dkv_ref, cos_ref, sin_ref, n1t_ref, w_ref, dn_ref, dwq_ref, dwkv_ref
 ):
     z = pl.program_id(0)
 
@@ -168,15 +173,14 @@
     w = w_ref[0, :, : nq + 2 * nk]
     dn_ref[...] += dot(d, w, ((1,), (1,)))
     grad = dot(n1t_ref[...], d).astype(bf16)
-    half = grad.shape[0] // 2
-    keep_ref[0] = grad[:half]
-    send_ref[0] = grad[half:]
-
-
-def qkv_back(me, dq, dkv, cosine, sine, n1t, w, nq, nk):
+    place(dwq_ref, me_ref, grad[:, :nq])
+    place(dwkv_ref, me_ref, grad[:, nq:])
+
+
+def qkv_back(me, dq, dkv, cosine, sine, n1t, w, nq, nk, n_dp):
     zs, _, rows = dq.shape
     width = n1t.shape[0]
-    half = width // 2
+    block = width // n_dp
     cols = w.shape[2]
     out = nq + 2 * nk
     return pl.pallas_call(
@@ -194,26 +198,19 @@
             ],
             out_specs=[
                 pl.BlockSpec((rows, width), lambda z, m: (0, 0)),
-                pl.BlockSpec((1, half, out), lambda z, m: (z ^ m[0], 0, 0)),
-                pl.BlockSpec((1, half, out), lambda z, m: (z ^ m[0], 0, 0)),
+                pl.BlockSpec((1, n_dp, block, nq), lambda z, m: (z ^ m[0], 0, 0, 0)),
+                pl.BlockSpec((1, n_dp, block, 2 * nk), lambda z, m: (z ^ m[0], 0, 0, 0)),
             ],
         ),
         out_shape=[
             jax.ShapeDtypeStruct((rows, width), f32),
-            jax.ShapeDtypeStruct((zs, half, out), bf16),
-            jax.ShapeDtypeStruct((zs, half, out), bf16),
+            jax.ShapeDtypeStruct((zs, n_dp, block, nq), bf16),
+            jax.ShapeDtypeStruct((zs, n_dp, block, 2 * nk), bf16),
         ],
         compiler_params=params("arbitrary"),
         cost_estimate=cost(4 * rows * width * out * zs, 4 * zs * width * cols + 8 * rows * width),
         name="qkv_back",
     )(me, dq, dkv, cosine, sine, n1t, w)
-
-
-def side_by_side(ref):
-    group = ref.shape[0] // HEAD_SIZE
-    return jnp.concatenate(
-        [ref[a * HEAD_SIZE : (a + 1) * HEAD_SIZE] for a in range(group)], axis=1
-    )
 
 
 def key_mask(s, key_first, query_first, length, rows, diagonal):
@@ -226,93 +223,13 @@
     return jnp.broadcast_to(ok, s.shape)
 
 
-def attend_kernel(blocks, group, sc_ref, q_ref, *refs):
-    kv_refs = refs[: 2 * blocks]
-    o_ref, lse_ref, m_ref, l_ref, acc_ref = refs[2 * blocks :]
-    z, length = sc_ref[0], sc_ref[1]
-    rows = q_ref.shape[1]
-    first = z * rows
-    m_ref[...] = jnp.full_like(m_ref, NEG)
-    l_ref[...] = jnp.zeros_like(l_ref)
-    acc_ref[...] = jnp.zeros_like(acc_ref)
-
-    for r in range(blocks):
-        k_ref, v_ref = kv_refs[2 * r], kv_refs[2 * r + 1]
-
-        @pl.when((z >= r) & (first - r * rows < length))
-        def _():
-            q = side_by_side(q_ref)
-            for j in range(rows // KEY_TILE):
-                part = slice(j * KEY_TILE, (j + 1) * KEY_TILE)
-                k, v = k_ref[0, :, part], v_ref[0, :, part]
-                s = dot(k, q, ((0,), (0,)))
-                ok = key_mask(s, first - r * rows + j * KEY_TILE, first, length, rows, r == 0)
-                s = jnp.where(ok, s, NEG)
-                old = m_ref[...]
-                new = jnp.maximum(old, jnp.max(s, axis=0, keepdims=True))
-                shrink = jnp.exp2((old - new) * SCALE2)
-                p = jnp.exp2(s * SCALE2 - new * SCALE2)
-                l_ref[...] = l_ref[...] * shrink + jnp.sum(p, axis=0, keepdims=True)
-                acc_ref[...] = acc_ref[...] * shrink + dot(v, p.astype(bf16))
-                m_ref[...] = new
-
-    total = l_ref[...]
-    total = jnp.where(total > 0.0, total, 1.0)
-    out = acc_ref[...] / total
-    log_total = m_ref[...] * SCALE2 + jnp.log2(total)
-    for a in range(group):
-        lanes = slice(a * rows, (a + 1) * rows)
-        o_ref[a * HEAD_SIZE : (a + 1) * HEAD_SIZE] = out[:, lanes].astype(bf16)
-    lse_ref[0] = log_total
-
-
-def attend(sc, q, kvs):
-    heads_rows, rows = q.shape
-    blocks = len(kvs)
-    groups = kvs[0].shape[1] // HEAD_SIZE
-    per = heads_rows // groups
-    group = per // HEAD_SIZE
-    kv_specs, kv_args = [], []
-    for kv in kvs:
-        for which in (0, 1):
-            kv_specs.append(
-                pl.BlockSpec((1, HEAD_SIZE, rows), lambda g, s, which=which: (which, g, 0))
-            )
-            kv_args.append(kv)
-    work = heads_rows // HEAD_SIZE * rows * rows * blocks
-    return pl.pallas_call(
-        functools.partial(attend_kernel, blocks, group),
-        grid_spec=pltpu.PrefetchScalarGridSpec(
-            num_scalar_prefetch=1,
-            grid=(groups,),
-            in_specs=[pl.BlockSpec((per, rows), lambda g, s: (g, 0))] + kv_specs,
-            out_specs=[
-                pl.BlockSpec((per, rows), lambda g, s: (g, 0)),
-                pl.BlockSpec((1, 1, group * rows), lambda g, s: (g, 0, 0)),
-            ],
-            scratch_shapes=[
-                pltpu.VMEM((1, group * rows), f32),
-                pltpu.VMEM((1, group * rows), f32),
-                pltpu.VMEM((HEAD_SIZE, group * rows), f32),
-            ],
-        ),
-        out_shape=[
-            jax.ShapeDtypeStruct((heads_rows, rows), bf16),
-            jax.ShapeDtypeStruct((groups, 1, group * rows), f32),
-        ],
-        compiler_params=params("arbitrary"),
-        cost_estimate=cost(4 * work * HEAD_SIZE, 2 * (blocks + 2) * heads_rows * rows, work),
-        name="attend",
-    )(sc, q, *kv_args)
-
-
 def mlp_kernel(
     tile, first, me_ref, n2_ref, n2t_ref, g_ref, gt_ref, w_ref, *refs
 ):
     if first:
-        out_ref, dn_ref, keep_ref, send_ref = refs
+        out_ref, dn_ref, grad_ref = refs
     else:
-        out_in, dn_in, out_ref, dn_ref, keep_ref, send_ref = refs
+        out_in, dn_in, out_ref, dn_ref, grad_ref = refs
     z = pl.program_id(0)
 
     @pl.when(z == 0)
@@ -338,21 +255,18 @@
     d_up = (d_hidden * active).astype(bf16)
     out_ref[...] += dot(hidden, wd, ((1,), (1,)))
     dn_ref[...] += dot(d_gate, wg, ((1,), (1,))) + dot(d_up, wu, ((1,), (1,)))
-    half = n2t_ref.shape[0] // 2
-    for ref, rows in ((keep_ref, slice(0, half)), (send_ref, slice(half, 2 * half))):
-        n2t, gt = n2t_ref[rows], gt_ref[rows]
-        ref[0, :, :tile] = dot(n2t, d_gate).astype(bf16)
-        ref[0, :, tile : 2 * tile] = dot(n2t, d_up).astype(bf16)
-        ref[0, :, 2 * tile :] = dot(gt, hidden).astype(bf16)
-
-
-def mlp(me, n2, n2t, g, gt, w, chunk, tile, carry):
+    place(grad_ref, me_ref, dot(n2t_ref[...], d_gate).astype(bf16), 0)
+    place(grad_ref, me_ref, dot(n2t_ref[...], d_up).astype(bf16), tile)
+    place(grad_ref, me_ref, dot(gt_ref[...], hidden).astype(bf16), 2 * tile)
+
+
+def mlp(me, n2, n2t, g, gt, w, chunk, tile, carry, n_dp):
     rows, width = n2.shape
     zs = w.shape[0]
-    half = width // 2
+    block = width // n_dp
     full = pl.BlockSpec((rows, width), lambda z, m: (0, 0))
     full_t = pl.BlockSpec((width, rows), lambda z, m: (0, 0))
-    grad_spec = pl.BlockSpec((1, half, 3 * tile), lambda z, m: (z ^ m[0], 0, 0))
+    grad_spec = pl.BlockSpec((1, n_dp, block, 3 * tile), lambda z, m: (z ^ m[0], 0, 0, 0))
     first = carry is None
     in_specs = [
         full,
@@ -373,13 +287,12 @@
             num_scalar_prefetch=1,
             grid=(zs,),
             in_specs=in_specs,
-            out_specs=[full, full, grad_spec, grad_spec],
+            out_specs=[full, full, grad_spec],
         ),
         out_shape=[
             jax.ShapeDtypeStruct((rows, width), f32),
             jax.ShapeDtypeStruct((rows, width), f32),
-            jax.ShapeDtypeStruct((zs, half, 3 * tile), bf16),
-            jax.ShapeDtypeStruct((zs, half, 3 * tile), bf16),
+            jax.ShapeDtypeStruct((zs, n_dp, block, 3 * tile), bf16),
         ],
         input_output_aliases=aliases,
         compiler_params=params("arbitrary"),
@@ -620,26 +533,107 @@
             self.hop(r).wait_send()
 
 
+def attend_part(r, z, length, q_ref, kv_ref, m_ref, l_ref, acc_ref):
+    rows = q_ref.shape[1]
+    groups = m_ref.shape[0]
+    group = q_ref.shape[0] // (groups * HEAD_SIZE)
+    first = z * rows
+
+    @pl.when(z >= r)
+    def _():
+        def body(g, _):
+            base = pl.multiple_of(g * (group * HEAD_SIZE), 32)
+            at = pl.multiple_of(g * HEAD_SIZE, 32)
+            q = jnp.concatenate(
+                [q_ref[pl.ds(base + a * HEAD_SIZE, HEAD_SIZE), :] for a in range(group)], axis=1
+            )
+            if r == 0:
+                m = jnp.full((1, group * rows), NEG, f32)
+                total = jnp.zeros((1, group * rows), f32)
+                acc = jnp.zeros((HEAD_SIZE, group * rows), f32)
+            else:
+                m, total, acc = m_ref[g], l_ref[g], acc_ref[g]
+            for j in range(rows // KEY_TILE):
+                part = slice(j * KEY_TILE, (j + 1) * KEY_TILE)
+                k = kv_ref[0, pl.ds(at, HEAD_SIZE), part]
+                v = kv_ref[1, pl.ds(at, HEAD_SIZE), part]
+                s = dot(k, q, ((0,), (0,)))
+                ok = key_mask(s, first - r * rows + j * KEY_TILE, first, length, rows, r == 0)
+                s = jnp.where(ok, s, NEG)
+                new = jnp.maximum(m, jnp.max(s, axis=0, keepdims=True))
+                shrink = jnp.exp2((m - new) * SCALE2)
+                p = jnp.exp2(s * SCALE2 - new * SCALE2)
+                total = total * shrink + jnp.sum(p, axis=0, keepdims=True)
+                acc = acc * shrink + dot(v, p.astype(bf16))
+                m = new
+            m_ref[g], l_ref[g], acc_ref[g] = m, total, acc
+            return 0
+
+        lax.fori_loop(0, groups, body, 0)
+
+
+def attend_end(q_shape, m_ref, l_ref, acc_ref, att_ref):
+    groups = m_ref.shape[0]
+    rows = q_shape[1]
+    group = q_shape[0] // (groups * HEAD_SIZE)
+
+    def body(g, _):
+        out = acc_ref[g] / l_ref[g]
+        for a in range(group):
+            own = pl.ds(pl.multiple_of((g * group + a) * HEAD_SIZE, 32), HEAD_SIZE)
+            att_ref[own, :] = out[:, a * rows : (a + 1) * rows].astype(bf16)
+        m_ref[g] = m_ref[g] * SCALE2 + jnp.log2(l_ref[g])
+        return 0
+
+    lax.fori_loop(0, groups, body, 0)
+
+
 def gather_kernel(n_dp, n_t, count, climbs, *refs):
-    shards, refs = refs[:count], refs[count:]
+    refs = list(refs)
+
+    def take(k):
+        out = refs[:k]
+        del refs[:k]
+        return out
+
+    shards = take(count)
     if climbs:
-        own, refs = refs[0], refs[1:]
-    wholes, refs = refs[:count], refs[count:]
+        own, q_ref, length_ref = take(3)
+    wholes = take(count)
     if climbs:
-        kept, refs = refs[: n_t - 1], refs[n_t - 1 :]
-    sems, refs = refs[:5], refs[5:]
+        kept = take(n_t - 1)
+        att_ref, lse_ref = take(2)
+    sems = take(5)
     me, z = lax.axis_index("dp"), lax.axis_index("tensor")
     neighbours(n_dp, n_t, me, z)
     works = [
         Gather(n_dp, n_t, me, z, c, shards[c], wholes[c], sems) for c in range(count)
     ]
-    climb = Climb(n_t, me, z, own, kept, refs) if climbs else None
+    if climbs:
+        climb_sems = take(2)
+        l_ref, acc_ref, kv_ref, kv_sem = take(4)
+        climb = Climb(n_t, me, z, own, kept, climb_sems)
+        climb.start(0)
+        length = length_ref[0]
+
+    def attend_step(r):
+        if r > 0:
+            climb.arrive(r)
+            if r < n_t - 1:
+                climb.start(r)
+
+        @pl.when(z >= r)
+        def _():
+            fetch = pltpu.make_async_copy(own if r == 0 else kept[r - 1], kv_ref, kv_sem)
+            fetch.start()
+            fetch.wait()
+
+        attend_part(r, z, length, q_ref, kv_ref, lse_ref, l_ref, acc_ref)
+
     stages = log2(n_dp)
     works[0].send_own()
-    if climbs:
-        climb.start(0)
     total = count * n_t
-    passed = 0
+    todo = list(range(n_t)) if climbs else []
     for n in range(total + 2 * (stages - 1)):
         if n < total:
             c, k = divmod(n, n_t)
@@ -647,15 +641,16 @@
             works[c].spread(k, 0)
             if k == 0 and c + 1 < count:
                 works[c + 1].send_own()
-            if climbs and n in (5, 9, 13)[: n_t - 1]:
-                passed += 1
-                climb.arrive(passed)
-                if passed < n_t - 1:
-                    climb.start(passed)
         for stage in range(1, stages):
             at = n - 2 * stage
             if 0 <= at < total:
                 works[at // n_t].spread(at % n_t, stage)
+        if todo and (n == 2 if todo[0] == 0 else n == CLIMB_AT + CLIMB_STEP * (todo[0] - 1)):
+            attend_step(todo.pop(0))
+    for r in todo:
+        attend_step(r)
+    if climbs:
+        attend_end(q_ref.shape, lse_ref, l_ref, acc_ref, att_ref)
     for c in range(count):
         for k in range(n_t):
             works[c].finish(k)
@@ -664,12 +659,16 @@
             climb.finish(r)
 
 
-def gather(shards, n_dp, n_t, collective_id, own=None):
+def gather(shards, n_dp, n_t, collective_id, attention=None):
     count = len(shards)
     shapes = [
         jax.ShapeDtypeStruct((n_t, n_dp) + s.shape, s.dtype) for s in shards
     ]
     args = list(shards)
+    anywhere = pl.BlockSpec(memory_space=pl.ANY)
+    vmem = pl.BlockSpec(memory_space=pltpu.VMEM)
+    in_specs = [anywhere] * count
+    out_specs = [anywhere] * count
     scratch = [
         pltpu.SemaphoreType.DMA((count,)),
         pltpu.SemaphoreType.DMA((count, 2, n_t)),
@@ -677,18 +676,35 @@
         pltpu.SemaphoreType.DMA((count, n_t, n_dp - 1)),
         pltpu.SemaphoreType.DMA((count, n_t, n_dp - 1)),
     ]
-    if own is not None:
-        args.append(own)
-        shapes += [jax.ShapeDtypeStruct(own.shape, own.dtype)] * (n_t - 1)
+    if attention is not None:
+        kv, q, length = attention
+        rows = q.shape[1]
+        groups = kv.shape[1] // HEAD_SIZE
+        lanes = q.shape[0] // (groups * HEAD_SIZE) * rows
+        args += [kv, q, length.reshape(1)]
+        in_specs += [anywhere, vmem, pl.BlockSpec(memory_space=pltpu.SMEM)]
+        shapes += [jax.ShapeDtypeStruct(kv.shape, kv.dtype)] * (n_t - 1)
+        shapes += [
+            jax.ShapeDtypeStruct(q.shape, bf16),
+            jax.ShapeDtypeStruct((groups, 1, lanes), f32),
+        ]
+        out_specs += [anywhere] * (n_t - 1) + [vmem, vmem]
         scratch += [pltpu.SemaphoreType.DMA((n_t,))] * 2
-    anywhere = pl.BlockSpec(memory_space=pl.ANY)
+        scratch += [
+            pltpu.VMEM((groups, 1, lanes), f32),
+            pltpu.VMEM((groups, HEAD_SIZE, lanes), f32),
+            pltpu.VMEM(kv.shape, bf16),
+            pltpu.SemaphoreType.DMA,
+        ]
     return pl.pallas_call(
-        functools.partial(gather_kernel, n_dp, n_t, count, own is not None),
-        in_specs=[anywhere] * len(args),
-        out_specs=[anywhere] * len(shapes),
+        functools.partial(gather_kernel, n_dp, n_t, count, attention is not None),
+        in_specs=in_specs,
+        out_specs=out_specs,
         out_shape=shapes,
         scratch_shapes=scratch,
-        compiler_params=pltpu.CompilerParams(collective_id=collective_id, has_side_effects=True),
+        compiler_params=pltpu.CompilerParams(
+            collective_id=collective_id, has_side_effects=True, vmem_limit_bytes=VMEM_LIMIT
+        ),
         name="gather_weights",
     )(*args)
 
@@ -723,9 +739,10 @@
 
 
 class Scatter:
-    def __init__(self, n_dp, n_t, me, z, index, keep, send, land, out, held, tile, landings, sems):
+    def __init__(self, n_dp, n_t, me, z, index, grad, land, out, held, tile, landings, sems):
         self.n_t, self.me, self.z, self.index = n_t, me, z, index
-        self.keep, self.send, self.land, self.out, self.held = keep, send, land, out, held
+        self.keep, self.send = grad.at[:, 0], grad.at[:, 1]
+        self.land, self.out, self.held = land, out, held
         self.tile, self.landings, self.sems = tile, landings, sems
         self.bits, self.t_bits = log2(n_dp) - 1, log2(n_t)
         self.stages = 2 + self.bits + self.t_bits
@@ -949,7 +966,7 @@
         return out
 
     attention = group > 0
-    keeps, sends = take(count), take(count)
+    grads = take(count)
     if attention:
         (sc_ref, q_ref, do_ref, lse_ref, delta_ref) = take(5)
         kvs = take(n_t)
@@ -964,7 +981,7 @@
     greet_all(n_dp, n_t, me, z)
     works = [
         Scatter(
-            n_dp, n_t, me, z, c, keeps[c], sends[c], lands[c], outs[c], helds[c], tile, landings, sems
+            n_dp, n_t, me, z, c, grads[c], lands[c], outs[c], helds[c], tile, landings, sems
         )
         for c in range(count)
     ]
@@ -1011,15 +1028,13 @@
             descend.finish(r)
 
 
-def scatter(keeps, sends, n_dp, n_t, collective_id, attention=None):
-    count = len(keeps)
+def scatter(grads, n_dp, n_t, collective_id, attention=None):
+    count = len(grads)
     bits = log2(n_dp) - 1
-    block = keeps[0].shape[1] >> bits
-    widest = max(k.shape[2] for k in keeps)
-    shapes = [(n_t,) + (2,) * bits + (block, k.shape[2]) for k in keeps]
-    args = [k.reshape(s) for k, s in zip(keeps, shapes)] + [
-        k.reshape(s) for k, s in zip(sends, shapes)
-    ]
+    block = grads[0].shape[2]
+    widest = max(k.shape[3] for k in grads)
+    shapes = [(n_t,) + (2,) * bits + (block, k.shape[3]) for k in grads]
+    args = [k.reshape(s[:1] + (2,) + s[1:]) for k, s in zip(grads, shapes)]
     anywhere = pl.BlockSpec(memory_space=pl.ANY)
     vmem = pl.BlockSpec(memory_space=pltpu.VMEM)
     smem = pl.BlockSpec(memory_space=pltpu.SMEM)
@@ -1093,7 +1108,7 @@
     me_dp = lax.axis_index("dp")
     me_t = lax.axis_index("tensor")
     length = lengths[0]
-    me = jnp.stack([me_t, me_t]).astype(jnp.int32)
+    me = jnp.stack([me_t, me_dp]).astype(jnp.int32)
     sc = jnp.stack([me_t.astype(jnp.int32), length])
 
     gains = jnp.stack([attn_gain, mlp_gain], axis=1)
@@ -1120,28 +1135,28 @@
     inv_one = lax.rsqrt(jnp.mean(x * x, axis=1, keepdims=True) + eps_norm)
     g32 = cotangent.astype(f32) * live
     g = g32.astype(bf16)
-    gt = to_relative(g.T, me_dp, n_dp)
+    gt = g.T
     n1 = (x * inv_one * gain_one).astype(bf16)
     q, kv = qkv_project(n1, w_qkv, cosine, sine, nq, nk)
     q = q.reshape(n_t * nq, rows)
 
-    *w_all, = gather([out_weight.T] + shard_mlp, n_dp, n_t, 1, kv)
-    kvs = [kv] + w_all[1 + CHUNKS :]
-    w_all = w_all[: 1 + CHUNKS]
-    w_out, *w_mlp = [w.reshape(n_t, width, w.shape[-1]) for w in w_all]
-    att, lse = attend(sc, q, kvs)
+    *gathered, att, lse = gather([out_weight.T] + shard_mlp, n_dp, n_t, 1, (kv, q, length))
+    w_out, *w_mlp = [w.reshape(n_t, width, w.shape[-1]) for w in gathered[: 1 + CHUNKS]]
+    kvs = [kv] + gathered[1 + CHUNKS :]
     att_z = att.reshape(n_t, no, rows)
     h_one = out_project(att_z, w_out, tokens, no, 0)
 
     inv_two = lax.rsqrt(jnp.mean(h_one * h_one, axis=1, keepdims=True) + eps_norm)
     n2 = (h_one * inv_two * gain_two).astype(bf16)
-    n2t = to_relative(n2.T, me_dp, n_dp)
+    n2t = n2.T
     carry = None
     shares = []
     for c in range(CHUNKS):
-        out_sum, dn_sum, keep, send = mlp(me, n2, n2t, g, gt, w_mlp[c], 0, tile, carry)
+        out_sum, dn_sum, share = mlp(
+            me, n2, n2t, g, gt, w_mlp[c], 0, tile, carry, n_dp
+        )
         carry = (out_sum, dn_sum)
-        shares.append((keep, send))
+        shares.append(share)
     mlp_out, d_n2 = carry
     block_out = (live * (h_one + mlp_out)).astype(bf16)
 
@@ -1150,30 +1165,26 @@
     gain_two_part = jnp.sum(d_n2 * h_one * inv_two, axis=0)
     d_h = g32 + inv_two * scaled - h_one * (inv_two * inv_two * inv_two * inner)
     d_h_low = d_h.astype(bf16)
-    d_h_t = to_relative(d_h_low.T, me_dp, n_dp)
-    d_att, keep, send = out_back(me, d_h_low, d_h_t, att_z, w_out, no, 0)
-    shares.append((keep, send))
+    d_h_t = d_h_low.T
+    d_att, share = out_back(me, d_h_low, d_h_t, att_z, w_out, no, 0, n_dp)
+    shares.append(share)
 
     d_att = d_att.reshape(n_t * no, rows)
     groups, _, lanes = lse.shape
     delta = (d_att.astype(f32) * att.astype(f32)).reshape(groups, -1, HEAD_SIZE, rows).sum(axis=2)
     delta = delta.reshape(groups, 1, lanes)
     *grads, out_share, d_q, d_kv = scatter(
-        [s[0] for s in shares],
-        [s[1] for s in shares],
+        shares,
         n_dp,
         n_t,
         2,
         (sc, q, d_att, lse, delta, kvs),
     )
-    n1t = to_relative(n1.T, me_dp, n_dp)
-    d_n1, keep, send = qkv_back(
-        me, d_q.reshape(n_t, nq, rows), d_kv, cosine, sine, n1t, w_qkv, nq, nk
+    n1t = n1.T
+    d_n1, q_part, kv_part = qkv_back(
+        me, d_q.reshape(n_t, nq, rows), d_kv, cosine, sine, n1t, w_qkv, nq, nk, n_dp
     )
-    middle = nq
-    q_share, kv_share = scatter(
-        [keep[:, :, :middle], keep[:, :, middle:]], [send[:, :, :middle], send[:, :, middle:]], n_dp, n_t, 3
-    )
+    q_share, kv_share = scatter([q_part, kv_part], n_dp, n_t, 3)
 
     scaled = d_n1 * gain_one
     inner = jnp.mean(scaled * x, axis=1, keepdims=True)

time: 1030 us -> 933 us (0.906)
  local copies, waits for them, and re-layouts: 96.8 us -> 40.8 us
  Pallas kernels: 878 us -> 827 us
  other arithmetic: 32.6 us -> 45.2 us
    pallas_call x2, Pallas kernels: 414 us -> 352 us  [scatter(): pl.pallas_call(functools.partial(scatter_kernel, n_dp, n_t, count, group)...]
    unnamed x149 -> x82, local copies, waits for them, and re-layouts: 44.4 us -> 9.41 us
    slice x2 -> x0, local copies, waits for them, and re-layouts: 10.6 us -> none  [the longest x1 5.4 us: local(): send[:, :, middle:]]
    pallas_call x3 -> x2, Pallas kernels: 325 us -> 327 us  [gather(): pl.pallas_call(functools.partial(gather_kernel, n_dp, n_t, count, attenti...]
  transfers between devices with their start and end apart: 5 -> 5, of which waited for: 1 -> 1; matrix products, arithmetic and copies ran while one was open for 3% -> 3% of each run, Pallas kernels for 7% -> 8%
where the time goes in v2:
time: 933 us; the launch traced here: 924 us
  Pallas kernels  827 us (89%)
  other arithmetic  45.2 us (5%)
  local copies, waits for them, and re-layouts  40.8 us (4%)
    pallas_call x2, Pallas kernels, scatter(): pl.pallas_call(functools.partial(scatter_kernel, n_dp, n_t, count, group)...  352 us
    pallas_call x2, Pallas kernels, gather(): pl.pallas_call(functools.partial(gather_kernel, n_dp, n_t, count, attenti...  327 us
    pallas_call x4, Pallas kernels, mlp(): pl.pallas_call(functools.partial(mlp_kernel, tile, first), grid_spec=pltp...  101 us
  transfers between devices with their start and end apart: 5, of which 1 were waited for; matrix products, arithmetic and copies ran while one was open for 3% of the time, Pallas kernels for 8%

profile of v2, /device:TPU:0, one launch (start us, length us, event | category | flops | bytes accessed | tf_op | source)
XLA Modules:
  0.0 923.6 jit_solution(5355225429851972067)
XLA Ops:
  5.1 76.9 %gather_weights.2 = bf16[4,8,192,896]{3,2,1,0:T(8,128)(2,1)} custom-call(bf16[192,896]{1,0:T(8,128)(2,1)} %fusion.12.refs_0_), custom_call_target="tpu_custom_call" | custom-call | tf_op jit(solution)/shard_map/gather_weights/pallas_call | solution.py:699
  87.7 10.0 %qkv_project.1 = (bf16[4,384,512]{2,1,0:T(8,128)(2,1)}, bf16[2,768,512]{2,1,0:T(8,128)(2,1)}) custom-call(bf16[512,1536]{1,0:T(8,128)(2,1)} %copy.81.n1_ref, bf16[4,1536,896]{2,1,0:T(8,128)(2,1)} %bitcast.52, f32[48,512]{1,0:T(8,128)} %get-tuple-element.163.cos_ref, f32[48,512]{1,0:T(8,128)} %get-tuple-element.162.sin_ref), custom_call_target="tpu_custom_call" | custom-call | flops 5637144576 | bytes 17301504 | tf_op jit(solution)/shard_map/qkv_project/pallas_call | solution.py:72
  99.4 250.3 %gather_weights.3 = (bf16[4,8,192,384]{3,2,1,0:T(8,128)(2,1)}, bf16[4,8,192,768]{3,2,1,0:T(8,128)(2,1)}, bf16[4,8,192,768]{3,2,1,0:T(8,128)(2,1)}, bf16[4,8,192,...) custom-call(bf16[192,384]{1,0:T(8,128)(2,1)} %bitcast.71, ...), custom_call_target="tpu_custom_call" | custom-call | tf_op jit(solution)/shard_map/gather_weights/pallas_call | solution.py:699
  349.7 8.4 out_project.1
  360.5 3.3 multiply_reduce_fusion.2
  366.9 2.6 copy.83
  369.5 3.1 fusion.9
  375.7 2.6 copy.90.n2_ref
  381.6 23.9 %mlp.4 = (f32[512,1536]{1,0:T(8,128)}, f32[512,1536]{1,0:T(8,128)}, bf16[4,8,192,768]{3,2,1,0:T(8,128)(2,1)}) custom-call(s32[2]{0:T(128)} %get-tuple-element.166.me_ref, bf16[512,1536]{1,0:T(8,128)(2,1)} %copy.90.n2_ref, bf16[1536,512]{1,0:T(8,128)(2,1)} %fusion.35.n2t_ref, bf16[512,1536]{1,0:T(8,128)(2,1)} %copy.91.g_ref, ...), custom_call_target="tpu_custom_call" | custom-call | flops 14495514624 | bytes 37748736 | tf_op jit(solution)/shard_map/mlp/pallas_call | solution.py:284
  405.5 25.9 %mlp.5 = (f32[512,1536]{1,0:T(8,128)}, f32[512,1536]{1,0:T(8,128)}, bf16[4,8,192,768]{3,2,1,0:T(8,128)(2,1)}) custom-call(s32[2]{0:T(128)} %get-tuple-element.166.me_ref, bf16[512,1536]{1,0:T(8,128)(2,1)} %copy.90.n2_ref, bf16[1536,512]{1,0:T(8,128)(2,1)} %fusion.35.n2t_ref, ...), custom_call_target="tpu_custom_call", output_to_operand_aliasing={{0}: (6, {}), {1}: (7, {})} | custom-call | flops 14495514624 | bytes 37748736 | tf_op jit(solution)/shard_map/mlp/pallas_call | solution.py:284
  431.4 25.8 %mlp.6 = (f32[512,1536]{1,0:T(8,128)}, f32[512,1536]{1,0:T(8,128)}, bf16[4,8,192,768]{3,2,1,0:T(8,128)(2,1)}) custom-call(s32[2]{0:T(128)} %get-tuple-element.166.me_ref, bf16[512,1536]{1,0:T(8,128)(2,1)} %copy.90.n2_ref, bf16[1536,512]{1,0:T(8,128)(2,1)} %fusion.35.n2t_ref, ...), custom_call_target="tpu_custom_call", output_to_operand_aliasing={{0}: (6, {}), {1}: (7, {})} | custom-call | flops 14495514624 | bytes 37748736 | tf_op jit(solution)/shard_map/mlp/pallas_call | solution.py:284
  457.2 25.7 %mlp.7 = (f32[512,1536]{1,0:T(8,128)}, f32[512,1536]{1,0:T(8,128)}, bf16[4,8,192,768]{3,2,1,0:T(8,128)(2,1)}) custom-call(s32[2]{0:T(128)} %get-tuple-element.166.me_ref, bf16[512,1536]{1,0:T(8,128)(2,1)} %copy.90.n2_ref, bf16[1536,512]{1,0:T(8,128)(2,1)} %fusion.35.n2t_ref, ...), custom_call_target="tpu_custom_call", output_to_operand_aliasing={{0}: (6, {}), {1}: (7, {})} | custom-call | flops 14495514624 | bytes 37748736 | tf_op jit(solution)/shard_map/mlp/pallas_call | solution.py:284
  483.0 3.7 copy.94
  486.7 2.9 multiply_reduce_fusion
  492.1 2.6 copy.97.dh_ref
  494.7 11.6 %out_back.1 = (bf16[4,384,512]{2,1,0:T(8,128)(2,1)}, bf16[4,8,192,384]{3,2,1,0:T(8,128)(2,1)}) custom-call(s32[2]{0:T(128)} %get-tuple-element.166.me_ref, bf16[512,1536]{1,0:T(8,128)(2,1)} %copy.97.dh_ref, bf16[1536,512]{1,0:T(8,128)(2,1)} %bitcast.58, bf16[4,384,512]{2,1,0:T(8,128)(2,1)} %bitcast.60, bf16[4,1536,384]{2,1,0:T(8,128)(2,1)} %bitcast.67), custom_call_target="tpu_custom_call" | custom-call | flops 4831838208 | bytes 15728640 | tf_op jit(solution)/shard_map/out_back/pallas_call | solution.py:134
  509.3 274.3 %scatter_grads.2 = (bf16[4,2,2,192,768]{4,3,2,1,0:T(8,128)(2,1)}, bf16[4,2,2,192,768]{4,3,2,1,0:T(8,128)(2,1)}, bf16[4,2,2,192,768]{4,3,2,1,0:T(8,128)(2,1)}, bf...) custom-call(bf16[4,2,2,2,192,768]{5,4,3,2,1,0:T(8,128)(2,1)} %bitcas, ...), custom_call_target="tpu_custom_call" | custom-call | tf_op jit(solution)/shard_map/scatter_grads/pallas_call | solution.py:1072
  783.6 16.8 %qkv_back.1 = (f32[512,1536]{1,0:T(8,128)}, bf16[4,8,192,384]{3,2,1,0:T(8,128)(2,1)}, bf16[4,8,192,384]{3,2,1,0:T(8,128)(2,1)}) custom-call(s32[2]{0:T(128)} %get-tuple-element.166.me_ref, f32[4,384,512]{2,1,0:T(8,128)} %bitcast.78, bf16[2,768,512]{2,1,0:T(8,128)(2,1)} %get-tuple-element.76.dkv_ref, f32[48,512]{1,0:T(8,128)} %get-tuple-element.163.cos_ref, ...), custom_call_target="tpu_custom_call" | custom-call | flops 9663676416 | bytes 28311552 | tf_op jit(solution)/shard_map/qkv_back/pallas_call | solution.py:186
  800.4 3.7 copy.98
  804.1 3.1 fusion.8
  812.7 3.8 copy.93
  816.5 6.8 fusion.6
  824.1 77.3 %scatter_grads.3 = (bf16[4,2,2,192,384]{4,3,2,1,0:T(8,128)(2,1)}, bf16[4,2,2,192,384]{4,3,2,1,0:T(8,128)(2,1)}, f32[192,384]{1,0:T(8,128)}, f32[192,384]{1,0:T(8,128)}) custom-call(bf16[4,2,2,2,192,384]{5,4,3,2,1,0:T(8,128)(2,1)} %bitcast.64, bf16[4,2,2,2,192,384]{5,4,3,2,1,0:T(8,128)(2,1)} %bitcast.65), custom_call_target="tpu_custom_call" | custom-call | tf_op jit(solution)/shard_map/scatter_grads/pallas_call | solution.py:1072
  909.7 2.6 collective-permute-start.3
  (145 shorter events, 53.7 us)
Async XLA Ops:
  2.9 80.9 %copy-start.2 = (bf16[512,1536]{0,1:T(8,128)(2,1)}, bf16[512,1536]{0,1:T(8,128)(2,1)S(1)}, u32[]{:S(2)}) copy-start(bf16[512,1536]{0,1:T(8,128)(2,1)S(1)} %copy.79) | copy-start | bytes 4718596
  5.1 78.7 %copy-start.25 = (f32[512]{0:T(512)S(1)}, f32[512]{0:T(512)}, u32[]{:S(2)}) copy-start(f32[512]{0:T(512)} %add_rsqrt_fusion.1) | copy-start | bytes 6148
  360.5 129.1 %copy-start = (f32[512,1536]{0,1:T(8,128)}, f32[512,1536]{0,1:T(8,128)S(1)}, u32[]{:S(2)}) copy-start(f32[512,1536]{0,1:T(8,128)S(1)} %copy.92) | copy-start | bytes 9437188
  363.8 125.8 %copy-start.24 = (f32[512]{0:T(512)}, f32[512]{0:T(512)S(1)}, u32[]{:S(2)}) copy-start(f32[512]{0:T(512)S(1)} %add_rsqrt_fusion) | copy-start | bytes 6148
  366.9 122.8 %copy-start.27 = (f32[512]{0:T(512)}, f32[512]{0:T(512)S(1)}, u32[]{:S(2)}) copy-start(f32[512]{0:T(512)S(1)} %fusion.26) | copy-start | bytes 6148
  369.5 4.7 copy-start.26
  494.7 11.6 %copy-start.8 = (bf16[1536,512]{1,0:T(8,128)(2,1)S(1)}, bf16[1536,512]{1,0:T(8,128)(2,1)}, u32[]{:S(2)}) copy-start(bf16[1536,512]{1,0:T(8,128)(2,1)} %get-tuple-element.51) | copy-start | bytes 4718596
  804.0 6.4 copy-start.15
  804.0 7.2 copy-start.14
  804.0 8.0 copy-start.29
  808.5 92.9 %collective-permute-start = (f32[4,2,192]{2,1,0:T(2,128)}, f32[4,2,192]{2,1,0:T(2,128)}, u32[]{:S(2)}, u32[]{:S(2)}) collective-permute-start(f32[4,2,192]{2,1,0:T(2,128)} %pad_maximum_fusion.7), channel_id=1, source_target_pairs={{0,4},{4,0},{8,12},{12,8},{16,20},{20,16},{24,28},{28,24},{1,5},{5... | collective-permute-start | bytes 18440 | tf_op jit(solution)/shard_map/ppermute | solution.py:331
  816.5 6.8 copy-start.13
  824.1 77.4 %copy-start.31 = (f32[1,2,192]{2,1,0:T(2,128)S(1)}, f32[1,2,192]{2,1,0:T(2,128)}, u32[]{:S(2)}) copy-start(f32[1,2,192]{2,1,0:T(2,128)} %get-tuple-element.154) | copy-start | bytes 4612
  824.1 77.4 %copy-start.32 = (f32[1,2,192]{2,1,0:T(2,128)S(1)}, f32[1,2,192]{2,1,0:T(2,128)}, u32[]{:S(2)}) copy-start(f32[1,2,192]{2,1,0:T(2,128)} %get-tuple-element.155) | copy-start | bytes 4612
  824.1 77.4 %copy-start.33 = (f32[1,2,192]{2,1,0:T(2,128)S(1)}, f32[1,2,192]{2,1,0:T(2,128)}, u32[]{:S(2)}) copy-start(f32[1,2,192]{2,1,0:T(2,128)} %get-tuple-element.156) | copy-start | bytes 4612
  824.1 77.4 %copy-start.34 = (f32[1,2,192]{2,1,0:T(2,128)S(1)}, f32[1,2,192]{2,1,0:T(2,128)}, u32[]{:S(2)}) copy-start(f32[1,2,192]{2,1,0:T(2,128)} %get-tuple-element.157) | copy-start | bytes 4612
  901.4 15.6 %copy-start.11 = (f32[192,256]{1,0:T(8,128)S(1)}, f32[192,256]{1,0:T(8,128)}, u32[]{:S(2)}) copy-start(f32[192,256]{1,0:T(8,128)} %get-tuple-element.136) | copy-start | bytes 589828
  901.4 15.6 %copy-start.12 = (f32[192,256]{1,0:T(8,128)S(1)}, f32[192,256]{1,0:T(8,128)}, u32[]{:S(2)}) copy-start(f32[192,256]{1,0:T(8,128)} %get-tuple-element.139) | copy-start | bytes 589828
  901.4 16.6 %copy-start.10 = (bf16[512,1536]{0,1:T(8,128)(2,1)S(1)}, bf16[512,1536]{0,1:T(8,128)(2,1)}, u32[]{:S(2)}) copy-start(bf16[512,1536]{0,1:T(8,128)(2,1)} %get-tuple-element.127) | copy-start | bytes 4718596
  902.3 3.7 collective-permute-start.1
  906.0 3.7 collective-permute-start.2
  909.7 4.9 collective-permute-start.3
  912.3 7.3 copy-start.9
  914.6 6.6 collective-permute-start.4
  (19 other events, 56.1 us)

commit v3 on v2

--- a/solution.py
+++ b/solution.py
@@ -12,8 +12,9 @@
 HALF = HEAD_SIZE // 2
 GAIN_LANES = 128
 CHUNKS = 4
-CLIMB_AT = 8
-CLIMB_STEP = 5
+MERGED = CHUNKS - 1
+CLIMB_AT = 7
+CLIMB_STEP = 4
 KEY_TILE = 256
 NEG = -1e30
 
@@ -39,10 +40,10 @@
     return pl.CostEstimate(flops=int(flops), bytes_accessed=int(nbytes), transcendentals=int(trans))
 
 
-def place(ref, me_ref, grad, col=0):
+def place(ref, me, grad, col=0):
     count, block = ref.shape[1], ref.shape[2]
     for d in range(count):
-        r = me_ref[1] ^ d
+        r = me ^ d
         at = (r & 1) * (count // 2) + (r >> 1)
         ref[0, at, :, col : col + grad.shape[1]] = grad[d * block : (d + 1) * block]
 
@@ -124,7 +125,7 @@
 def out_back_kernel(me_ref, dh_ref, dht_ref, att_ref, w_ref, da_ref, grad_ref):
     w = w_ref[0]
     da_ref[0] = dot(dh_ref[...], w).T.astype(bf16)
-    place(grad_ref, me_ref, dot(dht_ref[...], att_ref[0].T).astype(bf16))
+    place(grad_ref, me_ref[1], dot(dht_ref[...], att_ref[0].T).astype(bf16))
 
 
 def out_back(me, dh, dht, att, w, no, col, n_dp):
@@ -173,8 +174,8 @@
     w = w_ref[0, :, : nq + 2 * nk]
     dn_ref[...] += dot(d, w, ((1,), (1,)))
     grad = dot(n1t_ref[...], d).astype(bf16)
-    place(dwq_ref, me_ref, grad[:, :nq])
-    place(dwkv_ref, me_ref, grad[:, nq:])
+    place(dwq_ref, me_ref[1], grad[:, :nq])
+    place(dwkv_ref, me_ref[1], grad[:, nq:])
 
 
 def qkv_back(me, dq, dkv, cosine, sine, n1t, w, nq, nk, n_dp):
@@ -223,6 +224,24 @@
     return jnp.broadcast_to(ok, s.shape)
 
 
+def mlp_step(tile, me, n2_ref, n2t_ref, g_ref, gt_ref, w_ref, out_ref, dn_ref, grad_ref):
+    pair = w_ref[0, :, : 2 * tile]
+    wd = w_ref[0, :, 2 * tile :]
+    both = dot(n2_ref[...], pair)
+    gate, up = both[:, :tile], both[:, tile:]
+    d_hidden = dot(g_ref[...], wd)
+    sigma = 1.0 / (1.0 + jnp.exp(-gate))
+    active = gate * sigma
+    hidden = (active * up).astype(bf16)
+    d_gate = (d_hidden * up * (sigma * (1.0 + gate * (1.0 - sigma)))).astype(bf16)
+    d_up = (d_hidden * active).astype(bf16)
+    d_both = jnp.concatenate([d_gate, d_up], axis=1)
+    out_ref[...] += dot(hidden, wd, ((1,), (1,)))
+    dn_ref[...] += dot(d_both, pair, ((1,), (1,)))
+    place(grad_ref, me, dot(n2t_ref[...], d_both).astype(bf16), 0)
+    place(grad_ref, me, dot(gt_ref[...], hidden).astype(bf16), 2 * tile)
+
+
 def mlp_kernel(
     tile, first, me_ref, n2_ref, n2t_ref, g_ref, gt_ref, w_ref, *refs
 ):
@@ -241,23 +260,7 @@
             out_ref[...] = out_in[...]
             dn_ref[...] = dn_in[...]
 
-    wg = w_ref[0, :, :tile]
-    wu = w_ref[0, :, tile : 2 * tile]
-    wd = w_ref[0, :, 2 * tile : 3 * tile]
-    n2, g = n2_ref[...], g_ref[...]
-    gate = dot(n2, wg)
-    up = dot(n2, wu)
-    d_hidden = dot(g, wd)
-    sigma = 1.0 / (1.0 + jnp.exp(-gate))
-    active = gate * sigma
-    hidden = (active * up).astype(bf16)
-    d_gate = (d_hidden * up * (sigma * (1.0 + gate * (1.0 - sigma)))).astype(bf16)
-    d_up = (d_hidden * active).astype(bf16)
-    out_ref[...] += dot(hidden, wd, ((1,), (1,)))
-    dn_ref[...] += dot(d_gate, wg, ((1,), (1,))) + dot(d_up, wu, ((1,), (1,)))
-    place(grad_ref, me_ref, dot(n2t_ref[...], d_gate).astype(bf16), 0)
-    place(grad_ref, me_ref, dot(n2t_ref[...], d_up).astype(bf16), tile)
-    place(grad_ref, me_ref, dot(gt_ref[...], hidden).astype(bf16), 2 * tile)
+    mlp_step(tile, me_ref[1], n2_ref, n2t_ref, g_ref, gt_ref, w_ref, out_ref, dn_ref, grad_ref)
 
 
 def mlp(me, n2, n2t, g, gt, w, chunk, tile, carry, n_dp):
@@ -376,19 +379,24 @@
 
 
 class Gather:
-    def __init__(self, n_dp, n_t, me, z, index, shard, whole, sems):
+    def __init__(self, n_dp, n_t, me, z, index, shard, whole, sems, lanes=None):
         self.n_dp, self.n_t, self.me, self.z = n_dp, n_t, me, z
-        self.index, self.shard, self.whole = index, shard, whole
+        self.index, self.shard, self.whole, self.lanes = index, shard, whole, lanes
         self.own, self.z_send, self.z_recv, self.x_send, self.x_recv = sems
         self.bits = log2(n_dp) - 1
 
+    def place_of(self, piece, d):
+        if self.lanes is None:
+            return self.whole.at[piece, d]
+        return self.whole.at[piece, d, :, self.lanes]
+
     def local(self):
         return pltpu.make_async_copy(
-            self.shard, self.whole.at[self.z, self.me], self.own.at[self.index]
+            self.shard, self.place_of(self.z, self.me), self.own.at[self.index]
         )
 
     def hop(self, piece, direction, hops):
-        source = self.whole.at[piece, self.me]
+        source = self.place_of(piece, self.me)
         step = 1 - 2 * direction
         return pltpu.make_async_remote_copy(
             source,
@@ -435,7 +443,7 @@
         shift = jnp.where(odd, self.bits - stage + 1, 1)
         partner = self.me ^ bit
         origin = partner if incoming else self.me
-        held = self.whole.at[piece, origin ^ (i << shift)]
+        held = self.place_of(piece, origin ^ (i << shift))
         at = (1 << stage) - 1 + i
         return pltpu.make_async_remote_copy(
             held,
@@ -450,7 +458,7 @@
         piece = self.order(k)
         partner = self.me ^ 1
         origin = partner if incoming else self.me
-        held = self.whole.at[piece, origin ^ (i << 1)]
+        held = self.place_of(piece, origin ^ (i << 1))
         at = (1 << self.bits) - 1 + i
         return pltpu.make_async_remote_copy(
             held,
@@ -588,7 +596,7 @@
     lax.fori_loop(0, groups, body, 0)
 
 
-def gather_kernel(n_dp, n_t, count, climbs, *refs):
+def gather_kernel(n_dp, n_t, count, merged, climbs, *refs):
     refs = list(refs)
 
     def take(k):
@@ -599,7 +607,11 @@
     shards = take(count)
     if climbs:
         own, q_ref, length_ref = take(3)
-    wholes = take(count)
+    wholes = [(ref, None) for ref in take(count - merged)]
+    if merged:
+        (ref,) = take(1)
+        wide = shards[-1].shape[1]
+        wholes += [(ref, slice(i * wide, (i + 1) * wide)) for i in range(merged)]
     if climbs:
         kept = take(n_t - 1)
         att_ref, lse_ref = take(2)
@@ -607,7 +619,8 @@
     me, z = lax.axis_index("dp"), lax.axis_index("tensor")
     neighbours(n_dp, n_t, me, z)
     works = [
-        Gather(n_dp, n_t, me, z, c, shards[c], wholes[c], sems) for c in range(count)
+        Gather(n_dp, n_t, me, z, c, shards[c], wholes[c][0], sems, wholes[c][1])
+        for c in range(count)
     ]
     if climbs:
         climb_sems = take(2)
@@ -659,16 +672,19 @@
             climb.finish(r)
 
 
-def gather(shards, n_dp, n_t, collective_id, attention=None):
+def gather(shards, n_dp, n_t, collective_id, attention=None, merged=0):
     count = len(shards)
     shapes = [
-        jax.ShapeDtypeStruct((n_t, n_dp) + s.shape, s.dtype) for s in shards
+        jax.ShapeDtypeStruct((n_t, n_dp) + s.shape, s.dtype) for s in shards[: count - merged]
     ]
+    if merged:
+        block, wide = shards[-1].shape
+        shapes.append(jax.ShapeDtypeStruct((n_t, n_dp, block, merged * wide), bf16))
     args = list(shards)
     anywhere = pl.BlockSpec(memory_space=pl.ANY)
     vmem = pl.BlockSpec(memory_space=pltpu.VMEM)
     in_specs = [anywhere] * count
-    out_specs = [anywhere] * count
+    out_specs = [anywhere] * len(shapes)
     scratch = [
         pltpu.SemaphoreType.DMA((count,)),
         pltpu.SemaphoreType.DMA((count, 2, n_t)),
@@ -697,7 +713,7 @@
             pltpu.SemaphoreType.DMA,
         ]
     return pl.pallas_call(
-        functools.partial(gather_kernel, n_dp, n_t, count, attention is not None),
+        functools.partial(gather_kernel, n_dp, n_t, count, merged, attention is not None),
         in_specs=in_specs,
         out_specs=out_specs,
         out_shape=shapes,
@@ -709,6 +725,95 @@
     )(*args)
 
 
+def mlp_gather_kernel(
+    n_dp, n_t, tile, n2_ref, n2t_ref, g_ref, gt_ref, w_ref, shard_ref,
+    out_ref, dn_ref, grad_ref, whole_ref, *sems
+):
+    me, z = lax.axis_index("dp"), lax.axis_index("tensor")
+    step = pl.program_id(0) * pl.num_programs(1) + pl.program_id(1)
+    steps = w_ref.shape[0] * MERGED * n_t
+    work = Gather(n_dp, n_t, me, z, 0, shard_ref, whole_ref, sems)
+    stages = log2(n_dp)
+
+    @pl.when(step == 0)
+    def _():
+        neighbours(n_dp, n_t, me, z)
+        work.send_own()
+        out_ref[...] = jnp.zeros_like(out_ref)
+        dn_ref[...] = jnp.zeros_like(dn_ref)
+
+    for n in range(n_t + 2 * (stages - 1)):
+
+        @pl.when(step == min(n, steps - 1))
+        def _():
+            if n < n_t:
+                work.arrive(n)
+                work.spread(n, 0)
+            for stage in range(1, stages):
+                at = n - 2 * stage
+                if 0 <= at < n_t:
+                    work.spread(at, stage)
+
+    mlp_step(
+        tile, me, n2_ref, n2t_ref, g_ref, gt_ref, w_ref, out_ref, dn_ref, grad_ref.at[0]
+    )
+
+    @pl.when(step == steps - 1)
+    def _():
+        for k in range(n_t):
+            work.finish(k)
+
+
+def mlp_gather(n2, n2t, g, gt, w, shard, tile, n_dp, n_t, collective_id):
+    rows, width = n2.shape
+    block = width // n_dp
+    full = pl.BlockSpec((rows, width), lambda c, i: (0, 0))
+    full_t = pl.BlockSpec((width, rows), lambda c, i: (0, 0))
+    anywhere = pl.BlockSpec(memory_space=pl.ANY)
+    cols = 3 * tile
+    return pl.pallas_call(
+        functools.partial(mlp_gather_kernel, n_dp, n_t, tile),
+        grid=(MERGED, n_t),
+        in_specs=[
+            full,
+            full_t,
+            full,
+            full_t,
+            pl.BlockSpec((1, width, cols), lambda c, i: (i, 0, c)),
+            anywhere,
+        ],
+        out_specs=[
+            full,
+            full,
+            pl.BlockSpec(
+                (1, 1, n_dp, block, cols),
+                lambda c, i: (c, i ^ lax.axis_index("tensor"), 0, 0, 0),
+            ),
+            anywhere,
+        ],
+        out_shape=[
+            jax.ShapeDtypeStruct((rows, width), f32),
+            jax.ShapeDtypeStruct((rows, width), f32),
+            jax.ShapeDtypeStruct((MERGED, n_t, n_dp, block, cols), bf16),
+            jax.ShapeDtypeStruct((n_t, n_dp, block, cols), bf16),
+        ],
+        scratch_shapes=[
+            pltpu.SemaphoreType.DMA((1,)),
+            pltpu.SemaphoreType.DMA((1, 2, n_t)),
+            pltpu.SemaphoreType.DMA((1, 2, n_t)),
+            pltpu.SemaphoreType.DMA((1, n_t, n_dp - 1)),
+            pltpu.SemaphoreType.DMA((1, n_t, n_dp - 1)),
+        ],
+        compiler_params=pltpu.CompilerParams(
+            dimension_semantics=("arbitrary", "arbitrary"),
+            collective_id=collective_id,
+            has_side_effects=True,
+            vmem_limit_bytes=VMEM_LIMIT,
+        ),
+        name="mlp_gather",
+    )(n2, n2t, g, gt, w, shard)
+
+
 def greet_all(n_dp, n_t, me, z):
     barrier = pltpu.get_barrier_semaphore()
     masks = [1 << b for b in range(log2(n_dp))]
@@ -741,7 +846,8 @@
 class Scatter:
     def __init__(self, n_dp, n_t, me, z, index, grad, land, out, held, tile, landings, sems):
         self.n_t, self.me, self.z, self.index = n_t, me, z, index
-        self.keep, self.send = grad.at[:, 0], grad.at[:, 1]
+        ref, lead = grad
+        self.keep, self.send = ref.at[lead + (slice(None), 0)], ref.at[lead + (slice(None), 1)]
         self.land, self.out, self.held = land, out, held
         self.tile, self.landings, self.sems = tile, landings, sems
         self.bits, self.t_bits = log2(n_dp) - 1, log2(n_t)
@@ -957,7 +1063,7 @@
             dq_ref[...] = jnp.zeros_like(dq_ref)
 
 
-def scatter_kernel(n_dp, n_t, count, group, *refs):
+def scatter_kernel(n_dp, n_t, stacked, group, *refs):
     refs = list(refs)
 
     def take(k):
@@ -966,7 +1072,10 @@
         return out
 
     attention = group > 0
-    grads = take(count)
+    grads = []
+    for ref, depth in zip(take(len(stacked)), stacked):
+        grads += [(ref, (c,)) for c in range(depth)] if depth else [(ref, ())]
+    count = len(grads)
     if attention:
         (sc_ref, q_ref, do_ref, lse_ref, delta_ref) = take(5)
         kvs = take(n_t)
@@ -1029,12 +1138,17 @@
 
 
 def scatter(grads, n_dp, n_t, collective_id, attention=None):
-    count = len(grads)
     bits = log2(n_dp) - 1
-    block = grads[0].shape[2]
-    widest = max(k.shape[3] for k in grads)
-    shapes = [(n_t,) + (2,) * bits + (block, k.shape[3]) for k in grads]
-    args = [k.reshape(s[:1] + (2,) + s[1:]) for k, s in zip(grads, shapes)]
+    block = grads[0].shape[-2]
+    widest = max(k.shape[-1] for k in grads)
+    stacked = [k.shape[0] if k.ndim == 5 else 0 for k in grads]
+    shapes = []
+    for k, depth in zip(grads, stacked):
+        shapes += [(n_t,) + (2,) * bits + (block, k.shape[-1])] * max(depth, 1)
+    count = len(shapes)
+    args = [
+        k.reshape(k.shape[: k.ndim - 3] + (2,) * (bits + 1) + k.shape[-2:]) for k in grads
+    ]
     anywhere = pl.BlockSpec(memory_space=pl.ANY)
     vmem = pl.BlockSpec(memory_space=pltpu.VMEM)
     smem = pl.BlockSpec(memory_space=pltpu.SMEM)
@@ -1070,7 +1184,7 @@
         scratch += [pltpu.VMEM(kvs[0].shape, bf16)] * (2 * (n_t - 1))
         scratch += [pltpu.SemaphoreType.DMA((n_t,))] * 2
     outs = pl.pallas_call(
-        functools.partial(scatter_kernel, n_dp, n_t, count, group),
+        functools.partial(scatter_kernel, n_dp, n_t, stacked, group),
         in_specs=in_specs,
         out_specs=out_specs,
         out_shape=out_shape,
@@ -1140,23 +1254,28 @@
     q, kv = qkv_project(n1, w_qkv, cosine, sine, nq, nk)
     q = q.reshape(n_t * nq, rows)
 
-    *gathered, att, lse = gather([out_weight.T] + shard_mlp, n_dp, n_t, 1, (kv, q, length))
-    w_out, *w_mlp = [w.reshape(n_t, width, w.shape[-1]) for w in gathered[: 1 + CHUNKS]]
-    kvs = [kv] + gathered[1 + CHUNKS :]
+    w_out, w_mlp, *above, att, lse = gather(
+        [out_weight.T] + shard_mlp[:MERGED], n_dp, n_t, 1, (kv, q, length), MERGED
+    )
+    w_out = w_out.reshape(n_t, width, no)
+    w_mlp = w_mlp.reshape(n_t, width, 3 * tile * MERGED)
+    kvs = [kv] + above
     att_z = att.reshape(n_t, no, rows)
     h_one = out_project(att_z, w_out, tokens, no, 0)
 
     inv_two = lax.rsqrt(jnp.mean(h_one * h_one, axis=1, keepdims=True) + eps_norm)
     n2 = (h_one * inv_two * gain_two).astype(bf16)
     n2t = n2.T
-    carry = None
-    shares = []
-    for c in range(CHUNKS):
-        out_sum, dn_sum, share = mlp(
-            me, n2, n2t, g, gt, w_mlp[c], 0, tile, carry, n_dp
-        )
-        carry = (out_sum, dn_sum)
-        shares.append(share)
+    out_sum, dn_sum, share, w_last = mlp_gather(
+        n2, n2t, g, gt, w_mlp, shard_mlp[MERGED], tile, n_dp, n_t, 4
+    )
+    w_last = w_last.reshape(n_t, width, 3 * tile)
+    shares = [share]
+    out_sum, dn_sum, share = mlp(
+        me, n2, n2t, g, gt, w_last, 0, tile, (out_sum, dn_sum), n_dp
+    )
+    shares.append(share)
+    carry = (out_sum, dn_sum)
     mlp_out, d_n2 = carry
     block_out = (live * (h_one + mlp_out)).astype(bf16)
 

time: 933 us -> 906 us (0.971)
  Pallas kernels: 827 us -> 801 us
    pallas_call x4 -> x1, Pallas kernels: 101 us -> 24.9 us  [mlp(): pl.pallas_call(functools.partial(mlp_kernel, tile, first), grid_spec=pltp...]
    pallas_call x4 -> x5, Pallas kernels: 679 us -> 729 us  [the longest x2 340 us: scatter(): pl.pallas_call(functools.partial(scatter_kernel, n_dp, n_t, stacked, grou...]
  transfers between devices with their start and end apart: 5 -> 5, of which waited for: 1 -> 2; matrix products, arithmetic and copies ran while one was open for 3% -> 3% of each run, Pallas kernels for 8% -> 9%
where the time goes in v3:
time: 906 us; the launch traced here: 896 us
  Pallas kernels  801 us (88%)
  other arithmetic  45 us (5%)
  local copies, waits for them, and re-layouts  40.7 us (4%)
    pallas_call x2, Pallas kernels, scatter(): pl.pallas_call(functools.partial(scatter_kernel, n_dp, n_t, stacked, grou...  340 us
    pallas_call x2, Pallas kernels, gather(): pl.pallas_call(functools.partial(gather_kernel, n_dp, n_t, count, merged,...  274 us
    pallas_call x1, Pallas kernels, mlp_gather(): pl.pallas_call(functools.partial(mlp_gather_kernel, n_dp, n_t, tile), gri...  115 us
    pallas_call x1, Pallas kernels, mlp(): pl.pallas_call(functools.partial(mlp_kernel, tile, first), grid_spec=pltp...  24.9 us
  transfers between devices with their start and end apart: 5, of which 2 were waited for; matrix products, arithmetic and copies ran while one was open for 3% of the time, Pallas kernels for 9%

profile of v3, /device:TPU:0, one launch (start us, length us, event | category | flops | bytes accessed | tf_op | source)
XLA Modules:
  0.0 896.3 jit_solution(4041134819762243503)
XLA Ops:
  5.1 76.9 %gather_weights.2 = bf16[4,8,192,896]{3,2,1,0:T(8,128)(2,1)} custom-call(bf16[192,896]{1,0:T(8,128)(2,1)} %fusion.12.refs_0_), custom_call_target="tpu_custom_call" | custom-call | tf_op jit(solution)/shard_map/gather_weights/pallas_call | solution.py:715
  87.7 10.0 %qkv_project.1 = (bf16[4,384,512]{2,1,0:T(8,128)(2,1)}, bf16[2,768,512]{2,1,0:T(8,128)(2,1)}) custom-call(bf16[512,1536]{1,0:T(8,128)(2,1)} %copy.69.n1_ref, bf16[4,1536,896]{2,1,0:T(8,128)(2,1)} %bitcast.50, f32[48,512]{1,0:T(8,128)} %get-tuple-element.147.cos_ref, f32[48,512]{1,0:T(8,128)} %get-tuple-element.146.sin_ref), custom_call_target="tpu_custom_call" | custom-call | flops 5637144576 | bytes 17301504 | tf_op jit(solution)/shard_map/qkv_project/pallas_call | solution.py:73
  99.4 197.1 %gather_weights.3 = (bf16[4,8,192,384]{3,2,1,0:T(8,128)(2,1)}, bf16[4,8,192,2304]{3,2,1,0:T(8,128)(2,1)}, bf16[2,768,512]{2,1,0:T(8,128)(2,1)}, bf16[2,768,512]{...) custom-call(bf16[192,384]{1,0:T(8,128)(2,1)} %bitcast.66, ...), custom_call_target="tpu_custom_call" | custom-call | tf_op jit(solution)/shard_map/gather_weights/pallas_call | solution.py:715
  296.6 8.4 out_project.1
  305.0 2.4 copy.76
  307.4 3.3 multiply_reduce_fusion.2
  313.7 2.7 copy.71
  316.3 3.0 fusion.9
  322.5 2.6 copy.74.n2_ref
  325.1 2.6 copy.75.g_ref
  328.3 114.9 %mlp_gather.1 = (f32[512,1536]{1,0:T(8,128)}, f32[512,1536]{1,0:T(8,128)}, bf16[3,4,8,192,768]{4,3,2,1,0:T(8,128)(2,1)}, bf16[4,8,192,768]{3,2,1,0:T(8,128)(2,1)}) custom-call(bf16[512,1536]{1,0:T(8,128)(2,1)} %copy.74.n2_ref, bf16[1536,512]{1,0:T(8,128)(2,1)} %fusion.35.n2t_ref, bf16[512,1536]{1,0:T(8,128)(2,1)} %copy.75.g_ref, ...), custom_call_target="tpu_custom_call" | custom-call | tf_op jit(solution)/shard_map/mlp_gather/pallas_call | solution.py:774
  443.1 24.9 %mlp.1 = (f32[512,1536]{1,0:T(8,128)}, f32[512,1536]{1,0:T(8,128)}, bf16[4,8,192,768]{3,2,1,0:T(8,128)(2,1)}) custom-call(s32[2]{0:T(128)} %get-tuple-element.150.me_ref, bf16[512,1536]{1,0:T(8,128)(2,1)} %copy.74.n2_ref, bf16[1536,512]{1,0:T(8,128)(2,1)} %fusion.35.n2t_ref, ...), custom_call_target="tpu_custom_call", output_to_operand_aliasing={{0}: (6, {}), {1}: (7, {})} | custom-call | flops 14495514624 | bytes 37748736 | tf_op jit(solution)/shard_map/mlp/pallas_call | solution.py:287
  468.1 3.6 copy.78
  471.6 2.9 multiply_reduce_fusion
  477.0 2.6 copy.81.dh_ref
  479.6 11.6 %out_back.1 = (bf16[4,384,512]{2,1,0:T(8,128)(2,1)}, bf16[4,8,192,384]{3,2,1,0:T(8,128)(2,1)}) custom-call(s32[2]{0:T(128)} %get-tuple-element.150.me_ref, bf16[512,1536]{1,0:T(8,128)(2,1)} %copy.81.dh_ref, bf16[1536,512]{1,0:T(8,128)(2,1)} %bitcast.53, bf16[4,384,512]{2,1,0:T(8,128)(2,1)} %bitcast.55, bf16[4,1536,384]{2,1,0:T(8,128)(2,1)} %bitcast.62), custom_call_target="tpu_custom_call" | custom-call | flops 4831838208 | bytes 15728640 | tf_op jit(solution)/shard_map/out_back/pallas_call | solution.py:135
  494.2 263.7 %scatter_grads.2 = (bf16[4,2,2,192,768]{4,3,2,1,0:T(8,128)(2,1)}, bf16[4,2,2,192,768]{4,3,2,1,0:T(8,128)(2,1)}, bf16[4,2,2,192,768]{4,3,2,1,0:T(8,128)(2,1)}, bf...) custom-call(bf16[3,4,2,2,2,192,768]{6,5,4,3,2,1,0:T(8,128)(2,1)} %bi, ...), custom_call_target="tpu_custom_call" | custom-call | tf_op jit(solution)/shard_map/scatter_grads/pallas_call | solution.py:1186
  757.8 17.2 %qkv_back.1 = (f32[512,1536]{1,0:T(8,128)}, bf16[4,8,192,384]{3,2,1,0:T(8,128)(2,1)}, bf16[4,8,192,384]{3,2,1,0:T(8,128)(2,1)}) custom-call(s32[2]{0:T(128)} %get-tuple-element.150.me_ref, f32[4,384,512]{2,1,0:T(8,128)} %bitcast.70, bf16[2,768,512]{2,1,0:T(8,128)(2,1)} %get-tuple-element.60.dkv_ref, f32[48,512]{1,0:T(8,128)} %get-tuple-element.147.cos_ref, ...), custom_call_target="tpu_custom_call" | custom-call | flops 9663676416 | bytes 28311552 | tf_op jit(solution)/shard_map/qkv_back/pallas_call | solution.py:187
  775.1 3.7 copy.82
  778.8 3.1 fusion.8
  787.4 3.8 copy.77
  791.2 6.8 fusion.6
  798.8 76.5 %scatter_grads.3 = (bf16[4,2,2,192,384]{4,3,2,1,0:T(8,128)(2,1)}, bf16[4,2,2,192,384]{4,3,2,1,0:T(8,128)(2,1)}, f32[192,384]{1,0:T(8,128)}, f32[192,384]{1,0:T(8,128)}) custom-call(bf16[4,2,2,2,192,384]{5,4,3,2,1,0:T(8,128)(2,1)} %bitcast.59, bf16[4,2,2,2,192,384]{5,4,3,2,1,0:T(8,128)(2,1)} %bitcast.60), custom_call_target="tpu_custom_call" | custom-call | tf_op jit(solution)/shard_map/scatter_grads/pallas_call | solution.py:1186
  883.5 2.5 collective-permute-start.3
  (143 shorter events, 47.7 us)
Async XLA Ops:
  2.9 80.9 %copy-start.2 = (bf16[512,1536]{0,1:T(8,128)(2,1)}, bf16[512,1536]{0,1:T(8,128)(2,1)S(1)}, u32[]{:S(2)}) copy-start(bf16[512,1536]{0,1:T(8,128)(2,1)S(1)} %copy.67) | copy-start | bytes 4718596
  5.1 78.7 %copy-start.25 = (f32[512]{0:T(512)S(1)}, f32[512]{0:T(512)}, u32[]{:S(2)}) copy-start(f32[512]{0:T(512)} %add_rsqrt_fusion.1) | copy-start | bytes 6148
  307.3 167.2 %copy-start = (f32[512,1536]{0,1:T(8,128)}, f32[512,1536]{0,1:T(8,128)S(1)}, u32[]{:S(2)}) copy-start(f32[512,1536]{0,1:T(8,128)S(1)} %copy.76) | copy-start | bytes 9437188
  310.7 163.9 %copy-start.24 = (f32[512]{0:T(512)}, f32[512]{0:T(512)S(1)}, u32[]{:S(2)}) copy-start(f32[512]{0:T(512)S(1)} %add_rsqrt_fusion) | copy-start | bytes 6148
  313.7 160.9 %copy-start.27 = (f32[512]{0:T(512)}, f32[512]{0:T(512)S(1)}, u32[]{:S(2)}) copy-start(f32[512]{0:T(512)S(1)} %fusion.26) | copy-start | bytes 6148
  316.3 4.6 copy-start.26
  479.6 11.6 %copy-start.8 = (bf16[1536,512]{1,0:T(8,128)(2,1)S(1)}, bf16[1536,512]{1,0:T(8,128)(2,1)}, u32[]{:S(2)}) copy-start(bf16[1536,512]{1,0:T(8,128)(2,1)} %get-tuple-element.43) | copy-start | bytes 4718596
  778.7 6.4 copy-start.15
  778.8 7.2 copy-start.14
  778.8 8.0 copy-start.29
  783.3 92.1 %collective-permute-start = (f32[4,2,192]{2,1,0:T(2,128)}, f32[4,2,192]{2,1,0:T(2,128)}, u32[]{:S(2)}, u32[]{:S(2)}) collective-permute-start(f32[4,2,192]{2,1,0:T(2,128)} %pad_maximum_fusion.7), channel_id=1, source_target_pairs={{0,4},{4,0},{8,12},{12,8},{16,20},{20,16},{24,28},{28,24},{1,5},{5... | collective-permute-start | bytes 18440 | tf_op jit(solution)/shard_map/ppermute | solution.py:334
  791.2 6.8 copy-start.13
  798.8 76.6 %copy-start.31 = (f32[1,2,192]{2,1,0:T(2,128)S(1)}, f32[1,2,192]{2,1,0:T(2,128)}, u32[]{:S(2)}) copy-start(f32[1,2,192]{2,1,0:T(2,128)} %get-tuple-element.138) | copy-start | bytes 4612
  798.8 76.6 %copy-start.32 = (f32[1,2,192]{2,1,0:T(2,128)S(1)}, f32[1,2,192]{2,1,0:T(2,128)}, u32[]{:S(2)}) copy-start(f32[1,2,192]{2,1,0:T(2,128)} %get-tuple-element.139) | copy-start | bytes 4612
  798.8 76.6 %copy-start.33 = (f32[1,2,192]{2,1,0:T(2,128)S(1)}, f32[1,2,192]{2,1,0:T(2,128)}, u32[]{:S(2)}) copy-start(f32[1,2,192]{2,1,0:T(2,128)} %get-tuple-element.140) | copy-start | bytes 4612
  798.8 76.6 %copy-start.34 = (f32[1,2,192]{2,1,0:T(2,128)S(1)}, f32[1,2,192]{2,1,0:T(2,128)}, u32[]{:S(2)}) copy-start(f32[1,2,192]{2,1,0:T(2,128)} %get-tuple-element.141) | copy-start | bytes 4612
  875.3 14.6 %copy-start.11 = (f32[192,256]{1,0:T(8,128)S(1)}, f32[192,256]{1,0:T(8,128)}, u32[]{:S(2)}) copy-start(f32[192,256]{1,0:T(8,128)} %get-tuple-element.120) | copy-start | bytes 589828
  875.3 14.6 %copy-start.12 = (f32[192,256]{1,0:T(8,128)S(1)}, f32[192,256]{1,0:T(8,128)}, u32[]{:S(2)}) copy-start(f32[192,256]{1,0:T(8,128)} %get-tuple-element.123) | copy-start | bytes 589828
  875.4 15.6 %copy-start.10 = (bf16[512,1536]{0,1:T(8,128)(2,1)S(1)}, bf16[512,1536]{0,1:T(8,128)(2,1)}, u32[]{:S(2)}) copy-start(bf16[512,1536]{0,1:T(8,128)(2,1)} %get-tuple-element.111) | copy-start | bytes 4718596
  876.3 3.7 collective-permute-start.1
  879.9 3.6 collective-permute-start.2
  883.5 4.8 collective-permute-start.3
  886.1 6.5 copy-start.9
  888.4 5.7 collective-permute-start.4
  (19 other events, 55.9 us)

commit v4 on v3

--- a/solution.py
+++ b/solution.py
@@ -156,62 +156,6 @@
         cost_estimate=cost(4 * rows * width * no * zs, 4 * zs * width * no + 8 * rows * width),
         name="out_back",
     )(me, dh, dht, att, w)
-
-
-def qkv_back_kernel(
-    nq, nk, me_ref, dq_ref, dkv_ref, cos_ref, sin_ref, n1t_ref, w_ref, dn_ref, dwq_ref, dwkv_ref
-):
-    z = pl.program_id(0)
-
-    @pl.when(z == 0)
-    def _():
-        dn_ref[...] = jnp.zeros_like(dn_ref)
-
-    cosine, sine = cos_ref[...], sin_ref[...]
-    dq = turn(dq_ref[0], cosine, sine, -1.0).astype(bf16)
-    dk = turn(dkv_ref[0].astype(f32), cosine, sine, -1.0).astype(bf16)
-    d = jnp.concatenate([dq, dk, dkv_ref[1]], axis=0).T
-    w = w_ref[0, :, : nq + 2 * nk]
-    dn_ref[...] += dot(d, w, ((1,), (1,)))
-    grad = dot(n1t_ref[...], d).astype(bf16)
-    place(dwq_ref, me_ref[1], grad[:, :nq])
-    place(dwkv_ref, me_ref[1], grad[:, nq:])
-
-
-def qkv_back(me, dq, dkv, cosine, sine, n1t, w, nq, nk, n_dp):
-    zs, _, rows = dq.shape
-    width = n1t.shape[0]
-    block = width // n_dp
-    cols = w.shape[2]
-    out = nq + 2 * nk
-    return pl.pallas_call(
-        functools.partial(qkv_back_kernel, nq, nk),
-        grid_spec=pltpu.PrefetchScalarGridSpec(
-            num_scalar_prefetch=1,
-            grid=(zs,),
-            in_specs=[
-                pl.BlockSpec((1, nq, rows), lambda z, m: (z, 0, 0)),
-                pl.BlockSpec((2, nk, rows), lambda z, m: (0, z, 0)),
-                pl.BlockSpec((HALF, rows), lambda z, m: (0, 0)),
-                pl.BlockSpec((HALF, rows), lambda z, m: (0, 0)),
-                pl.BlockSpec((width, rows), lambda z, m: (0, 0)),
-                pl.BlockSpec((1, width, cols), lambda z, m: (z, 0, 0)),
-            ],
-            out_specs=[
-                pl.BlockSpec((rows, width), lambda z, m: (0, 0)),
-                pl.BlockSpec((1, n_dp, block, nq), lambda z, m: (z ^ m[0], 0, 0, 0)),
-                pl.BlockSpec((1, n_dp, block, 2 * nk), lambda z, m: (z ^ m[0], 0, 0, 0)),
-            ],
-        ),
-        out_shape=[
-            jax.ShapeDtypeStruct((rows, width), f32),
-            jax.ShapeDtypeStruct((zs, n_dp, block, nq), bf16),
-            jax.ShapeDtypeStruct((zs, n_dp, block, 2 * nk), bf16),
-        ],
-        compiler_params=params("arbitrary"),
-        cost_estimate=cost(4 * rows * width * out * zs, 4 * zs * width * cols + 8 * rows * width),
-        name="qkv_back",
-    )(me, dq, dkv, cosine, sine, n1t, w)
 
 
 def key_mask(s, key_first, query_first, length, rows, diagonal):
@@ -844,7 +788,7 @@
 
 
 class Scatter:
-    def __init__(self, n_dp, n_t, me, z, index, grad, land, out, held, tile, landings, sems):
+    def __init__(self, n_dp, n_t, me, z, index, grad, land, out, held, first, cols, tile, landings, sems):
         self.n_t, self.me, self.z, self.index = n_t, me, z, index
         ref, lead = grad
         self.keep, self.send = ref.at[lead + (slice(None), 0)], ref.at[lead + (slice(None), 1)]
@@ -852,7 +796,8 @@
         self.tile, self.landings, self.sems = tile, landings, sems
         self.bits, self.t_bits = log2(n_dp) - 1, log2(n_t)
         self.stages = 2 + self.bits + self.t_bits
-        self.cols = held.shape[-1]
+        self.cols, self.lanes = cols, slice(first, first + cols)
+        self.lead = (n_t,) + (2,) * self.bits
 
     def remote(self, source, target, slot, dp, z):
         send, recv = self.sems[0], self.sems[1]
@@ -865,8 +810,13 @@
             device_id_type=MESH,
         )
 
+    def at(self, index=()):
+        return index + (slice(None),) * (len(self.lead) - len(index) + 1) + (self.lanes,)
+
     def load(self):
-        return pltpu.make_async_copy(self.keep, self.held, self.sems[2].at[self.index])
+        return pltpu.make_async_copy(
+            self.keep, self.held.at[self.at()], self.sems[2].at[self.index]
+        )
 
     def core(self):
         return self.remote(self.send, self.land, 0, self.me ^ 1, self.z)
@@ -875,8 +825,8 @@
         rest = (slice(None),) * (self.bits - 1 - stage)
         done = (0,) * stage
         if half == 0:
-            return self.held.at[(slice(0, self.n_t // 2),) + rest + (bit,) + done]
-        return self.held.at[(slice(self.n_t // 2, self.n_t),) + done + (bit,) + rest]
+            return self.held.at[self.at((slice(0, self.n_t // 2),) + rest + (bit,) + done)]
+        return self.held.at[self.at((slice(self.n_t // 2, self.n_t),) + done + (bit,) + rest)]
 
     def landing(self, which):
         ref = self.landings[which]
@@ -894,7 +844,7 @@
         )
 
     def column(self, stage, first, count):
-        return self.held.at[(slice(first, first + count),) + (0,) * self.bits]
+        return self.held.at[self.at((slice(first, first + count),) + (0,) * self.bits)]
 
     def along(self, stage):
         count = self.n_t >> (stage + 1)
@@ -938,12 +888,12 @@
                 )
                 self.start(number - 1)
             else:
-                mine = self.held[(0,) * (1 + self.bits)].astype(f32)
+                mine = self.held[self.at((0,) * (1 + self.bits))].astype(f32)
                 got = self.landing(2 * self.bits + stage)[0].astype(f32)
                 self.out[...] = mine + got
 
     def add_land(self):
-        lead = self.held.shape[:-2]
+        lead = self.lead
 
         def at_of(i):
             at = []
@@ -968,7 +918,7 @@
                 fetch(i + 1).start()
 
             fetch(i).wait()
-            at = at_of(i)
+            at = self.at(at_of(i))
             got = self.tile[lax.rem(i, 2), :, pl.ds(0, self.cols)].astype(f32)
             self.held[at] = (self.held[at].astype(f32) + got).astype(bf16)
             return 0
@@ -1010,7 +960,7 @@
             self.hop(r).wait_send()
 
 
-def attention_part(r, group, n_t, z, length, q_ref, do_ref, lse_ref, delta_ref, kv_ref, got_ref, dq_ref, sum_ref):
+def attention_part(r, group, n_t, z, length, q_ref, do_ref, lse_ref, delta_ref, kv_ref, dq_ref, sum_ref):
     rows = q_ref.shape[1]
     groups = lse_ref.shape[0]
     per = group * HEAD_SIZE
@@ -1063,7 +1013,55 @@
             dq_ref[...] = jnp.zeros_like(dq_ref)
 
 
-def scatter_kernel(n_dp, n_t, stacked, group, *refs):
+def back_part(
+    n_dp, n_t, me, z, nq, nk, dq_ref, dkv_ref, cos_ref, sin_ref, n1t_ref, w_hbm, wq_ref, wkv_ref,
+    dn_ref, gbufs, parts, sems
+):
+    width = n1t_ref.shape[0]
+    block = width // n_dp
+    bits = log2(n_dp) - 1
+    step = width // 4
+    cosine, sine = cos_ref[...], sin_ref[...]
+
+    def body(i, _):
+        copies = [
+            pltpu.make_async_copy(w_hbm.at[i, :, 0:nq], wq_ref.at[:, 0:nq], sems.at[0]),
+            pltpu.make_async_copy(w_hbm.at[i, :, nq : nq + 2 * nk], wkv_ref, sems.at[1]),
+        ]
+        for copy in copies:
+            copy.start()
+        q_rows = pl.ds(pl.multiple_of(i * nq, 32), nq)
+        k_rows = pl.ds(pl.multiple_of(i * nk, 32), nk)
+        dq = turn(dq_ref[q_rows, :], cosine, sine, -1.0).astype(bf16).T
+        dk = turn(dkv_ref[0, k_rows, :].astype(f32), cosine, sine, -1.0).astype(bf16)
+        dkv = jnp.concatenate([dk, dkv_ref[1, k_rows, :]], axis=0).T
+        for copy in copies:
+            copy.wait()
+        for c in range(4):
+            part = slice(c * step, (c + 1) * step)
+            dn_ref[:, part] += dot(dq, wq_ref[part, 0:nq], ((1,), (1,))) + dot(
+                dkv, wkv_ref[part, :], ((1,), (1,))
+            )
+            for d, gbuf in ((dq, gbufs[0]), (dkv, gbufs[1])):
+                grad = dot(n1t_ref[part, :], d).astype(bf16)
+                for b in range(step // block):
+                    r = me ^ (c * (step // block) + b)
+                    at = (r & 1,) + tuple((r >> bit) & 1 for bit in range(bits, 0, -1))
+                    gbuf[at] = grad[b * block : (b + 1) * block]
+        stores = [
+            pltpu.make_async_copy(gbufs[k], parts[k].at[i ^ z], sems.at[2 + k]) for k in (0, 1)
+        ]
+        for store in stores:
+            store.start()
+        for store in stores:
+            store.wait()
+        return 0
+
+    dn_ref[...] = jnp.zeros_like(dn_ref)
+    lax.fori_loop(0, n_t, body, 0)
+
+
+def scatter_kernel(n_dp, n_t, stacked, cols, nq, nk, *refs):
     refs = list(refs)
 
     def take(k):
@@ -1071,93 +1069,125 @@
         del refs[:k]
         return out
 
-    attention = group > 0
     grads = []
     for ref, depth in zip(take(len(stacked)), stacked):
         grads += [(ref, (c,)) for c in range(depth)] if depth else [(ref, ())]
-    count = len(grads)
-    if attention:
-        (sc_ref, q_ref, do_ref, lse_ref, delta_ref) = take(5)
-        kvs = take(n_t)
+    early = len(grads)
+    count = early + 2
+    sc_ref, q_hbm, do_hbm, lse_ref, delta_ref = take(5)
+    kvs = take(n_t)
+    cos_ref, sin_ref, n1t_hbm, w_hbm = take(4)
     lands, outs = take(count), take(count)
-    if attention:
-        dq_ref, dkv_ref = take(2)
-    helds = take(count)
+    dn_ref, q_part, kv_part = take(3)
+    grads += [(q_part, ()), (kv_part, ())]
+    helds = take(early)
     (tile,) = take(1)
     landings = take(2 * (log2(n_dp) - 1) + log2(n_t))
     sems = take(4)
+    dq_ref, dkv_ref, q_ref, do_ref, kv_ref, wkv_ref, gbuf_q, gbuf_kv, own_sems = take(9)
+    sums, landed = take(n_t - 1), take(n_t - 1)
+    chain_sems = take(2)
     me, z = lax.axis_index("dp"), lax.axis_index("tensor")
     greet_all(n_dp, n_t, me, z)
+    places = [(held, 0) for held in helds] + [(helds[0], 0), (helds[0], cols[early])]
     works = [
         Scatter(
-            n_dp, n_t, me, z, c, grads[c], lands[c], outs[c], helds[c], tile, landings, sems
+            n_dp, n_t, me, z, c, grads[c], lands[c], outs[c], *places[c], cols[c], tile, landings, sems
         )
         for c in range(count)
     ]
     stages = works[0].stages
 
+    shift = max(0, stages - 1 - early)
+    turns = [c if c < early else c + shift for c in range(count)]
+
     def tick(k):
         for number in range(stages - 1, 0, -1):
-            c = k - (number - 1)
-            if 0 <= c < count:
-                works[c].event(number)
-        if k + 2 < count:
+            if k - (number - 1) in turns:
+                works[turns.index(k - (number - 1))].event(number)
+        if k + 2 < early:
             works[k + 2].event(0)
 
     works[0].event(0)
-    if count > 1:
-        works[1].event(0)
-    ticks = list(range(count + stages - 2))
-    if attention:
-        sums = take(n_t - 1)
-        landed = take(n_t - 1)
-        chain_sems = take(2)
-        length = sc_ref[1]
-        descend = Descend(n_t, me, z, [dkv_ref] + sums, landed, chain_sems)
-        for r in range(n_t - 1, -1, -1):
-            target = dkv_ref if r == 0 else sums[r - 1]
-            attention_part(
-                r, group, n_t, z, length, q_ref, do_ref, lse_ref, delta_ref, kvs[r], None, dq_ref, target
-            )
-            if r < n_t - 1:
-                @pl.when((z + 1 < n_t) & (z >= r))
-                def _():
-                    descend.hop(r + 1).wait_recv()
-                    add_blocks(target, landed[r])
-
-            if r > 0:
-                descend.start(r)
-            tick(ticks.pop(0))
+    works[1].event(0)
+    loads = [
+        pltpu.make_async_copy(q_hbm, q_ref, own_sems.at[0]),
+        pltpu.make_async_copy(do_hbm, do_ref, own_sems.at[1]),
+    ]
+    for load in loads:
+        load.start()
+    for load in loads:
+        load.wait()
+    ticks = list(range(count + shift + stages - 2))
+    length = sc_ref[1]
+    descend = Descend(n_t, me, z, [dkv_ref] + sums, landed, chain_sems)
+    for r in range(n_t - 1, -1, -1):
+        target = dkv_ref if r == 0 else sums[r - 1]
+        fetch = pltpu.make_async_copy(kvs[r], kv_ref, own_sems.at[2])
+        fetch.start()
+        fetch.wait()
+        attention_part(
+            r, nq // nk, n_t, z, length, q_ref, do_ref, lse_ref, delta_ref, kv_ref, dq_ref, target
+        )
+        if r < n_t - 1:
+            @pl.when((z + 1 < n_t) & (z >= r))
+            def _():
+                descend.hop(r + 1).wait_recv()
+                add_blocks(target, landed[r])
+
+        if r > 0:
+            descend.start(r)
+        tick(ticks.pop(0))
+    fetch = pltpu.make_async_copy(n1t_hbm, do_ref, own_sems.at[3])
+    fetch.start()
+    fetch.wait()
+    back_part(
+        n_dp, n_t, me, z, nq, nk, dq_ref, dkv_ref, cos_ref, sin_ref, do_ref, w_hbm, q_ref, wkv_ref,
+        dn_ref, (gbuf_q, gbuf_kv), (q_part, kv_part), own_sems
+    )
+    while ticks[0] < stages - 1:
+        tick(ticks.pop(0))
+    works[0].finish()
+    works[early].event(0)
+    works[early + 1].event(0)
     for k in ticks:
         tick(k)
-    for work in works:
+    for work in works[1:]:
         work.finish()
-    if attention:
-        for r in range(1, n_t):
-            descend.finish(r)
-
-
-def scatter(grads, n_dp, n_t, collective_id, attention=None):
+    for r in range(1, n_t):
+        descend.finish(r)
+
+
+def scatter(grads, n_dp, n_t, collective_id, attention, back):
     bits = log2(n_dp) - 1
     block = grads[0].shape[-2]
     widest = max(k.shape[-1] for k in grads)
     stacked = [k.shape[0] if k.ndim == 5 else 0 for k in grads]
-    shapes = []
+    sc, q, do, lse, delta, kvs = attention
+    cosine, sine, n1t, w, nq, nk = back
+    cols = []
     for k, depth in zip(grads, stacked):
-        shapes += [(n_t,) + (2,) * bits + (block, k.shape[-1])] * max(depth, 1)
-    count = len(shapes)
+        cols += [k.shape[-1]] * max(depth, 1)
+    early = len(cols)
+    cols += [nq, 2 * nk]
+    shapes = [(n_t,) + (2,) * bits + (block, c) for c in cols]
     args = [
         k.reshape(k.shape[: k.ndim - 3] + (2,) * (bits + 1) + k.shape[-2:]) for k in grads
     ]
     anywhere = pl.BlockSpec(memory_space=pl.ANY)
     vmem = pl.BlockSpec(memory_space=pltpu.VMEM)
     smem = pl.BlockSpec(memory_space=pltpu.SMEM)
-    in_specs = [anywhere] * len(args)
+    in_specs = [anywhere] * len(args) + [smem, anywhere, anywhere, vmem, vmem] + [anywhere] * n_t
+    in_specs += [vmem, vmem, anywhere, anywhere]
+    args += [sc, q, do, lse, delta] + list(kvs) + [cosine, sine, n1t, w]
+    wide = [(2,) * (bits + 1) + (block, c) for c in cols[early:]]
     out_shape = [jax.ShapeDtypeStruct(s, bf16) for s in shapes] + [
-        jax.ShapeDtypeStruct((block, s[-1]), f32) for s in shapes
+        jax.ShapeDtypeStruct((block, c), f32) for c in cols
     ]
-    out_specs = [anywhere] * count + [vmem] * count
-    scratch = [pltpu.VMEM(s, bf16) for s in shapes]
+    out_shape.append(jax.ShapeDtypeStruct((n1t.shape[1], n1t.shape[0]), f32))
+    out_shape += [jax.ShapeDtypeStruct((n_t,) + s, bf16) for s in wide]
+    out_specs = [anywhere] * len(cols) + [vmem] * (len(cols) + 1) + [anywhere] * 2
+    scratch = [pltpu.VMEM(s, bf16) for s in shapes[:early]]
     scratch.append(pltpu.VMEM((2, block, widest), bf16))
     for stage in range(bits):
         for _ in (0, 1):
@@ -1168,33 +1198,34 @@
         scratch.append(pltpu.VMEM((2, n_t >> (stage + 1), block, widest), bf16))
     copies = 1 + 2 * bits + log2(n_t)
     scratch += [
-        pltpu.SemaphoreType.DMA((count, copies)),
-        pltpu.SemaphoreType.DMA((count, copies)),
-        pltpu.SemaphoreType.DMA((count,)),
+        pltpu.SemaphoreType.DMA((len(cols), copies)),
+        pltpu.SemaphoreType.DMA((len(cols), copies)),
+        pltpu.SemaphoreType.DMA((len(cols),)),
         pltpu.SemaphoreType.DMA((2,)),
+        pltpu.VMEM(q.shape, f32),
+        pltpu.VMEM(kvs[0].shape, bf16),
+        pltpu.VMEM(q.shape, bf16),
+        pltpu.VMEM(do.shape, bf16),
+        pltpu.VMEM(kvs[0].shape, bf16),
+        pltpu.VMEM((n1t.shape[0], 2 * nk), bf16),
+        pltpu.VMEM(wide[0], bf16),
+        pltpu.VMEM(wide[1], bf16),
+        pltpu.SemaphoreType.DMA((4,)),
     ]
-    group = 0
-    if attention is not None:
-        sc, q, do, lse, delta, kvs = attention
-        args += [sc, q, do, lse, delta] + list(kvs)
-        in_specs += [smem] + [vmem] * (4 + n_t)
-        group = q.shape[0] // kvs[0].shape[1]
-        out_shape += [jax.ShapeDtypeStruct(q.shape, f32), jax.ShapeDtypeStruct(kvs[0].shape, bf16)]
-        out_specs += [vmem, vmem]
-        scratch += [pltpu.VMEM(kvs[0].shape, bf16)] * (2 * (n_t - 1))
-        scratch += [pltpu.SemaphoreType.DMA((n_t,))] * 2
+    scratch += [pltpu.VMEM(kvs[0].shape, bf16)] * (2 * (n_t - 1))
+    scratch += [pltpu.SemaphoreType.DMA((n_t,))] * 2
     outs = pl.pallas_call(
-        functools.partial(scatter_kernel, n_dp, n_t, stacked, group),
+        functools.partial(scatter_kernel, n_dp, n_t, stacked, cols, nq, nk),
         in_specs=in_specs,
         out_specs=out_specs,
         out_shape=out_shape,
         scratch_shapes=scratch,
         compiler_params=pltpu.CompilerParams(
-            collective_id=collective_id, has_side_effects=True, vmem_limit_bytes=62 * 1024 * 1024
+            collective_id=collective_id, has_side_effects=True, vmem_limit_bytes=63 * 1024 * 1024
         ),
         name="scatter_grads",
     )(*args)
-    return outs[count:]
+    return outs[len(cols) : 2 * len(cols) + 1]
 
 
 def local(
@@ -1292,18 +1323,14 @@
     groups, _, lanes = lse.shape
     delta = (d_att.astype(f32) * att.astype(f32)).reshape(groups, -1, HEAD_SIZE, rows).sum(axis=2)
     delta = delta.reshape(groups, 1, lanes)
-    *grads, out_share, d_q, d_kv = scatter(
+    *grads, out_share, q_share, kv_share, d_n1 = scatter(
         shares,
         n_dp,
         n_t,
         2,
         (sc, q, d_att, lse, delta, kvs),
+        (cosine, sine, n1.T, w_qkv, nq, nk),
     )
-    n1t = n1.T
-    d_n1, q_part, kv_part = qkv_back(
-        me, d_q.reshape(n_t, nq, rows), d_kv, cosine, sine, n1t, w_qkv, nq, nk, n_dp
-    )
-    q_share, kv_share = scatter([q_part, kv_part], n_dp, n_t, 3)
 
     scaled = d_n1 * gain_one
     inner = jnp.mean(scaled * x, axis=1, keepdims=True)

time: 906 us -> 840 us (0.927)
  Pallas kernels: 801 us -> 735 us
    pallas_call x3 -> x1, Pallas kernels: 357 us -> 291 us  [scatter(): pl.pallas_call(functools.partial(scatter_kernel, n_dp, n_t, stacked, cols...]
  transfers between devices with their start and end apart: 5 -> 5, of which waited for: 2 -> 3; matrix products, arithmetic and copies ran while one was open for 3% -> 3% of each run, Pallas kernels for 9% -> 0%
where the time goes in v4:
time: 840 us; the launch traced here: 831 us
  Pallas kernels  735 us (88%)
  other arithmetic  42.5 us (5%)
  local copies, waits for them, and re-layouts  38.8 us (5%)
  starting transfers between devices  8.89 us (1%)
    pallas_call x1, Pallas kernels, scatter(): pl.pallas_call(functools.partial(scatter_kernel, n_dp, n_t, stacked, cols...  291 us
    pallas_call x2, Pallas kernels, gather(): pl.pallas_call(functools.partial(gather_kernel, n_dp, n_t, count, merged,...  274 us
    pallas_call x1, Pallas kernels, mlp_gather(): pl.pallas_call(functools.partial(mlp_gather_kernel, n_dp, n_t, tile), gri...  115 us
    pallas_call x1, Pallas kernels, mlp(): pl.pallas_call(functools.partial(mlp_kernel, tile, first), grid_spec=pltp...  24.9 us
  transfers between devices with their start and end apart: 5, of which 3 were waited for; matrix products, arithmetic and copies ran while one was open for 3% of the time, Pallas kernels for 0%

profile of v4, /device:TPU:0, one launch (start us, length us, event | category | flops | bytes accessed | tf_op | source)
XLA Modules:
  0.0 830.8 jit_solution(12264610211948546669)
XLA Ops:
  5.1 76.9 %gather_weights.2 = bf16[4,8,192,896]{3,2,1,0:T(8,128)(2,1)} custom-call(bf16[192,896]{1,0:T(8,128)(2,1)} %fusion.12.refs_0_), custom_call_target="tpu_custom_call" | custom-call | tf_op jit(solution)/shard_map/gather_weights/pallas_call | solution.py:659
  87.8 10.0 %qkv_project.1 = (bf16[4,384,512]{2,1,0:T(8,128)(2,1)}, bf16[2,768,512]{2,1,0:T(8,128)(2,1)}) custom-call(bf16[512,1536]{1,0:T(8,128)(2,1)} %copy.69.n1_ref, bf16[4,1536,896]{2,1,0:T(8,128)(2,1)} %bitcast.44, f32[48,512]{1,0:T(8,128)} %get-tuple-element.139.cos_ref.refs_12_, f32[48,512]{1,0:T(8,128)} %get-tuple-element.138.sin_ref.refs_13_), custom_call_target="tpu_custom_call" | custom-call | flops 5637144576 | bytes 17301504 | tf_op jit(solution)/shard_map/qkv_project/pallas_call | solution.py:73
  99.4 197.2 %gather_weights.3 = (bf16[4,8,192,384]{3,2,1,0:T(8,128)(2,1)}, bf16[4,8,192,2304]{3,2,1,0:T(8,128)(2,1)}, bf16[2,768,512]{2,1,0:T(8,128)(2,1)}, bf16[2,768,512]{...) custom-call(bf16[192,384]{1,0:T(8,128)(2,1)} %bitcast.61, ...), custom_call_target="tpu_custom_call" | custom-call | tf_op jit(solution)/shard_map/gather_weights/pallas_call | solution.py:659
  296.6 8.4 %out_project.1 = f32[512,1536]{1,0:T(8,128)} custom-call(bf16[4,384,512]{2,1,0:T(8,128)(2,1)} %bitcast.51, bf16[4,1536,384]{2,1,0:T(8,128)(2,1)} %bitcast.57, bf16[512,1536]{1,0:T(8,128)(2,1)} %x_ref.1), custom_call_target="tpu_custom_call" | custom-call | flops 2415919104 | bytes 11010048 | tf_op jit(solution)/shard_map/out_project/pallas_call | solution.py:109
  305.0 2.4 copy.76
  307.4 3.3 multiply_reduce_fusion.2
  313.7 2.6 copy.71
  316.4 3.0 fusion.9
  322.5 2.6 copy.74.n2_ref
  325.1 2.6 copy.75.g_ref
  328.3 114.9 %mlp_gather.1 = (f32[512,1536]{1,0:T(8,128)}, f32[512,1536]{1,0:T(8,128)}, bf16[3,4,8,192,768]{4,3,2,1,0:T(8,128)(2,1)}, bf16[4,8,192,768]{3,2,1,0:T(8,128)(2,1)}) custom-call(bf16[512,1536]{1,0:T(8,128)(2,1)} %copy.74.n2_ref, bf16[1536,512]{1,0:T(8,128)(2,1)} %fusion.35.n2t_ref, bf16[512,1536]{1,0:T(8,128)(2,1)} %copy.75.g_ref, ...), custom_call_target="tpu_custom_call" | custom-call | tf_op jit(solution)/shard_map/mlp_gather/pallas_call | solution.py:718
  443.2 24.9 %mlp.1 = (f32[512,1536]{1,0:T(8,128)}, f32[512,1536]{1,0:T(8,128)}, bf16[4,8,192,768]{3,2,1,0:T(8,128)(2,1)}) custom-call(s32[2]{0:T(128)} %get-tuple-element.146.me_ref, bf16[512,1536]{1,0:T(8,128)(2,1)} %copy.74.n2_ref, bf16[1536,512]{1,0:T(8,128)(2,1)} %fusion.35.n2t_ref, ...), custom_call_target="tpu_custom_call", output_to_operand_aliasing={{0}: (6, {}), {1}: (7, {})} | custom-call | flops 14495514624 | bytes 37748736 | tf_op jit(solution)/shard_map/mlp/pallas_call | solution.py:231
  468.0 3.6 copy.78
  471.6 2.9 multiply_reduce_fusion
  476.9 2.6 copy.81.dh_ref
  479.5 11.7 %out_back.1 = (bf16[4,384,512]{2,1,0:T(8,128)(2,1)}, bf16[4,8,192,384]{3,2,1,0:T(8,128)(2,1)}) custom-call(s32[2]{0:T(128)} %get-tuple-element.146.me_ref, bf16[512,1536]{1,0:T(8,128)(2,1)} %copy.81.dh_ref, bf16[1536,512]{1,0:T(8,128)(2,1)} %bitcast.50, bf16[4,384,512]{2,1,0:T(8,128)(2,1)} %bitcast.52, bf16[4,1536,384]{2,1,0:T(8,128)(2,1)} %bitcast.58), custom_call_target="tpu_custom_call" | custom-call | flops 4831838208 | bytes 15728640 | tf_op jit(solution)/shard_map/out_back/pallas_call | solution.py:135
  494.2 290.7 %scatter_grads.1 = (bf16[4,2,2,192,768]{4,3,2,1,0:T(8,128)(2,1)}, bf16[4,2,2,192,768]{4,3,2,1,0:T(8,128)(2,1)}, bf16[4,2,2,192,768]{4,3,2,1,0:T(8,128)(2,1)}, bf...) custom-call(bf16[3,4,2,2,2,192,768]{6,5,4,3,2,1,0:T(8,128)(2,1)} %bi, ...), custom_call_target="tpu_custom_call" | custom-call | tf_op jit(solution)/shard_map/scatter_grads/pallas_call | solution.py:1217
  784.8 3.6 copy.82
  788.5 3.1 fusion.8
  797.1 3.7 copy.77
  800.9 6.8 fusion.6
  808.8 4.1 collective-permute-start.1
  819.0 2.6 collective-permute-done.3
  821.6 2.9 collective-permute-start.4
  (153 shorter events, 42.0 us)
Async XLA Ops:
  2.9 80.9 %copy-start.2 = (bf16[512,1536]{0,1:T(8,128)(2,1)}, bf16[512,1536]{0,1:T(8,128)(2,1)S(1)}, u32[]{:S(2)}) copy-start(bf16[512,1536]{0,1:T(8,128)(2,1)S(1)} %copy.67) | copy-start | bytes 4718596
  5.1 78.7 %copy-start.31 = (f32[512]{0:T(512)S(1)}, f32[512]{0:T(512)}, u32[]{:S(2)}) copy-start(f32[512]{0:T(512)} %add_rsqrt_fusion.1) | copy-start | bytes 6148
  307.4 167.1 %copy-start = (f32[512,1536]{0,1:T(8,128)}, f32[512,1536]{0,1:T(8,128)S(1)}, u32[]{:S(2)}) copy-start(f32[512,1536]{0,1:T(8,128)S(1)} %copy.76) | copy-start | bytes 9437188
  310.7 163.8 %copy-start.30 = (f32[512]{0:T(512)}, f32[512]{0:T(512)S(1)}, u32[]{:S(2)}) copy-start(f32[512]{0:T(512)S(1)} %add_rsqrt_fusion) | copy-start | bytes 6148
  313.7 160.8 %copy-start.33 = (f32[512]{0:T(512)}, f32[512]{0:T(512)S(1)}, u32[]{:S(2)}) copy-start(f32[512]{0:T(512)S(1)} %fusion.26) | copy-start | bytes 6148
  479.5 11.7 %copy-start.8 = (bf16[1536,512]{1,0:T(8,128)(2,1)S(1)}, bf16[1536,512]{1,0:T(8,128)(2,1)}, u32[]{:S(2)}) copy-start(bf16[1536,512]{1,0:T(8,128)(2,1)} %get-tuple-element.39) | copy-start | bytes 4718596
  788.5 7.2 copy-start.19
  788.5 8.0 copy-start.35
  793.0 14.8 %collective-permute-start = (f32[4,2,192]{2,1,0:T(2,128)}, f32[4,2,192]{2,1,0:T(2,128)}, u32[]{:S(2)}, u32[]{:S(2)}) collective-permute-start(f32[4,2,192]{2,1,0:T(2,128)} %pad_maximum_fusion.7), channel_id=1, source_target_pairs={{0,4},{4,0},{8,12},{12,8},{16,20},{20,16},{24,28},{28,24},{1,5},{5... | collective-permute-start | bytes 18440 | tf_op jit(solution)/shard_map/ppermute | solution.py:278
  800.8 7.0 copy-start.38
  800.9 12.0 %copy-start.21 = (f32[192,384]{1,0:T(8,128)S(1)}, f32[192,384]{1,0:T(8,128)}, u32[]{:S(2)}) copy-start(f32[192,384]{1,0:T(8,128)} %get-tuple-element.57) | copy-start | bytes 884740
  800.9 15.5 %copy-start.15 = (f32[256,192]{0,1:T(8,128)S(1)}, f32[256,192]{0,1:T(8,128)}, u32[]{:S(2)}) copy-start(f32[256,192]{0,1:T(8,128)} %get-tuple-element.104) | copy-start | bytes 589828
  800.9 15.5 %copy-start.16 = (f32[256,192]{0,1:T(8,128)S(1)}, f32[256,192]{0,1:T(8,128)}, u32[]{:S(2)}) copy-start(f32[256,192]{0,1:T(8,128)} %get-tuple-element.107) | copy-start | bytes 589828
  800.9 15.5 %copy-start.17 = (f32[256,192]{0,1:T(8,128)S(1)}, f32[256,192]{0,1:T(8,128)}, u32[]{:S(2)}) copy-start(f32[256,192]{0,1:T(8,128)} %get-tuple-element.110) | copy-start | bytes 589828
  807.7 10.3 %copy-start.12 = (f32[192,256]{1,0:T(8,128)S(1)}, f32[192,256]{1,0:T(8,128)}, u32[]{:S(2)}) copy-start(f32[192,256]{1,0:T(8,128)} %get-tuple-element.105) | copy-start | bytes 589828
  807.7 10.3 %copy-start.13 = (f32[192,256]{1,0:T(8,128)S(1)}, f32[192,256]{1,0:T(8,128)}, u32[]{:S(2)}) copy-start(f32[192,256]{1,0:T(8,128)} %get-tuple-element.108) | copy-start | bytes 589828
  807.7 10.3 %copy-start.14 = (f32[192,256]{1,0:T(8,128)S(1)}, f32[192,256]{1,0:T(8,128)}, u32[]{:S(2)}) copy-start(f32[192,256]{1,0:T(8,128)} %get-tuple-element.111) | copy-start | bytes 589828
  807.7 16.8 %copy-start.11 = (f32[192,256]{1,0:T(8,128)S(1)}, f32[192,256]{1,0:T(8,128)}, u32[]{:S(2)}) copy-start(f32[192,256]{1,0:T(8,128)} %get-tuple-element.112) | copy-start | bytes 589828
  807.8 17.7 %copy-start.10 = (bf16[512,1536]{0,1:T(8,128)(2,1)S(1)}, bf16[512,1536]{0,1:T(8,128)(2,1)}, u32[]{:S(2)}) copy-start(bf16[512,1536]{0,1:T(8,128)(2,1)} %get-tuple-element.103) | copy-start | bytes 4718596
  808.8 5.6 collective-permute-start.1
  814.4 3.6 collective-permute-start.2
  818.0 3.6 collective-permute-start.3
  818.0 9.0 %copy-start.9 = (bf16[512,1536]{0,1:T(8,128)(2,1)S(1)}, bf16[512,1536]{0,1:T(8,128)(2,1)}, u32[]{:S(2)}) copy-start(bf16[512,1536]{0,1:T(8,128)(2,1)} %get-tuple-element.102) | copy-start | bytes 4718596
  821.6 7.0 collective-permute-start.4
  (25 other events, 94.9 us)

commit v5 on v4

--- a/solution.py
+++ b/solution.py
@@ -58,7 +58,11 @@
     return jnp.concatenate(parts, axis=0)
 
 
-def qkv_kernel(nq, nk, n1_ref, w_ref, cos_ref, sin_ref, q_ref, kv_ref):
+def qkv_kernel(nq, nk, n1_ref, w_ref, cos_ref, sin_ref, q_ref, kv_ref, n1t_ref):
+    @pl.when(pl.program_id(0) == 0)
+    def _():
+        n1t_ref[...] = n1_ref[...].T
+
     w = w_ref[0, :, : nq + 2 * nk]
     y = dot(n1_ref[...], w).T
     cosine, sine = cos_ref[...], sin_ref[...]
@@ -82,10 +86,12 @@
         out_specs=[
             pl.BlockSpec((1, nq, rows), lambda z: (z, 0, 0)),
             pl.BlockSpec((2, nk, rows), lambda z: (0, z, 0)),
+            pl.BlockSpec((width, rows), lambda z: (0, 0)),
         ],
         out_shape=[
             jax.ShapeDtypeStruct((zs, nq, rows), bf16),
             jax.ShapeDtypeStruct((2, zs * nk, rows), bf16),
+            jax.ShapeDtypeStruct((width, rows), bf16),
         ],
         compiler_params=params("arbitrary"),
         cost_estimate=cost(2 * rows * width * cols * zs, 2 * zs * width * cols + 8 * rows * width),
@@ -122,13 +128,17 @@
     )(att, w, x)
 
 
-def out_back_kernel(me_ref, dh_ref, dht_ref, att_ref, w_ref, da_ref, grad_ref):
+def out_back_kernel(me_ref, dh_ref, att_ref, w_ref, da_ref, grad_ref, dht_ref):
+    @pl.when(pl.program_id(0) == 0)
+    def _():
+        dht_ref[...] = dh_ref[...].T
+
     w = w_ref[0]
     da_ref[0] = dot(dh_ref[...], w).T.astype(bf16)
     place(grad_ref, me_ref[1], dot(dht_ref[...], att_ref[0].T).astype(bf16))
 
 
-def out_back(me, dh, dht, att, w, no, col, n_dp):
+def out_back(me, dh, att, w, no, col, n_dp):
     zs, _, rows = att.shape
     width = dh.shape[1]
     block = width // n_dp
@@ -139,7 +149,6 @@
             grid=(zs,),
             in_specs=[
                 pl.BlockSpec((rows, width), lambda z, m: (0, 0)),
-                pl.BlockSpec((width, rows), lambda z, m: (0, 0)),
                 pl.BlockSpec((1, no, rows), lambda z, m: (z, 0, 0)),
                 pl.BlockSpec((1, width, no), lambda z, m: (z, 0, col)),
             ],
@@ -147,6 +156,7 @@
                 pl.BlockSpec((1, no, rows), lambda z, m: (z, 0, 0)),
                 pl.BlockSpec((1, n_dp, block, no), lambda z, m: (z ^ m[0], 0, 0, 0)),
             ],
+            scratch_shapes=[pltpu.VMEM((width, rows), bf16)],
         ),
         out_shape=[
             jax.ShapeDtypeStruct((zs, no, rows), bf16),
@@ -155,7 +165,7 @@
         compiler_params=params("arbitrary"),
         cost_estimate=cost(4 * rows * width * no * zs, 4 * zs * width * no + 8 * rows * width),
         name="out_back",
-    )(me, dh, dht, att, w)
+    )(me, dh, att, w)
 
 
 def key_mask(s, key_first, query_first, length, rows, diagonal):
@@ -670,8 +680,8 @@
 
 
 def mlp_gather_kernel(
-    n_dp, n_t, tile, n2_ref, n2t_ref, g_ref, gt_ref, w_ref, shard_ref,
-    out_ref, dn_ref, grad_ref, whole_ref, *sems
+    n_dp, n_t, tile, n2_ref, g_ref, w_ref, shard_ref,
+    out_ref, dn_ref, n2t_ref, gt_ref, grad_ref, whole_ref, *sems
 ):
     me, z = lax.axis_index("dp"), lax.axis_index("tensor")
     step = pl.program_id(0) * pl.num_programs(1) + pl.program_id(1)
@@ -683,6 +693,8 @@
     def _():
         neighbours(n_dp, n_t, me, z)
         work.send_own()
+        n2t_ref[...] = n2_ref[...].T
+        gt_ref[...] = g_ref[...].T
         out_ref[...] = jnp.zeros_like(out_ref)
         dn_ref[...] = jnp.zeros_like(dn_ref)
 
@@ -708,7 +720,7 @@
             work.finish(k)
 
 
-def mlp_gather(n2, n2t, g, gt, w, shard, tile, n_dp, n_t, collective_id):
+def mlp_gather(n2, g, w, shard, tile, n_dp, n_t, collective_id):
     rows, width = n2.shape
     block = width // n_dp
     full = pl.BlockSpec((rows, width), lambda c, i: (0, 0))
@@ -720,15 +732,15 @@
         grid=(MERGED, n_t),
         in_specs=[
             full,
-            full_t,
             full,
-            full_t,
             pl.BlockSpec((1, width, cols), lambda c, i: (i, 0, c)),
             anywhere,
         ],
         out_specs=[
             full,
             full,
+            full_t,
+            full_t,
             pl.BlockSpec(
                 (1, 1, n_dp, block, cols),
                 lambda c, i: (c, i ^ lax.axis_index("tensor"), 0, 0, 0),
@@ -738,6 +750,8 @@
         out_shape=[
             jax.ShapeDtypeStruct((rows, width), f32),
             jax.ShapeDtypeStruct((rows, width), f32),
+            jax.ShapeDtypeStruct((width, rows), bf16),
+            jax.ShapeDtypeStruct((width, rows), bf16),
             jax.ShapeDtypeStruct((MERGED, n_t, n_dp, block, cols), bf16),
             jax.ShapeDtypeStruct((n_t, n_dp, block, cols), bf16),
         ],
@@ -755,7 +769,7 @@
             vmem_limit_bytes=VMEM_LIMIT,
         ),
         name="mlp_gather",
-    )(n2, n2t, g, gt, w, shard)
+    )(n2, g, w, shard)
 
 
 def greet_all(n_dp, n_t, me, z):
@@ -1280,9 +1294,8 @@
     inv_one = lax.rsqrt(jnp.mean(x * x, axis=1, keepdims=True) + eps_norm)
     g32 = cotangent.astype(f32) * live
     g = g32.astype(bf16)
-    gt = g.T
     n1 = (x * inv_one * gain_one).astype(bf16)
-    q, kv = qkv_project(n1, w_qkv, cosine, sine, nq, nk)
+    q, kv, n1t = qkv_project(n1, w_qkv, cosine, sine, nq, nk)
     q = q.reshape(n_t * nq, rows)
 
     w_out, w_mlp, *above, att, lse = gather(
@@ -1296,9 +1309,8 @@
 
     inv_two = lax.rsqrt(jnp.mean(h_one * h_one, axis=1, keepdims=True) + eps_norm)
     n2 = (h_one * inv_two * gain_two).astype(bf16)
-    n2t = n2.T
-    out_sum, dn_sum, share, w_last = mlp_gather(
-        n2, n2t, g, gt, w_mlp, shard_mlp[MERGED], tile, n_dp, n_t, 4
+    out_sum, dn_sum, n2t, gt, share, w_last = mlp_gather(
+        n2, g, w_mlp, shard_mlp[MERGED], tile, n_dp, n_t, 4
     )
     w_last = w_last.reshape(n_t, width, 3 * tile)
     shares = [share]
@@ -1315,8 +1327,7 @@
     gain_two_part = jnp.sum(d_n2 * h_one * inv_two, axis=0)
     d_h = g32 + inv_two * scaled - h_one * (inv_two * inv_two * inv_two * inner)
     d_h_low = d_h.astype(bf16)
-    d_h_t = d_h_low.T
-    d_att, share = out_back(me, d_h_low, d_h_t, att_z, w_out, no, 0, n_dp)
+    d_att, share = out_back(me, d_h_low, att_z, w_out, no, 0, n_dp)
     shares.append(share)
 
     d_att = d_att.reshape(n_t * no, rows)
@@ -1329,7 +1340,7 @@
         n_t,
         2,
         (sc, q, d_att, lse, delta, kvs),
-        (cosine, sine, n1.T, w_qkv, nq, nk),
+        (cosine, sine, n1t, w_qkv, nq, nk),
     )
 
     scaled = d_n1 * gain_one

time: 840 us -> 805 us (0.958)
  local copies, waits for them, and re-layouts: 38.8 us -> 11.7 us
  other arithmetic: 42.5 us -> 32.5 us
    pallas_call x4 -> x0, local copies, waits for them, and re-layouts: 13.3 us -> none  [the longest x2 7.24 us: mlp(): pl.pallas_call(functools.partial(mlp_kernel, tile, first), grid_spec=pltp...]
    convert_element_type x4 -> x0, local copies, waits for them, and re-layouts: 9.35 us -> none  [the longest x1 2.62 us: local(): n2 = (h_one * inv_two * gain_two).astype(bf16)]
  transfers between devices with their start and end apart: 5 -> 5, of which waited for: 3 -> 4; matrix products, arithmetic and copies ran while one was open for 3% -> 1% of each run, Pallas kernels for 0% -> 0%
where the time goes in v5:
time: 805 us; the launch traced here: 796 us
  Pallas kernels  737 us (92%)
  other arithmetic  32.5 us (4%)
  local copies, waits for them, and re-layouts  11.7 us (1%)
    pallas_call x1, Pallas kernels, scatter(): pl.pallas_call(functools.partial(scatter_kernel, n_dp, n_t, stacked, cols...  292 us
    pallas_call x2, Pallas kernels, gather(): pl.pallas_call(functools.partial(gather_kernel, n_dp, n_t, count, merged,...  274 us
    pallas_call x1, Pallas kernels, mlp_gather(): pl.pallas_call(functools.partial(mlp_gather_kernel, n_dp, n_t, tile), gri...  115 us
    pallas_call x1, Pallas kernels, mlp(): pl.pallas_call(functools.partial(mlp_kernel, tile, first), grid_spec=pltp...  24.6 us
  transfers between devices with their start and end apart: 5, of which 4 were waited for; matrix products, arithmetic and copies ran while one was open for 1% of the time, Pallas kernels for 0%

profile of v5, /device:TPU:0, one launch (start us, length us, event | category | flops | bytes accessed | tf_op | source)
XLA Modules:
  0.0 795.9 jit_solution(10025773124383048208)
XLA Ops:
  5.4 1.9 fusion.12.refs_0_
  7.3 76.9 %gather_weights.2 = bf16[4,8,192,896]{3,2,1,0:T(8,128)(2,1)} custom-call(bf16[192,896]{1,0:T(8,128)(2,1)} %fusion.12.refs_0_), custom_call_target="tpu_custom_call" | custom-call | tf_op jit(solution)/shard_map/gather_weights/pallas_call | solution.py:669
  84.2 1.2 fusion.11
  87.1 1.6 fusion.2.n1_ref
  89.8 11.0 %qkv_project.1 = (bf16[4,384,512]{2,1,0:T(8,128)(2,1)}, bf16[2,768,512]{2,1,0:T(8,128)(2,1)}, bf16[1536,512]{1,0:T(8,128)(2,1)}) custom-call(bf16[512,1536]{1,0:T(8,128)(2,1)} %fusion.2.n1_ref, bf16[4,1536,896]{2,1,0:T(8,128)(2,1)} %bitcast.37, f32[48,512]{1,0:T(8,128)} %get-tuple-element.113.cos_ref.refs_12_, f32[48,512]{1,0:T(8,128)} %get-tuple-element.112.sin_ref.refs_13_), custom_call_target="tpu_custom_call" | custom-call | flops 5637144576 | bytes 17301504 | tf_op jit(solution)/shard_map/qkv_project/pallas_call | solution.py:77
  102.5 197.2 %gather_weights.3 = (bf16[4,8,192,384]{3,2,1,0:T(8,128)(2,1)}, bf16[4,8,192,2304]{3,2,1,0:T(8,128)(2,1)}, bf16[2,768,512]{2,1,0:T(8,128)(2,1)}, bf16[2,768,512]{...) custom-call(bf16[192,384]{1,0:T(8,128)(2,1)} %bitcast.53, ...), custom_call_target="tpu_custom_call" | custom-call | tf_op jit(solution)/shard_map/gather_weights/pallas_call | solution.py:669
  299.6 8.3 %out_project.1 = f32[512,1536]{1,0:T(8,128)} custom-call(bf16[4,384,512]{2,1,0:T(8,128)(2,1)} %bitcast.43, bf16[4,1536,384]{2,1,0:T(8,128)(2,1)} %bitcast.49, bf16[512,1536]{1,0:T(8,128)(2,1)} %x_ref.1), custom_call_target="tpu_custom_call" | custom-call | flops 2415919104 | bytes 11010048 | tf_op jit(solution)/shard_map/out_project/pallas_call | solution.py:115
  308.0 2.3 multiply_reduce_fusion.2
  310.9 1.5 multiply_convert_fusion.1.n2_ref
  312.4 1.5 fusion.9.g_ref
  313.9 114.9 %mlp_gather.1 = (f32[512,1536]{1,0:T(8,128)}, f32[512,1536]{1,0:T(8,128)}, bf16[1536,512]{1,0:T(8,128)(2,1)}, bf16[1536,512]{1,0:T(8,128)(2,1)}, bf16[3,4,8,192,...) custom-call(bf16[512,1536]{1,0:T(8,128)(2,1)} %multiply_convert_fusion.1.n2_ref, bf16[512,1536]{1,0:T(8,128)(2,1)} %fusion.9.g_ref, ...), custom_call_target="tpu_custom_call" | custom-call | tf_op jit(solution)/shard_map/mlp_gather/pallas_call | solution.py:730
  428.7 24.6 %mlp.1 = (f32[512,1536]{1,0:T(8,128)}, f32[512,1536]{1,0:T(8,128)}, bf16[4,8,192,768]{3,2,1,0:T(8,128)(2,1)}) custom-call(s32[2]{0:T(128)} %get-tuple-element.120.me_ref, bf16[512,1536]{1,0:T(8,128)(2,1)} %multiply_convert_fusion.1.n2_ref, bf16[1536,512]{1,0:T(8,128)(2,1)} %get-tuple-element.45.n2t_ref, ...), custom_call_target="tpu_custom_call", output_to_operand_aliasing={{0}: (6, {}), {1}: (7, {})} | custom-call | flops 14495514624 | bytes 37748736 | tf_op jit(solution)/shard_map/mlp/pallas_call | solution.py:241
  453.4 2.8 multiply_reduce_fusion
  457.1 3.3 fusion.27
  460.5 11.6 %out_back.1 = (bf16[4,384,512]{2,1,0:T(8,128)(2,1)}, bf16[4,8,192,384]{3,2,1,0:T(8,128)(2,1)}) custom-call(s32[2]{0:T(128)} %get-tuple-element.120.me_ref, bf16[512,1536]{1,0:T(8,128)(2,1)} %get-tuple-element.75.dh_ref, bf16[4,384,512]{2,1,0:T(8,128)(2,1)} %bitcast.44, bf16[4,1536,384]{2,1,0:T(8,128)(2,1)} %bitcast.50), custom_call_target="tpu_custom_call" | custom-call | flops 4831838208 | bytes 15728640 | tf_op jit(solution)/shard_map/out_back/pallas_call | solution.py:145
  472.1 1.9 convert_multiply_fusion.5
  475.1 292.4 %scatter_grads.1 = (bf16[4,2,2,192,768]{4,3,2,1,0:T(8,128)(2,1)}, bf16[4,2,2,192,768]{4,3,2,1,0:T(8,128)(2,1)}, bf16[4,2,2,192,768]{4,3,2,1,0:T(8,128)(2,1)}, bf...) custom-call(bf16[3,4,2,2,2,192,768]{6,5,4,3,2,1,0:T(8,128)(2,1)} %bi, ...), custom_call_target="tpu_custom_call" | custom-call | tf_op jit(solution)/shard_map/scatter_grads/pallas_call | solution.py:1231
  767.5 3.5 fusion.8
  771.5 1.5 copy-done.3
  773.1 3.9 fusion.6
  777.0 3.2 collective-permute-start.1
  781.8 1.9 collective-permute-start.2
  786.4 2.6 collective-permute-done.3
  789.0 2.8 collective-permute-start.4
  (80 shorter events, 19.7 us)
Async XLA Ops:
  84.2 1.9 copy-start.1
  308.0 3.0 copy-start
  310.3 2.1 copy-start.5
  453.4 2.8 copy-start.4
  453.4 3.8 copy-start.7
  460.4 11.7 %copy-start.6 = (bf16[1536,512]{1,0:T(8,128)(2,1)S(1)}, bf16[1536,512]{1,0:T(8,128)(2,1)}, u32[]{:S(2)}) copy-start(bf16[1536,512]{1,0:T(8,128)(2,1)} %get-tuple-element.42) | copy-start | bytes 4718596
  767.4 3.9 copy-start.11
  767.5 3.9 copy-start.10
  767.5 4.0 copy-start.9
  767.5 4.1 copy-start.2
  771.2 1.9 copy-start.3
  771.2 5.8 collective-permute-start
  773.0 3.9 copy-start.8
  773.0 7.2 copy-start.12
  776.9 17.1 %copy-start.14 = (f32[192,384]{1,0:T(8,128)S(1)}, f32[192,384]{1,0:T(8,128)}, u32[]{:S(2)}) copy-start(f32[192,384]{1,0:T(8,128)} %get-tuple-element.136) | copy-start | bytes 884740
  777.0 17.8 %copy-start.13 = (f32[192,384]{1,0:T(8,128)S(1)}, f32[192,384]{1,0:T(8,128)}, u32[]{:S(2)}) copy-start(f32[192,384]{1,0:T(8,128)} %get-tuple-element.64) | copy-start | bytes 884740
  777.0 4.8 collective-permute-start.1
  781.8 3.6 collective-permute-start.2
  785.4 3.6 collective-permute-start.3
  789.0 4.5 collective-permute-start.4
